TPU v7x, 1024 devices: a whole 4x4x32 slice. The times are simulated.
1024 devices in a mesh: lat: 32 (over x, z_hi, core), lon: 32 (over y, z_lo).
Axes of the slice: x: 4, y: 4, z: 32 (z_hi: 4, z_lo: 8; z = z_hi * 8 + z_lo), core: 2. Of those that a mesh axis runs over, the one named last changes fastest.
Arguments:
- grad_out: bfloat16 [704, 1440, 256], P('lat', 'lon'), may hold values from -6 to 6
- block_input: bfloat16 [704, 1440, 256], P('lat', 'lon'), may hold values from -6 to 6
- leg_table: bfloat16 [384, 384, 704], P('lat'), may hold values from -1 to 1, as said below
- spec_coeff: bfloat16 [384, 384, 2, 256], P(None, 'lat', None, 'lon'), may hold values from -6 to 6
- spec_filter: float32 [384, 256], P(None, 'lon'), may hold values from -6 to 6
- cycle_weight: float32 [704, 3], replicated, may hold values from 0.2 to 2
- cycle_shift: int32 [704, 3], replicated, may hold values from -1 to 1
- tap_weight: bfloat16 [3, 256, 256], replicated, may hold values from -0.21875 to 0.21875
Outputs:
- spec_grad: bfloat16 [384, 384, 2, 256], P(None, 'lat', None, 'lon')
- filter_grad: float32 [384, 256], P(None, 'lon')
- input_grad: bfloat16 [704, 1440, 256], P('lat', 'lon')
- taps_grad: float32 [3, 256, 256], replicated
Inputs may be any that keep to these rules, and one draw needn't show every extreme that they name: `leg_table`: zero wherever the degree l is below the order m.
All inputs are finite; a program needn't handle non-finite values.
Results may differ from a plain program's by a relative error of at most 0.013.
Values may be sent and summed in bfloat16 or wider, within the bound.
No kernel may reach another device: no remote copies, remote signals or barrier semaphores. Data moves between devices by JAX's collectives and lax.ppermute only.
A program may use at most 64 MiB of HBM per device.

v0:
```python
import math

import jax
import jax.numpy as jnp
from jax import lax
from jax.sharding import PartitionSpec as P


def padded_2(shard, sides, width):
    for axis, dim in sides:
        size, length = (lax.axis_size(axis), shard.shape[dim])
        up = [(i, (i + 1) % size) for i in range(size)]
        down = [(j, i) for i, j in up]
        last = lax.slice_in_dim(shard, length - width, length, axis=dim)
        first = lax.slice_in_dim(shard, 0, width, axis=dim)
        before = lax.ppermute(last, axis, up)
        after = lax.ppermute(first, axis, down)
        shard = jnp.concatenate([before, shard, after], axis=dim)
    return shard


def fourier_table(lon_count, mode_count):
    longitude = jnp.arange(lon_count, dtype=jnp.int32)[:, None]
    orders = jnp.arange(mode_count, dtype=jnp.int32)[None, :]
    phase = (longitude * orders % lon_count).astype(jnp.float32) * (2.0 * math.pi / lon_count)
    table = jnp.stack([jnp.cos(phase), jnp.sin(phase)], axis=-1) / math.sqrt(lon_count)
    return table.astype(jnp.bfloat16)


def on_device(
    grad_out, block_input, leg_table, spec_coeff, spec_filter, cycle_weight, cycle_shift, tap_weight
):
    rows_here, lons_here, channels = grad_out.shape
    lon_total = lons_here * lax.axis_size("lon")
    cycle_total = rows_here * lax.axis_size("lat")
    order_total = leg_table.shape[0] * lax.axis_size("lat")
    table = fourier_table(lon_total, order_total)
    fourier = jnp.einsum(
        "opt,phu->tohu",
        lax.all_to_all(grad_out, "lon", split_axis=2, concat_axis=1, tiled=True),
        table,
        preferred_element_type=jnp.float32,
    ).astype(jnp.bfloat16)
    degree = jnp.einsum(
        "mla,camr->lmrc",
        leg_table,
        lax.all_to_all(fourier, "lat", split_axis=2, concat_axis=1, tiled=True),
        preferred_element_type=jnp.float32,
    )
    spec_grad = (degree * spec_filter[:, None, None, :]).astype(jnp.bfloat16)
    filter_part = jnp.sum(spec_coeff.astype(jnp.float32) * degree, axis=(1, 2)) / math.sqrt(
        2 * order_total
    )
    padded = padded_2(grad_out, (("lat", 0), ("lon", 1)), 1)
    cycle_start = lax.axis_index("lat") * rows_here
    weight_pad = jnp.pad(cycle_weight, ((1, 1), (0, 0)))
    shift_pad = jnp.pad(cycle_shift, ((1, 1), (0, 0)))
    flat_input = block_input.reshape(-1, channels)
    local_grad = jnp.zeros((rows_here * lons_here, channels), jnp.float32)
    partials = []
    for tap_index, offset in enumerate((-1, 0, 1)):
        source = padded[1 - offset : 1 - offset + rows_here]
        coef = lax.dynamic_slice_in_dim(weight_pad, cycle_start + 1 - offset, rows_here, 0)[
            :, tap_index
        ]
        shifts = lax.dynamic_slice_in_dim(shift_pad, cycle_start + 1 - offset, rows_here, 0)[
            :, tap_index
        ]
        picked = jnp.zeros((rows_here, lons_here, channels), jnp.float32)
        for column_shift in (-1, 0, 1):
            window = source[:, 1 - column_shift : 1 - column_shift + lons_here].astype(jnp.float32)
            picked = picked + (shifts == column_shift).astype(jnp.float32)[:, None, None] * window
        spread = (coef[:, None, None] * picked).astype(jnp.bfloat16).reshape(-1, channels)
        local_grad = local_grad + lax.dot_general(
            spread,
            tap_weight[tap_index],
            (((1,), (1,)), ((), ())),
            preferred_element_type=jnp.float32,
        )
        partials.append(
            lax.dot_general(
                flat_input, spread, (((0,), (0,)), ((), ())), preferred_element_type=jnp.float32
            )
        )
    taps_part = jnp.stack(partials) / math.sqrt(cycle_total * lon_total)
    input_grad = local_grad.reshape(rows_here, lons_here, channels).astype(jnp.bfloat16)
    taps_grad = lax.psum(taps_part, ("lat", "lon"))
    filter_grad = lax.psum(filter_part, "lat")
    return (spec_grad, filter_grad, input_grad, taps_grad)


def solution(mesh):
    in_specs = (
        P("lat", "lon", None),
        P("lat", "lon", None),
        P("lat", None, None),
        P(None, "lat", None, "lon"),
        P(None, "lon"),
        P(),
        P(),
        P(),
    )
    out_specs = (P(None, "lat", None, "lon"), P(None, "lon"), P("lat", "lon", None), P())
    return jax.shard_map(
        on_device, mesh=mesh, in_specs=in_specs, out_specs=out_specs, check_vma=False
    )
```

profile of v0, /device:TPU:1, one launch (start us, length us, event | category | flops | bytes accessed | tf_op | source)
XLA Modules:
  0.0 1265.7 jit_solution(4485617606310502766)
XLA Ops:
  7.2 0.0 copy-start
  7.2 1.9 copy.21
  9.1 0.0 copy-start.1
  9.1 4.0 reshape.187
  13.2 16.3 %all-to-all-start = ((bf16[32,2,3960]{2,1,0:T(2,128)(2,1)}), bf16[32,2,3960]{2,1,0:T(2,128)(2,1)}, u32[]{:S(2)}, u32[]{:S(2)}) async-start(bf16[32,2,3960]{2,1,0:T(2,128)(2,1)} %reshape.187), calls=%async_computation | async-start | bytes 1015808 | tf_op jit(solution)/shard_map/all_to_all | solution.py:40
  29.5 0.0 copy-done.1
  29.6 16.3 %collective-permute-start = (bf16[1,45,256]{2,1,0:T(8,128)(2,1)S(1)}, bf16[1,45,256]{2,1,0:T(8,128)(2,1)S(1)}, u32[]{:S(2)}, u32[]{:S(2)}) collective-permute-start(bf16[1,45,256]{2,1,0:T(8,128)(2,1)S(1)} %get-tuple-element.21), channel_id=1, source_target_pairs={{0,32},{32,64},{64,96},{96,128},{128,160},{160,192},{192,224},{224... | collective-permute-start | bytes 69128 | tf_op jit(solution)/shard_map/ppermute | solution.py:16
  45.8 1.9 collective-permute-start.1
  47.8 0.0 copy-done.12
  47.8 0.1 pad_dynamic-slice_fusion
  47.9 0.0 copy-done.13
  47.9 0.1 pad_dynamic-slice_fusion.3
  48.0 0.6 slice_bitcast_fusion
  48.6 0.6 fusion.34
  49.1 10.1 fusion.10
  59.2 0.6 slice_bitcast_fusion.2
  59.8 0.0 collective-permute-done
  59.9 0.0 collective-permute-done.1
  59.9 0.0 copy-start.9
  59.9 0.7 fusion.45
  60.6 3.3 collective-permute-start.3
  63.9 11.0 collective-permute-start.2
  75.0 0.0 copy-done.7
  75.0 0.0 all-to-all-done
  75.0 5.3 reshape.188
  80.3 2.1 copy.31
  82.4 3.4 reshape.180
  85.8 2.9 fusion.20
  88.7 1.3 copy.25
  90.0 0.0 copy-start.18
  90.1 4.0 reshape.189
  94.0 20.8 %all-to-all-start.1 = ((bf16[32,2,2112]{2,1,0:T(2,128)(2,1)}), bf16[32,2,2112]{2,1,0:T(2,128)(2,1)S(1)}, u32[]{:S(2)}, u32[]{:S(2)}) async-start(bf16[32,2,2112]{2,1,0:T(2,128)(2,1)} %reshape.189), calls=%async_computation.1 | async-start | bytes 557056 | tf_op jit(solution)/shard_map/all_to_all | solution.py:47
  114.9 0.3 all-reduce.4.cloned.1.call-start
  115.2 0.0 collective-permute-done.3
  115.2 0.0 collective-permute-done.2
  115.3 1.3 multiply_convert_fusion.2
  116.6 0.0 copy-start.2
  116.6 1.0 reshape.167
  117.6 0.0 copy-done.15
  117.6 0.0 copy-done.16
  117.6 0.0 copy-done.17
  117.6 2.4 multiply_convert_fusion
  120.1 1.0 reshape.168
  121.1 0.4 convolution_bitcast_fusion.1
  121.4 0.7 copy-done.3
  122.1 0.4 convolution_bitcast_fusion.2
  122.5 0.4 convolution_bitcast_fusion
  122.9 0.0 copy-start.4
  122.9 0.9 maximum_multiply_fusion.1
  123.8 0.0 all-reduce.4.cloned.1.call-update
  123.9 0.2 copy-done.4
  124.1 1.2 fusion.29
  125.3 1.2 convolution_add_fusion.1
  126.5 0.2 reshape.169
  126.7 1.2 fusion.13
  127.9 1.0 convert_element_type.202
  128.9 877.3 %all-reduce.4.cloned.1.call-done = f32[3,256,256]{1,2,0:T(8,128)} async-done(((f32[3,256,256]{1,2,0:T(8,128)}), f32[3,256,256]{1,2,0:T(8,128)}) %all-reduce.4.cloned.1.call-update) | async-done | bytes 786448 | tf_op jit(solution)/shard_map/psum | solution.py:87
  1006.2 2.3 copy.27
  1008.4 0.0 all-to-all-done.1
  1008.4 4.0 reshape.190
  1012.5 2.2 copy.26
  1014.7 3.6 all_to_all.33
  1018.3 4.5 multiply_reduce_fusion
  1022.8 236.0 %psum.14 = f32[384,8]{0,1:T(8,128)} all-reduce(f32[384,8]{0,1:T(8,128)S(1)} %broadcast_multiply_fusion), channel_id=1, replica_groups=mesh['lat'=32,'lon'=32] {'lat'}, use_global_device_ids=true, to_apply=%region_1.2 | all-reduce | flops 3072 | bytes 24576 | tf_op jit(solution)/shard_map/psum | solution.py:88
  (35 shorter events, 0.1 us)
Async XLA Ops:
  7.2 113.9 %copy-start = (bf16[22,45,256]{2,1,0:T(8,128)(2,1)S(1)}, bf16[22,45,256]{2,1,0:T(8,128)(2,1)}, u32[]{:S(2)}) copy-start(bf16[22,45,256]{2,1,0:T(8,128)(2,1)} %param.9) | copy-start | bytes 1520644
  9.1 20.4 %copy-start.1 = (bf16[22,45,256]{2,1,0:T(8,128)(2,1)S(1)}, bf16[22,45,256]{2,1,0:T(8,128)(2,1)}, u32[]{:S(2)}) copy-start(bf16[22,45,256]{2,1,0:T(8,128)(2,1)} %param.8) | copy-start | bytes 1520644
  13.2 34.6 %copy-start.12 = (s32[704,3]{0,1:T(4,128)S(1)}, s32[704,3]{0,1:T(4,128)}, u32[]{:S(2)}) copy-start(s32[704,3]{0,1:T(4,128)} %param.14) | copy-start | bytes 25348
  13.2 34.7 %copy-start.13 = (f32[704,3]{0,1:T(4,128)S(1)}, f32[704,3]{0,1:T(4,128)}, u32[]{:S(2)}) copy-start(f32[704,3]{0,1:T(4,128)} %param.13) | copy-start | bytes 25348
  13.2 61.8 %all-to-all-start = ((bf16[32,2,3960]{2,1,0:T(2,128)(2,1)}), bf16[32,2,3960]{2,1,0:T(2,128)(2,1)}, u32[]{:S(2)}, u32[]{:S(2)}) async-start(bf16[32,2,3960]{2,1,0:T(2,128)(2,1)} %reshape.187), calls=%async_computation | async-start | bytes 1015808 | tf_op jit(solution)/shard_map/all_to_all | solution.py:40
  29.6 30.3 %collective-permute-start = (bf16[1,45,256]{2,1,0:T(8,128)(2,1)S(1)}, bf16[1,45,256]{2,1,0:T(8,128)(2,1)S(1)}, u32[]{:S(2)}, u32[]{:S(2)}) collective-permute-start(bf16[1,45,256]{2,1,0:T(8,128)(2,1)S(1)} %get-tuple-element.21), channel_id=1, source_target_pairs={{0,32},{32,64},{64,96},{96,128},{128,160},{160,192},{192,224},{224... | collective-permute-start | bytes 69128 | tf_op jit(solution)/shard_map/ppermute | solution.py:16
  45.8 14.0 %collective-permute-start.1 = (bf16[1,45,256]{2,1,0:T(8,128)(2,1)S(1)}, bf16[1,45,256]{2,1,0:T(8,128)(2,1)S(1)}, u32[]{:S(2)}, u32[]{:S(2)}) collective-permute-start(bf16[1,45,256]{2,1,0:T(8,128)(2,1)S(1)} %get-tuple-element.20), channel_id=1, source_target_pairs={{32,0},{64,32},{96,64},{128,96},{160,128},{192,160},{224,192},{256... | collective-permute-start | bytes 69128 | tf_op jit(solution)/shard_map/ppermute | solution.py:17
  59.8 15.1 %copy-start.7 = (bf16[1,45,256]{2,1,0:T(8,128)(2,1)}, bf16[1,45,256]{2,1,0:T(8,128)(2,1)S(1)}, u32[]{:S(2)}) copy-start(bf16[1,45,256]{2,1,0:T(8,128)(2,1)S(1)} %collective-permute-done) | copy-start | bytes 69124
  59.9 15.1 %copy-start.9 = (bf16[1,45,256]{2,1,0:T(8,128)(2,1)}, bf16[1,45,256]{2,1,0:T(8,128)(2,1)S(1)}, u32[]{:S(2)}) copy-start(bf16[1,45,256]{2,1,0:T(8,128)(2,1)S(1)} %collective-permute-done.1) | copy-start | bytes 69124
  60.6 54.6 %collective-permute-start.3 = (bf16[24,1,256]{2,1,0:T(2,128)(2,1)}, bf16[24,1,256]{2,1,0:T(2,128)(2,1)}, u32[]{:S(2)}, u32[]{:S(2)}) collective-permute-start(bf16[24,1,256]{2,1,0:T(2,128)(2,1)} %get-tuple-element.19), channel_id=1, source_target_pairs={{0,1},{1,2},{2,3},{3,4},{4,5},{5,6},{6,7},{7,8},{8,9},{9,10},{10,1... | collective-permute-start | bytes 36872 | tf_op jit(solution)/shard_map/ppermute | solution.py:16
  63.9 51.2 %collective-permute-start.2 = (bf16[24,1,256]{2,1,0:T(2,128)(2,1)}, bf16[24,1,256]{2,1,0:T(2,128)(2,1)}, u32[]{:S(2)}, u32[]{:S(2)}) collective-permute-start(bf16[24,1,256]{2,1,0:T(2,128)(2,1)} %get-tuple-element.18), channel_id=1, source_target_pairs={{1,0},{2,1},{3,2},{4,3},{5,4},{6,5},{7,6},{8,7},{9,8},{10,9},{11,1... | collective-permute-start | bytes 36872 | tf_op jit(solution)/shard_map/ppermute | solution.py:17
  90.0 25.2 %copy-start.10 = (bf16[1,45,256]{2,1,0:T(8,128)(2,1)S(1)}, bf16[1,45,256]{2,1,0:T(8,128)(2,1)}, u32[]{:S(2)}) copy-start(bf16[1,45,256]{2,1,0:T(8,128)(2,1)} %copy-done.9) | copy-start | bytes 69124
  90.0 25.2 %copy-start.18 = (f32[22]{0:T(128)S(1)}, f32[22]{0:T(128)}, u32[]{:S(2)}) copy-start(f32[22]{0:T(128)} %get-tuple-element.36) | copy-start | bytes 268
  90.1 25.1 %copy-start.19 = (f32[22]{0:T(128)S(1)}, f32[22]{0:T(128)}, u32[]{:S(2)}) copy-start(f32[22]{0:T(128)} %get-tuple-element.37) | copy-start | bytes 268
  90.1 25.1 %copy-start.20 = (f32[22]{0:T(128)S(1)}, f32[22]{0:T(128)}, u32[]{:S(2)}) copy-start(f32[22]{0:T(128)} %get-tuple-element.38) | copy-start | bytes 268
  90.1 25.1 %copy-start.21 = (f32[22]{0:T(128)S(1)}, f32[22]{0:T(128)}, u32[]{:S(2)}) copy-start(f32[22]{0:T(128)} %slice_bitcast_fusion.2) | copy-start | bytes 268
  94.0 914.4 %all-to-all-start.1 = ((bf16[32,2,2112]{2,1,0:T(2,128)(2,1)}), bf16[32,2,2112]{2,1,0:T(2,128)(2,1)S(1)}, u32[]{:S(2)}, u32[]{:S(2)}) async-start(bf16[32,2,2112]{2,1,0:T(2,128)(2,1)} %reshape.189), calls=%async_computation.1 | async-start | bytes 557056 | tf_op jit(solution)/shard_map/all_to_all | solution.py:47
  114.9 891.3 %all-reduce.4.cloned.1.call-start = ((), (), s32[]{:S(2)}) async-start(), calls=%async_computation.2 | async-start | bytes 1572864 | tf_op jit(solution)/shard_map/psum | solution.py:87
  115.2 2.3 copy-start.8
  115.2 2.3 copy-start.14
  115.3 2.3 copy-start.15
  115.3 2.3 copy-start.16
  115.3 2.3 copy-start.17
  116.6 1.0 copy-start.2
  121.1 1.0 copy-start.3
  122.9 1.2 copy-start.4
  123.8 1.4 copy-start.5
  1014.6 3.6 copy-start.6
  1014.7 3.6 copy-start.11
Sparse Core Ops, SparseCore 0:
  124.0 882.1 all-reduce.3
where the time goes:
time: 1280 us; the launch traced here: 1270 us
  waiting for transfers between devices  877 us (69%)
  blocking collectives  236 us (18%)
  starting transfers between devices  70 us (5%)
  local copies, waits for them, and re-layouts  40.2 us (3%)
  other arithmetic  15.4 us (1%)
  between operations  14.5 us (1%)
    psum x1, waiting for transfers between devices, on_device(): taps_grad = lax.psum(taps_part, ('lat', 'lon'))  877 us
    psum x1, blocking collectives, on_device(): filter_grad = lax.psum(filter_part, 'lat')  236 us
  transfers between devices with their start and end apart: 7, of which 1 were waited for; matrix products, arithmetic and copies ran while one was open for 4% of the time, Pallas kernels for 0%

commit v1 on v0

v1 whole, which is shorter than its diff:
```python
import functools
import math

import jax
import jax.numpy as jnp
import ml_dtypes
import numpy as np
from jax import lax
from jax.experimental import pallas as pl
from jax.experimental.pallas import tpu as pltpu
from jax.sharding import PartitionSpec as P

F32 = jnp.float32
BF16 = jnp.bfloat16
ROW = 8
LANES = 128


def ceil_to(value, step):
    return -(-value // step) * step


CORE = (1, 2)
Z_HI = (2, 4)
X = (8, 4)


def turn(total, digit, shift):
    stride, size = digit
    pairs = []
    for source in range(total):
        place = source // stride % size
        pairs.append((source, source + ((place + shift) % size - place) * stride))
    return pairs


def sum_over_digits(value, digits):
    total = lax.axis_size("lat")
    for digit in digits:
        parts = [value] + [
            lax.ppermute(value, "lat", turn(total, digit, shift)) for shift in range(1, digit[1])
        ]
        while len(parts) > 1:
            half = len(parts) // 2
            parts = [parts[i] + parts[i + half] for i in range(half)]
        value = parts[0]
    return value


def transform_constants(sectors, sector, orders, chans):
    lon_total = sectors * sector
    width = ceil_to(sector, 16)
    turns = orders // sectors
    p, j, q, t = (np.arange(n) for n in (sectors, sectors, sector, turns))
    across = 2 * np.pi * (p[:, None] * j[None, :] % sectors) / sectors
    eye = np.eye(chans)
    across = np.concatenate([np.kron(np.cos(across), eye), np.kron(np.sin(across), eye)])
    phase = 2 * np.pi * (p[:, None] * q[None, :]) / lon_total
    twiddle = np.zeros((2, sectors, ROW, width))
    twiddle[0, :, :, :sector] = (np.cos(phase) / math.sqrt(lon_total))[:, None]
    twiddle[1, :, :, :sector] = (np.sin(phase) / math.sqrt(lon_total))[:, None]
    twiddle = np.repeat(twiddle.reshape(2, sectors, ROW * width), chans, axis=1)
    within = 2 * np.pi * (t[:, None] * q[None, :] % sector) / sector
    c, s = np.cos(within), np.sin(within)
    inner = np.zeros((turns, 2, ROW, 2, ROW, width))
    for row in range(ROW):
        inner[:, 0, row, 0, row, :sector] = c
        inner[:, 0, row, 1, row, :sector] = -s
        inner[:, 1, row, 0, row, :sector] = s
        inner[:, 1, row, 1, row, :sector] = c
    inner = inner.reshape(turns * 2 * ROW, 2 * ROW * width)
    kind = ml_dtypes.bfloat16
    return across.astype(kind), twiddle.astype(np.float32), inner.astype(kind)


def turn_kernel(x_ref, o_ref, s_ref):
    rows, lons, _ = x_ref.shape
    s_ref[...] = jnp.zeros_like(s_ref)
    s_ref[:rows, :lons, :] = x_ref[...]
    o_ref[...] = s_ref[...].reshape(-1, s_ref.shape[2]).T


def channels_first(field):
    rows, lons, channels = field.shape
    tall, wide = ceil_to(rows, ROW), ceil_to(lons, 16)
    return pl.pallas_call(
        turn_kernel,
        out_shape=jax.ShapeDtypeStruct((channels, tall * wide), field.dtype),
        scratch_shapes=[pltpu.VMEM((tall, wide, channels), field.dtype)],
        compiler_params=pltpu.CompilerParams(vmem_limit_bytes=32 << 20),
        name="channels_first",
    )(field)


def fourier_kernel(blocks, turns, span, keep, r_ref, d_ref, tw_ref, w_ref, o_ref, g_ref):
    half = r_ref.shape[0]
    wide = tw_ref.shape[2]
    tall = blocks * ROW
    for block in range(blocks):
        field = r_ref[:, block * wide : (block + 1) * wide]
        a = jnp.dot(d_ref[:half], field, preferred_element_type=F32)
        b = jnp.dot(d_ref[half:], field, preferred_element_type=F32)
        re = (a * tw_ref[0] - b * tw_ref[1]).astype(BF16)
        im = (a * tw_ref[1] + b * tw_ref[0]).astype(BF16)
        nt = (((1,), (1,)), ((), ()))
        out = lax.dot_general(w_ref[:, :wide], re, nt, preferred_element_type=F32)
        out += lax.dot_general(w_ref[:, wide:], im, nt, preferred_element_type=F32)
        for t in range(turns):
            for r in range(2):
                g_ref[
                    r * tall + block * ROW : r * tall + (block + 1) * ROW,
                    t * half : (t + 1) * half,
                ] = out[(t * 2 + r) * ROW : (t * 2 + r + 1) * ROW]
    count = o_ref.shape[0]
    group = math.lcm(span, LANES)
    lane = lax.broadcasted_iota(jnp.int32, (keep, LANES), 1)
    rest = LANES - span
    for start in range(0, count * span, group):
        values = g_ref[:, start : start + group]
        for k in range(group // span):
            shift = (group - k * span) % group
            piece = pltpu.roll(values, shift, 1) if shift else values
            piece = piece[:, :LANES]
            tail = piece[keep:]
            folds = [pltpu.roll(tail, span - n * rest, 1) for n in range(span // rest)]
            folds.append(jnp.zeros((keep - len(folds) * tail.shape[0], LANES), F32))
            folded = jnp.concatenate(folds, axis=0)
            o_ref[start // span + k] = jnp.where(lane < span, piece[:keep], folded).astype(BF16)


def fold_sizes(rows, span):
    tall = 2 * ceil_to(rows, ROW)
    return tall, tall - ROW


def fourier_chunks(received, rows, sector, orders, groups):
    sectors, chans, lanes = received.shape
    blocks = ceil_to(rows, ROW) // ROW
    turns = orders // sectors
    span = orders // groups * chans
    tall, keep = fold_sizes(rows, span)
    across, twiddle, inner = transform_constants(sectors, sector, orders, chans)
    return pl.pallas_call(
        functools.partial(fourier_kernel, blocks, turns, span, keep),
        out_shape=jax.ShapeDtypeStruct((groups, keep, LANES), BF16),
        scratch_shapes=[pltpu.VMEM((tall, orders * chans), F32)],
        compiler_params=pltpu.CompilerParams(vmem_limit_bytes=48 << 20),
        name="fourier_chunks",
    )(
        received.reshape(sectors * chans, lanes),
        jnp.asarray(across),
        jnp.asarray(twiddle),
        jnp.asarray(inner),
    )


def unfold_kernel(rows, span, q_ref, o_ref, s_ref):
    count, keep, _ = q_ref.shape
    tall = ceil_to(rows, ROW)
    rest = LANES - span
    lane = lax.broadcasted_iota(jnp.int32, (ROW, LANES), 1)
    used = count * rows
    if s_ref.shape[0] > used:
        s_ref[used:, :] = jnp.zeros((s_ref.shape[0] - used, s_ref.shape[1]), F32)
    for n in range(count):
        block = q_ref[n].astype(F32)
        tail = pltpu.roll(block[:ROW], rest, 1)
        for k in range(1, span // rest):
            piece = pltpu.roll(block[k * ROW : (k + 1) * ROW], (k + 1) * rest, 1)
            tail = jnp.where(lane < k * rest, tail, piece)
        s_ref[n * rows : (n + 1) * rows, :LANES] = block[:rows]
        middle = keep - tall
        s_ref[n * rows : n * rows + middle, LANES:] = block[tall:keep]
        s_ref[n * rows + middle : (n + 1) * rows, LANES:] = tail[: rows - middle]
    orders, both, _ = o_ref.shape
    chans = both // 2
    for r in range(2):
        flipped = s_ref[:, r * LANES : (r + 1) * LANES].T[:, :used].astype(BF16)
        for m in range(orders):
            o_ref[m, r * chans : (r + 1) * chans, :] = flipped[m * chans : (m + 1) * chans]


def unfold(received, rows, orders, chans):
    count = received.shape[0]
    used = count * rows
    return pl.pallas_call(
        functools.partial(unfold_kernel, rows, orders * chans),
        out_shape=jax.ShapeDtypeStruct((orders, 2 * chans, used), BF16),
        scratch_shapes=[pltpu.VMEM((ceil_to(used, LANES), 2 * LANES), F32)],
        compiler_params=pltpu.CompilerParams(vmem_limit_bytes=32 << 20),
        name="unfold",
    )(received)


def padded_2(shard):
    for axis, dim in (("lat", 0), ("lon", 1)):
        size, length = (lax.axis_size(axis), shard.shape[dim])
        up = [(i, (i + 1) % size) for i in range(size)]
        down = [(j, i) for i, j in up]
        last = lax.index_in_dim(shard, length - 1, axis=dim, keepdims=False)
        first = lax.index_in_dim(shard, 0, axis=dim, keepdims=False)
        before = jnp.expand_dims(lax.ppermute(last, axis, up), dim)
        after = jnp.expand_dims(lax.ppermute(first, axis, down), dim)
        shard = jnp.concatenate([before, shard, after], axis=dim)
    return shard


def total_taps(part):
    shape = part.shape
    lat, lon = lax.axis_size("lat"), lax.axis_size("lon")
    core = lax.axis_index("lat") % 2
    swap = turn(lat, CORE, 1)
    halves = part.reshape(2, -1, shape[-1])
    mine = lax.dynamic_index_in_dim(halves, core, 0, keepdims=False)
    other = lax.dynamic_index_in_dim(halves, 1 - core, 0, keepdims=False)
    mine = mine + lax.ppermute(other, "lat", swap)
    rows, columns = mine.shape
    parts = columns // LANES
    high = rows * parts // lon
    chunks = mine.reshape(lon // parts, high, parts, LANES).transpose(0, 2, 1, 3)
    chunks = lax.all_to_all(chunks.reshape(lon, high, LANES), "lon", 0, 0)
    chunk = sum_over_digits(jnp.sum(chunks, axis=0), (X, Z_HI)).astype(BF16)
    chunks = lax.all_to_all(jnp.broadcast_to(chunk, (lon, high, LANES)), "lon", 0, 0)
    mine = chunks.reshape(lon // parts, parts, high, LANES).transpose(0, 2, 1, 3)
    mine = mine.reshape(rows, columns)
    other = lax.ppermute(mine, "lat", swap)
    low = jnp.where(core == 0, mine, other)
    high = jnp.where(core == 0, other, mine)
    return jnp.stack([low, high]).astype(F32).reshape(shape)


def disco(grad_out, block_input, cycle_weight, cycle_shift, tap_weight):
    rows_here, lons_here, channels = grad_out.shape
    lon_total = lons_here * lax.axis_size("lon")
    cycle_total = rows_here * lax.axis_size("lat")
    padded = padded_2(grad_out)
    cycle_start = lax.axis_index("lat") * rows_here
    weight_pad = jnp.pad(cycle_weight, ((1, 1), (0, 0)))
    shift_pad = jnp.pad(cycle_shift, ((1, 1), (0, 0)))
    flat_input = block_input.reshape(-1, channels)
    local_grad = jnp.zeros((rows_here * lons_here, channels), F32)
    partials = []
    for tap_index, offset in enumerate((-1, 0, 1)):
        source = padded[1 - offset : 1 - offset + rows_here]
        coef = lax.dynamic_slice_in_dim(weight_pad, cycle_start + 1 - offset, rows_here, 0)[
            :, tap_index
        ]
        shifts = lax.dynamic_slice_in_dim(shift_pad, cycle_start + 1 - offset, rows_here, 0)[
            :, tap_index
        ]
        picked = jnp.zeros((rows_here, lons_here, channels), F32)
        for column_shift in (-1, 0, 1):
            window = source[:, 1 - column_shift : 1 - column_shift + lons_here].astype(F32)
            picked = picked + (shifts == column_shift).astype(F32)[:, None, None] * window
        spread = (coef[:, None, None] * picked).astype(BF16).reshape(-1, channels)
        local_grad = local_grad + lax.dot_general(
            spread,
            tap_weight[tap_index],
            (((1,), (1,)), ((), ())),
            preferred_element_type=F32,
        )
        partials.append(
            lax.dot_general(flat_input, spread, (((0,), (0,)), ((), ())), preferred_element_type=F32)
        )
    taps_part = jnp.stack(partials) / math.sqrt(cycle_total * lon_total)
    return local_grad.reshape(rows_here, lons_here, channels).astype(BF16), taps_part


def on_device(
    grad_out, block_input, leg_table, spec_coeff, spec_filter, cycle_weight, cycle_shift, tap_weight
):
    rows_here, lons_here, channels = grad_out.shape
    lat, lon = lax.axis_size("lat"), lax.axis_size("lon")
    chans = channels // lon
    orders_here, degrees, _ = leg_table.shape
    orders = orders_here * lat

    sent = channels_first(grad_out).reshape(lon, chans, -1)
    rows = lax.all_to_all(sent, "lon", 0, 0)

    input_grad, taps_part = disco(grad_out, block_input, cycle_weight, cycle_shift, tap_weight)
    taps_grad = total_taps(taps_part)

    blocks = fourier_chunks(rows, rows_here, lons_here, orders, lat)
    columns = lax.all_to_all(blocks, "lat", 0, 0)
    fourier = unfold(columns, rows_here, orders_here, chans)
    degree = jnp.einsum("mla,mxa->mxl", leg_table, fourier, preferred_element_type=F32)
    degree = degree.reshape(orders_here, 2, chans, degrees)
    spec_grad = (degree * spec_filter.T).astype(BF16).transpose(3, 0, 1, 2)
    coeff = spec_coeff.transpose(1, 2, 3, 0).astype(F32)
    filter_part = jnp.sum(coeff * degree, axis=(0, 1)) / math.sqrt(2 * orders)
    filter_grad = sum_over_digits(filter_part, (CORE, X, Z_HI)).T
    return (spec_grad, filter_grad, input_grad, taps_grad)


def solution(mesh):
    in_specs = (
        P("lat", "lon", None),
        P("lat", "lon", None),
        P("lat", None, None),
        P(None, "lat", None, "lon"),
        P(None, "lon"),
        P(),
        P(),
        P(),
    )
    out_specs = (P(None, "lat", None, "lon"), P(None, "lon"), P("lat", "lon", None), P())
    return jax.shard_map(
        on_device, mesh=mesh, in_specs=in_specs, out_specs=out_specs, check_vma=False
    )
```

time: 1280 us -> 260 us (0.20)
  waiting for transfers between devices: 877 us -> 59.2 us
  blocking collectives: 236 us -> 0 us
  starting transfers between devices: 70 us -> 170 us
  local copies, waits for them, and re-layouts: 40.2 us -> 9.54 us
  between operations: 14.5 us -> 1.27 us
    psum x1 -> x0, waiting for transfers between devices: 877 us -> none  [on_device(): taps_grad = lax.psum(taps_part, ('lat', 'lon'))]
    psum x1 -> x0, blocking collectives: 236 us -> none  [on_device(): filter_grad = lax.psum(filter_part, 'lat')]
    ppermute x4 -> x19, starting transfers between devices: 32.6 us -> 128 us  [the longest x13 88.9 us: sum_over_digits(): lax.ppermute(value, 'lat', turn(total, digit, shift))]
    ppermute x4 -> x19, waiting for transfers between devices: 0.01 us -> 37.8 us  [the longest x13 13 us: sum_over_digits(): lax.ppermute(value, 'lat', turn(total, digit, shift))]
    all_to_all x2 -> x4, waiting for transfers between devices: 0.01 us -> 21.4 us  [the longest x1 21.3 us: total_taps(): chunks = lax.all_to_all(chunks.reshape(lon, high, LANES), 'lon', 0, 0)]
    unnamed x52 -> x33, local copies, waits for them, and re-layouts: 22.5 us -> 2.36 us
    all_to_all x2 -> x4, starting transfers between devices: 37.2 us -> 41.9 us  [the longest x1 16.1 us: on_device(): rows = lax.all_to_all(sent, 'lon', 0, 0)]
  transfers between devices with their start and end apart: 7 -> 23, of which waited for: 1 -> 8; matrix products, arithmetic and copies ran while one was open for 4% -> 7% of each run, Pallas kernels for 0% -> 1%
where the time goes in v1:
time: 260 us; the launch traced here: 257 us
  starting transfers between devices  170 us (65%)
  waiting for transfers between devices  59.2 us (23%)
  local copies, waits for them, and re-layouts  9.54 us (4%)
  matrix products  7.6 us (3%)
  other arithmetic  5.32 us (2%)
  Pallas kernels  3.98 us (2%)
    ppermute x13, starting transfers between devices, sum_over_digits(): lax.ppermute(value, 'lat', turn(total, digit, shift))  88.9 us
    all_to_all x1, waiting for transfers between devices, total_taps(): chunks = lax.all_to_all(chunks.reshape(lon, high, LANES), 'lon', 0, 0)  21.3 us
    ppermute x2, starting transfers between devices, padded_2(): before = jnp.expand_dims(lax.ppermute(last, axis, up), dim)  18.2 us
    all_to_all x1, starting transfers between devices, on_device(): rows = lax.all_to_all(sent, 'lon', 0, 0)  16.1 us
    ppermute x2, starting transfers between devices, padded_2(): after = jnp.expand_dims(lax.ppermute(first, axis, down), dim)  14.2 us
    all_to_all x1, starting transfers between devices, on_device(): columns = lax.all_to_all(blocks, 'lat', 0, 0)  14 us
    ppermute x13, waiting for transfers between devices, sum_over_digits(): lax.ppermute(value, 'lat', turn(total, digit, shift))  13 us
    ppermute x2, waiting for transfers between devices, padded_2(): after = jnp.expand_dims(lax.ppermute(first, axis, down), dim)  11.8 us
  transfers between devices with their start and end apart: 23, of which 8 were waited for; matrix products, arithmetic and copies ran while one was open for 7% of the time, Pallas kernels for 1%

profile of v1, /device:TPU:1, one launch (start us, length us, event | category | flops | bytes accessed | tf_op | source)
XLA Modules:
  0.0 256.8 jit_solution(13079856075404147543)
XLA Ops:
  0.7 1.1 copy-done.1
  1.8 1.0 channels_first.1
  2.8 16.1 %all-to-all-start = ((bf16[32,8,1152]{2,1,0:T(8,128)(2,1)}), bf16[32,8,1152]{2,1,0:T(8,128)(2,1)S(1)}, u32[]{:S(2)}, u32[]{:S(2)}) async-start(bf16[32,8,1152]{2,1,0:T(8,128)(2,1)} %bitcast), calls=%async_computation | async-start | bytes 1179648 | tf_op jit(solution)/shard_map/all_to_all | solution.py:279
  18.9 16.3 %collective-permute-start.7 = (bf16[45,256]{1,0:T(8,128)(2,1)S(1)}, bf16[45,256]{1,0:T(8,128)(2,1)S(1)}, u32[]{:S(2)}, u32[]{:S(2)}) collective-permute-start(bf16[45,256]{1,0:T(8,128)(2,1)S(1)} %get-tuple-element.10), channel_id=1, source_target_pairs={{0,32},{32,64},{64,96},{96,128},{128,160},{160,192},{192,224},{224... | collective-permute-start | bytes 69128 | tf_op jit(solution)/shard_map/ppermute | solution.py:202
  35.2 1.9 collective-permute-start.8
  37.2 0.1 pad_dynamic-slice_fusion
  37.3 0.1 pad_dynamic-slice_fusion.3
  37.4 11.8 %collective-permute-done.8 = bf16[45,256]{1,0:T(8,128)(2,1)S(1)} collective-permute-done((bf16[45,256]{1,0:T(8,128)(2,1)S(1)}, bf16[45,256]{1,0:T(8,128)(2,1)S(1)}, u32[]{:S(2)}, u32[]{:S(2)}) %collective-permute-start.8) | collective-permute-done | bytes 23072 | tf_op jit(solution)/shard_map/ppermute | solution.py:203
  49.2 12.2 %collective-permute-start.9 = (bf16[24,256]{1,0:T(8,128)(2,1)S(1)}, bf16[24,256]{1,0:T(8,128)(2,1)S(1)}, u32[]{:S(2)}, u32[]{:S(2)}) collective-permute-start(bf16[24,256]{1,0:T(8,128)(2,1)S(1)} %bitcast.133), channel_id=1, source_target_pairs={{1,0},{2,1},{3,2},{4,3},{5,4},{6,5},{7,6},{8,7},{9,8},{10,9},{11,1... | collective-permute-start | bytes 36872 | tf_op jit(solution)/shard_map/ppermute | solution.py:203
  61.5 1.9 collective-permute-start.10
  63.5 11.2 %collective-permute-done.10 = bf16[24,256]{1,0:T(8,128)(2,1)S(1)} collective-permute-done((bf16[24,256]{1,0:T(8,128)(2,1)S(1)}, bf16[24,256]{1,0:T(8,128)(2,1)S(1)}, u32[]{:S(2)}, u32[]{:S(2)}) %collective-permute-start.10) | collective-permute-done | bytes 12320 | tf_op jit(solution)/shard_map/ppermute | solution.py:202
  74.7 0.4 pad_maximum_fusion
  75.1 0.8 multiply_convert_fusion
  75.9 0.4 convolution_bitcast_fusion.1
  76.3 0.4 convolution_bitcast_fusion.2
  76.7 0.2 copy-done.8
  76.9 0.5 multiply_convert_fusion.2
  77.4 0.4 convolution_bitcast_fusion.3
  77.7 0.1 maximum_multiply_fusion
  77.8 0.8 dynamic-slice_bitcast_fusion
  78.6 1.9 collective-permute-start.11
  80.5 1.9 collective-permute-done.11
  82.4 0.8 bitcast_add_fusion
  83.2 2.1 reshape.149
  85.3 1.8 copy.55
  87.1 6.7 %all-to-all-start.2 = ((f32[32,24,128]{2,1,0:T(8,128)}), f32[32,24,128]{2,1,0:T(8,128)}, u32[]{:S(2)}, u32[]{:S(2)}) async-start(f32[32,24,128]{2,1,0:T(8,128)} %bitcast.121), calls=%async_computation.2 | async-start | bytes 786432 | tf_op jit(solution)/shard_map/all_to_all | solution.py:221
  93.8 2.7 %fourier_chunks.1 = bf16[32,40,128]{2,1,0:T(8,128)(2,1)} custom-call(bf16[256,1152]{1,0:T(8,128)(2,1)S(1)} %bitcast.116, bf16[512,256]{1,0:T(8,128)(2,1)S(1)} %copy-done.5, f32[2,256,384]{2,1,0:T(8,128)S(1)} %copy-done.3, bf16[192,768]{1,0:T(8,128)(2,1)S(1)} %copy-done.4), custom_call_target="tpu_custom_call" | custom-call | tf_op jit(solution)/shard_map/fourier_chunks/pallas_call | solution.py:143
  96.5 21.3 %all-to-all-done.2 = f32[32,24,128]{2,1,0:T(8,128)} async-done(((f32[32,24,128]{2,1,0:T(8,128)}), f32[32,24,128]{2,1,0:T(8,128)}, u32[]{:S(2)}, u32[]{:S(2)}) %all-to-all-start.2) | async-done | bytes 393248 | tf_op jit(solution)/shard_map/all_to_all | solution.py:221
  117.8 14.0 %all-to-all-start.1 = ((bf16[32,40,128]{2,1,0:T(8,128)(2,1)}), bf16[32,40,128]{2,1,0:T(8,128)(2,1)S(1)}, u32[]{:S(2)}, u32[]{:S(2)}) async-start(bf16[32,40,128]{2,1,0:T(8,128)(2,1)} %fourier_chunks.1), calls=%async_computation.1 | async-start | bytes 655360 | tf_op jit(solution)/shard_map/all_to_all | solution.py:285
  131.9 1.0 reduce_sum.19
  132.9 4.8 %collective-permute-start.12 = (f32[24,128]{1,0:T(8,128)S(1)}, f32[24,128]{1,0:T(8,128)S(1)}, u32[]{:S(2)}, u32[]{:S(2)}) collective-permute-start(f32[24,128]{1,0:T(8,128)S(1)} %reduce_sum.19), channel_id=1, source_target_pairs={{0,512},{32,544},{64,576},{96,608},{128,640},{160,672},{192,704},{... | collective-permute-start | bytes 36872 | tf_op jit(solution)/shard_map/ppermute | solution.py:41
  137.7 2.2 collective-permute-start.13
  140.0 4.3 %collective-permute-start.14 = (f32[24,128]{1,0:T(8,128)S(1)}, f32[24,128]{1,0:T(8,128)S(1)}, u32[]{:S(2)}, u32[]{:S(2)}) collective-permute-start(f32[24,128]{1,0:T(8,128)S(1)} %reduce_sum.19), channel_id=1, source_target_pairs={{0,768},{32,800},{64,832},{96,864},{128,896},{160,928},{192,960},{... | collective-permute-start | bytes 36872 | tf_op jit(solution)/shard_map/ppermute | solution.py:41
  144.3 0.8 collective-permute-done.14
  145.0 21.4 %collective-permute-start.15 = (f32[24,128]{1,0:T(8,128)S(1)}, f32[24,128]{1,0:T(8,128)S(1)}, u32[]{:S(2)}, u32[]{:S(2)}) collective-permute-start(f32[24,128]{1,0:T(8,128)S(1)} %add_add_fusion), channel_id=1, source_target_pairs={{0,128},{32,160},{64,192},{96,224},{128,0},{160,32},{192,64},{224,... | collective-permute-start | bytes 36872 | tf_op jit(solution)/shard_map/ppermute | solution.py:41
  166.5 2.2 collective-permute-start.16
  168.7 11.8 %collective-permute-start.17 = (f32[24,128]{1,0:T(8,128)S(1)}, f32[24,128]{1,0:T(8,128)S(1)}, u32[]{:S(2)}, u32[]{:S(2)}) collective-permute-start(f32[24,128]{1,0:T(8,128)S(1)} %add_add_fusion), channel_id=1, source_target_pairs={{0,192},{32,224},{64,0},{96,32},{128,64},{160,96},{192,128},{224,1... | collective-permute-start | bytes 36872 | tf_op jit(solution)/shard_map/ppermute | solution.py:41
  180.5 1.4 collective-permute-done.17
  182.0 0.7 broadcast_in_dim.14
  182.7 5.1 %all-to-all-start.3 = ((bf16[32,24,128]{2,1,0:T(8,128)(2,1)}), bf16[32,24,128]{2,1,0:T(8,128)(2,1)S(1)}, u32[]{:S(2)}, u32[]{:S(2)}) async-start(bf16[32,24,128]{2,1,0:T(8,128)(2,1)} %broadcast_in_dim.14), calls=%async_computation.3 | async-start | bytes 393216 | tf_op jit(solution)/shard_map/all_to_all | solution.py:223
  187.8 0.2 reshape.147
  187.9 0.2 reshape.146
  188.1 0.7 copy-done.7
  188.8 0.2 reshape.148
  189.0 1.3 fusion.5
  190.3 0.3 convolution_add_fusion.1
  190.6 0.2 unfold.1
  190.9 0.3 copy-done.10
  191.2 4.5 %fusion.1 = (f32[8,384]{1,0:T(8,128)S(1)}, bf16[384,12,2,8]{0,3,2,1:T(8,128)(2,1)}) fusion(bf16[384,12,2,8]{0,3,2,1:T(8,128)(2,1)S(1)} %copy-done.10, f32[8,384]{1,0:T(8,128)S(1)} %bitcast.132, bf16[12,16,704]{2,1,0:T(8,128)(2,1)S(1)} %unfold.1, bf16[12,384,704]{1,2,0:T(8,128)(2,1)} %param.13), kind=kOutput, calls=%fused_computation.19 | convolution fusion | flops 104174592 | bytes 7077888 | tf_op jit(solution)/shard_map/mla,mxa->mxl/dot_general | solution.py:287
  195.7 5.4 %collective-permute-start = (f32[8,384]{1,0:T(8,128)S(1)}, f32[8,384]{1,0:T(8,128)S(1)}, u32[]{:S(2)}, u32[]{:S(2)}) collective-permute-start(f32[8,384]{1,0:T(8,128)S(1)} %broadcast_multiply_fusion), channel_id=1, source_target_pairs={{0,32},{32,0},{64,96},{96,64},{128,160},{160,128},{192,224},{224,1... | collective-permute-start | bytes 36872 | tf_op jit(solution)/shard_map/ppermute | solution.py:41
  201.2 0.3 fusion
  201.5 1.0 convert_element_type.187
  202.5 0.2 copy.56
  202.7 4.9 %collective-permute-start.18 = (bf16[384,256]{1,0:T(8,128)(2,1)S(1)}, bf16[384,256]{1,0:T(8,128)(2,1)S(1)}, u32[]{:S(2)}, u32[]{:S(2)}) collective-permute-start(bf16[384,256]{1,0:T(8,128)(2,1)S(1)} %bitcast.131), channel_id=1, source_target_pairs={{0,32},{32,0},{64,96},{96,64},{128,160},{160,128},{192,224},{224,1... | collective-permute-start | bytes 589832 | tf_op jit(solution)/shard_map/ppermute | solution.py:226
  207.6 4.7 %collective-permute-start.1 = (f32[8,384]{1,0:T(8,128)S(1)}, f32[8,384]{1,0:T(8,128)S(1)}, u32[]{:S(2)}, u32[]{:S(2)}) collective-permute-start(f32[8,384]{1,0:T(8,128)S(1)} %fusion.19), channel_id=1, source_target_pairs={{0,512},{32,544},{64,576},{96,608},{128,640},{160,672},{192,704},{... | collective-permute-start | bytes 36872 | tf_op jit(solution)/shard_map/ppermute | solution.py:41
  212.3 2.7 %collective-permute-start.2 = (f32[8,384]{1,0:T(8,128)S(1)}, f32[8,384]{1,0:T(8,128)S(1)}, u32[]{:S(2)}, u32[]{:S(2)}) collective-permute-start(f32[8,384]{1,0:T(8,128)S(1)} %fusion.19), channel_id=1, source_target_pairs={{0,256},{32,288},{64,320},{96,352},{128,384},{160,416},{192,448},{... | collective-permute-start | bytes 36872 | tf_op jit(solution)/shard_map/ppermute | solution.py:41
  215.0 3.8 %collective-permute-start.3 = (f32[8,384]{1,0:T(8,128)S(1)}, f32[8,384]{1,0:T(8,128)S(1)}, u32[]{:S(2)}, u32[]{:S(2)}) collective-permute-start(f32[8,384]{1,0:T(8,128)S(1)} %fusion.19), channel_id=1, source_target_pairs={{0,768},{32,800},{64,832},{96,864},{128,896},{160,928},{192,960},{... | collective-permute-start | bytes 36872 | tf_op jit(solution)/shard_map/ppermute | solution.py:41
  218.9 0.7 collective-permute-done.3
  219.6 11.5 %collective-permute-start.4 = (f32[8,384]{1,0:T(8,128)S(1)}, f32[8,384]{1,0:T(8,128)S(1)}, u32[]{:S(2)}, u32[]{:S(2)}) collective-permute-start(f32[8,384]{1,0:T(8,128)S(1)} %add_add_fusion.1), channel_id=1, source_target_pairs={{0,128},{32,160},{64,192},{96,224},{128,0},{160,32},{192,64},{224,... | collective-permute-start | bytes 36872 | tf_op jit(solution)/shard_map/ppermute | solution.py:41
  231.2 11.8 %collective-permute-start.5 = (f32[8,384]{1,0:T(8,128)S(1)}, f32[8,384]{1,0:T(8,128)S(1)}, u32[]{:S(2)}, u32[]{:S(2)}) collective-permute-start(f32[8,384]{1,0:T(8,128)S(1)} %add_add_fusion.1), channel_id=1, source_target_pairs={{0,64},{32,96},{64,128},{96,160},{128,192},{160,224},{192,0},{224,... | collective-permute-start | bytes 36872 | tf_op jit(solution)/shard_map/ppermute | solution.py:41
  243.0 2.2 collective-permute-start.6
  245.2 0.9 convert.11
  246.2 10.0 %collective-permute-done.6 = f32[8,384]{1,0:T(8,128)S(1)} collective-permute-done((f32[8,384]{1,0:T(8,128)S(1)}, f32[8,384]{1,0:T(8,128)S(1)}, u32[]{:S(2)}, u32[]{:S(2)}) %collective-permute-start.6) | collective-permute-done | bytes 12320 | tf_op jit(solution)/shard_map/ppermute | solution.py:41
  256.2 0.6 add_bitcast_fusion
  (59 shorter events, 0.4 us)
Async XLA Ops:
  0.6 75.3 %copy-start = (bf16[22,45,256]{2,1,0:T(8,128)(2,1)S(1)}, bf16[22,45,256]{2,1,0:T(8,128)(2,1)}, u32[]{:S(2)}) copy-start(bf16[22,45,256]{2,1,0:T(8,128)(2,1)} %param.12) | copy-start | bytes 1520644
  0.6 1.1 copy-start.1
  1.8 17.1 %copy-start.2 = (bf16[22,45,256]{2,1,0:T(8,128)(2,1)S(1)}, bf16[22,45,256]{2,1,0:T(8,128)(2,1)}, u32[]{:S(2)}) copy-start(bf16[22,45,256]{2,1,0:T(8,128)(2,1)} %x_ref.1) | copy-start | bytes 1520644
  1.8 35.4 %copy-start.13 = (s32[704,3]{0,1:T(4,128)S(1)}, s32[704,3]{0,1:T(4,128)}, u32[]{:S(2)}) copy-start(s32[704,3]{0,1:T(4,128)} %param.17) | copy-start | bytes 25348
  1.8 35.5 %copy-start.14 = (f32[704,3]{0,1:T(4,128)S(1)}, f32[704,3]{0,1:T(4,128)}, u32[]{:S(2)}) copy-start(f32[704,3]{0,1:T(4,128)} %param.16) | copy-start | bytes 25348
  2.8 84.3 %all-to-all-start = ((bf16[32,8,1152]{2,1,0:T(8,128)(2,1)}), bf16[32,8,1152]{2,1,0:T(8,128)(2,1)S(1)}, u32[]{:S(2)}, u32[]{:S(2)}) async-start(bf16[32,8,1152]{2,1,0:T(8,128)(2,1)} %bitcast), calls=%async_computation | async-start | bytes 1179648 | tf_op jit(solution)/shard_map/all_to_all | solution.py:279
  18.9 18.5 %collective-permute-start.7 = (bf16[45,256]{1,0:T(8,128)(2,1)S(1)}, bf16[45,256]{1,0:T(8,128)(2,1)S(1)}, u32[]{:S(2)}, u32[]{:S(2)}) collective-permute-start(bf16[45,256]{1,0:T(8,128)(2,1)S(1)} %get-tuple-element.10), channel_id=1, source_target_pairs={{0,32},{32,64},{64,96},{96,128},{128,160},{160,192},{192,224},{224... | collective-permute-start | bytes 69128 | tf_op jit(solution)/shard_map/ppermute | solution.py:202
  35.2 14.0 %collective-permute-start.8 = (bf16[45,256]{1,0:T(8,128)(2,1)S(1)}, bf16[45,256]{1,0:T(8,128)(2,1)S(1)}, u32[]{:S(2)}, u32[]{:S(2)}) collective-permute-start(bf16[45,256]{1,0:T(8,128)(2,1)S(1)} %get-tuple-element.11), channel_id=1, source_target_pairs={{32,0},{64,32},{96,64},{128,96},{160,128},{192,160},{224,192},{256... | collective-permute-start | bytes 69128 | tf_op jit(solution)/shard_map/ppermute | solution.py:203
  49.2 14.2 %collective-permute-start.9 = (bf16[24,256]{1,0:T(8,128)(2,1)S(1)}, bf16[24,256]{1,0:T(8,128)(2,1)S(1)}, u32[]{:S(2)}, u32[]{:S(2)}) collective-permute-start(bf16[24,256]{1,0:T(8,128)(2,1)S(1)} %bitcast.133), channel_id=1, source_target_pairs={{1,0},{2,1},{3,2},{4,3},{5,4},{6,5},{7,6},{8,7},{9,8},{10,9},{11,1... | collective-permute-start | bytes 36872 | tf_op jit(solution)/shard_map/ppermute | solution.py:203
  61.5 13.2 %collective-permute-start.10 = (bf16[24,256]{1,0:T(8,128)(2,1)S(1)}, bf16[24,256]{1,0:T(8,128)(2,1)S(1)}, u32[]{:S(2)}, u32[]{:S(2)}) collective-permute-start(bf16[24,256]{1,0:T(8,128)(2,1)S(1)} %bitcast.135), channel_id=1, source_target_pairs={{0,1},{1,2},{2,3},{3,4},{4,5},{5,6},{6,7},{7,8},{8,9},{9,10},{10,1... | collective-permute-start | bytes 36872 | tf_op jit(solution)/shard_map/ppermute | solution.py:202
  75.9 0.8 copy-start.6
  75.9 1.0 copy-start.8
  78.6 3.8 %collective-permute-start.11 = (f32[384,256]{1,0:T(8,128)}, f32[384,256]{1,0:T(8,128)S(1)}, u32[]{:S(2)}, u32[]{:S(2)}) collective-permute-start(f32[384,256]{1,0:T(8,128)} %dynamic-slice_bitcast_fusion), channel_id=1, source_target_pairs={{0,32},{32,0},{64,96},{96,64},{128,160},{160,128},{192,224},{224,1... | collective-permute-start | bytes 1179656 | tf_op jit(solution)/shard_map/ppermute | solution.py:216
  83.2 10.5 %copy-start.3 = (f32[2,256,384]{2,1,0:T(8,128)S(1)}, f32[2,256,384]{2,1,0:T(8,128)}, u32[]{:S(2)}) copy-start(f32[2,256,384]{2,1,0:T(8,128)} %constant.61.clone.tw_ref) | copy-start | bytes 2359300
  83.2 10.5 %copy-start.4 = (bf16[192,768]{1,0:T(8,128)(2,1)S(1)}, bf16[192,768]{1,0:T(8,128)(2,1)}, u32[]{:S(2)}) copy-start(bf16[192,768]{1,0:T(8,128)(2,1)} %constant.62.clone.w_ref) | copy-start | bytes 884740
  83.2 10.5 %copy-start.5 = (bf16[512,256]{1,0:T(8,128)(2,1)S(1)}, bf16[512,256]{1,0:T(8,128)(2,1)}, u32[]{:S(2)}) copy-start(bf16[512,256]{1,0:T(8,128)(2,1)} %constant.60.clone.d_ref) | copy-start | bytes 786436
  87.1 30.8 %all-to-all-start.2 = ((f32[32,24,128]{2,1,0:T(8,128)}), f32[32,24,128]{2,1,0:T(8,128)}, u32[]{:S(2)}, u32[]{:S(2)}) async-start(f32[32,24,128]{2,1,0:T(8,128)} %bitcast.121), calls=%async_computation.2 | async-start | bytes 786432 | tf_op jit(solution)/shard_map/all_to_all | solution.py:221
  96.5 91.3 %copy-start.9 = (bf16[22,45,256]{2,1,0:T(8,128)(2,1)S(1)}, bf16[22,45,256]{2,1,0:T(8,128)(2,1)}, u32[]{:S(2)}) copy-start(bf16[22,45,256]{2,1,0:T(8,128)(2,1)} %copy-done.8) | copy-start | bytes 1520644
  117.8 64.1 %all-to-all-start.1 = ((bf16[32,40,128]{2,1,0:T(8,128)(2,1)}), bf16[32,40,128]{2,1,0:T(8,128)(2,1)S(1)}, u32[]{:S(2)}, u32[]{:S(2)}) async-start(bf16[32,40,128]{2,1,0:T(8,128)(2,1)} %fourier_chunks.1), calls=%async_computation.1 | async-start | bytes 655360 | tf_op jit(solution)/shard_map/all_to_all | solution.py:285
  132.9 11.3 %collective-permute-start.12 = (f32[24,128]{1,0:T(8,128)S(1)}, f32[24,128]{1,0:T(8,128)S(1)}, u32[]{:S(2)}, u32[]{:S(2)}) collective-permute-start(f32[24,128]{1,0:T(8,128)S(1)} %reduce_sum.19), channel_id=1, source_target_pairs={{0,512},{32,544},{64,576},{96,608},{128,640},{160,672},{192,704},{... | collective-permute-start | bytes 36872 | tf_op jit(solution)/shard_map/ppermute | solution.py:41
  137.7 6.5 %collective-permute-start.13 = (f32[24,128]{1,0:T(8,128)S(1)}, f32[24,128]{1,0:T(8,128)S(1)}, u32[]{:S(2)}, u32[]{:S(2)}) collective-permute-start(f32[24,128]{1,0:T(8,128)S(1)} %reduce_sum.19), channel_id=1, source_target_pairs={{0,256},{32,288},{64,320},{96,352},{128,384},{160,416},{192,448},{... | collective-permute-start | bytes 36872 | tf_op jit(solution)/shard_map/ppermute | solution.py:41
  140.0 5.1 %collective-permute-start.14 = (f32[24,128]{1,0:T(8,128)S(1)}, f32[24,128]{1,0:T(8,128)S(1)}, u32[]{:S(2)}, u32[]{:S(2)}) collective-permute-start(f32[24,128]{1,0:T(8,128)S(1)} %reduce_sum.19), channel_id=1, source_target_pairs={{0,768},{32,800},{64,832},{96,864},{128,896},{160,928},{192,960},{... | collective-permute-start | bytes 36872 | tf_op jit(solution)/shard_map/ppermute | solution.py:41
  145.0 35.4 %collective-permute-start.15 = (f32[24,128]{1,0:T(8,128)S(1)}, f32[24,128]{1,0:T(8,128)S(1)}, u32[]{:S(2)}, u32[]{:S(2)}) collective-permute-start(f32[24,128]{1,0:T(8,128)S(1)} %add_add_fusion), channel_id=1, source_target_pairs={{0,128},{32,160},{64,192},{96,224},{128,0},{160,32},{192,64},{224,... | collective-permute-start | bytes 36872 | tf_op jit(solution)/shard_map/ppermute | solution.py:41
  166.5 14.0 %collective-permute-start.16 = (f32[24,128]{1,0:T(8,128)S(1)}, f32[24,128]{1,0:T(8,128)S(1)}, u32[]{:S(2)}, u32[]{:S(2)}) collective-permute-start(f32[24,128]{1,0:T(8,128)S(1)} %add_add_fusion), channel_id=1, source_target_pairs={{0,64},{32,96},{64,128},{96,160},{128,192},{160,224},{192,0},{224,... | collective-permute-start | bytes 36872 | tf_op jit(solution)/shard_map/ppermute | solution.py:41
  168.7 13.3 %collective-permute-start.17 = (f32[24,128]{1,0:T(8,128)S(1)}, f32[24,128]{1,0:T(8,128)S(1)}, u32[]{:S(2)}, u32[]{:S(2)}) collective-permute-start(f32[24,128]{1,0:T(8,128)S(1)} %add_add_fusion), channel_id=1, source_target_pairs={{0,192},{32,224},{64,0},{96,32},{128,64},{160,96},{192,128},{224,1... | collective-permute-start | bytes 36872 | tf_op jit(solution)/shard_map/ppermute | solution.py:41
  182.7 19.8 %all-to-all-start.3 = ((bf16[32,24,128]{2,1,0:T(8,128)(2,1)}), bf16[32,24,128]{2,1,0:T(8,128)(2,1)S(1)}, u32[]{:S(2)}, u32[]{:S(2)}) async-start(bf16[32,24,128]{2,1,0:T(8,128)(2,1)} %broadcast_in_dim.14), calls=%async_computation.3 | async-start | bytes 393216 | tf_op jit(solution)/shard_map/all_to_all | solution.py:223
  187.8 1.0 copy-start.7
  189.0 1.3 copy-start.11
  190.3 0.9 copy-start.10
  190.3 0.9 copy-start.12
  195.7 11.8 %collective-permute-start = (f32[8,384]{1,0:T(8,128)S(1)}, f32[8,384]{1,0:T(8,128)S(1)}, u32[]{:S(2)}, u32[]{:S(2)}) collective-permute-start(f32[8,384]{1,0:T(8,128)S(1)} %broadcast_multiply_fusion), channel_id=1, source_target_pairs={{0,32},{32,0},{64,96},{96,64},{128,160},{160,128},{192,224},{224,1... | collective-permute-start | bytes 36872 | tf_op jit(solution)/shard_map/ppermute | solution.py:41
  202.7 16.1 %collective-permute-start.18 = (bf16[384,256]{1,0:T(8,128)(2,1)S(1)}, bf16[384,256]{1,0:T(8,128)(2,1)S(1)}, u32[]{:S(2)}, u32[]{:S(2)}) collective-permute-start(bf16[384,256]{1,0:T(8,128)(2,1)S(1)} %bitcast.131), channel_id=1, source_target_pairs={{0,32},{32,0},{64,96},{96,64},{128,160},{160,128},{192,224},{224,1... | collective-permute-start | bytes 589832 | tf_op jit(solution)/shard_map/ppermute | solution.py:226
  207.6 11.2 %collective-permute-start.1 = (f32[8,384]{1,0:T(8,128)S(1)}, f32[8,384]{1,0:T(8,128)S(1)}, u32[]{:S(2)}, u32[]{:S(2)}) collective-permute-start(f32[8,384]{1,0:T(8,128)S(1)} %fusion.19), channel_id=1, source_target_pairs={{0,512},{32,544},{64,576},{96,608},{128,640},{160,672},{192,704},{... | collective-permute-start | bytes 36872 | tf_op jit(solution)/shard_map/ppermute | solution.py:41
  212.3 6.6 %collective-permute-start.2 = (f32[8,384]{1,0:T(8,128)S(1)}, f32[8,384]{1,0:T(8,128)S(1)}, u32[]{:S(2)}, u32[]{:S(2)}) collective-permute-start(f32[8,384]{1,0:T(8,128)S(1)} %fusion.19), channel_id=1, source_target_pairs={{0,256},{32,288},{64,320},{96,352},{128,384},{160,416},{192,448},{... | collective-permute-start | bytes 36872 | tf_op jit(solution)/shard_map/ppermute | solution.py:41
  215.0 4.6 %collective-permute-start.3 = (f32[8,384]{1,0:T(8,128)S(1)}, f32[8,384]{1,0:T(8,128)S(1)}, u32[]{:S(2)}, u32[]{:S(2)}) collective-permute-start(f32[8,384]{1,0:T(8,128)S(1)} %fusion.19), channel_id=1, source_target_pairs={{0,768},{32,800},{64,832},{96,864},{128,896},{160,928},{192,960},{... | collective-permute-start | bytes 36872 | tf_op jit(solution)/shard_map/ppermute | solution.py:41
  219.6 26.6 %collective-permute-start.4 = (f32[8,384]{1,0:T(8,128)S(1)}, f32[8,384]{1,0:T(8,128)S(1)}, u32[]{:S(2)}, u32[]{:S(2)}) collective-permute-start(f32[8,384]{1,0:T(8,128)S(1)} %add_add_fusion.1), channel_id=1, source_target_pairs={{0,128},{32,160},{64,192},{96,224},{128,0},{160,32},{192,64},{224,... | collective-permute-start | bytes 36872 | tf_op jit(solution)/shard_map/ppermute | solution.py:41
  231.2 15.0 %collective-permute-start.5 = (f32[8,384]{1,0:T(8,128)S(1)}, f32[8,384]{1,0:T(8,128)S(1)}, u32[]{:S(2)}, u32[]{:S(2)}) collective-permute-start(f32[8,384]{1,0:T(8,128)S(1)} %add_add_fusion.1), channel_id=1, source_target_pairs={{0,64},{32,96},{64,128},{96,160},{128,192},{160,224},{192,0},{224,... | collective-permute-start | bytes 36872 | tf_op jit(solution)/shard_map/ppermute | solution.py:41
  243.0 13.2 %collective-permute-start.6 = (f32[8,384]{1,0:T(8,128)S(1)}, f32[8,384]{1,0:T(8,128)S(1)}, u32[]{:S(2)}, u32[]{:S(2)}) collective-permute-start(f32[8,384]{1,0:T(8,128)S(1)} %add_add_fusion.1), channel_id=1, source_target_pairs={{0,192},{32,224},{64,0},{96,32},{128,64},{160,96},{192,128},{224,1... | collective-permute-start | bytes 36872 | tf_op jit(solution)/shard_map/ppermute | solution.py:41

commit v2 on v1

--- a/solution.py
+++ b/solution.py
@@ -20,30 +20,57 @@
     return -(-value // step) * step
 
 
-CORE = (1, 2)
-Z_HI = (2, 4)
-X = (8, 4)
-
-
-def turn(total, digit, shift):
-    stride, size = digit
-    pairs = []
-    for source in range(total):
-        place = source // stride % size
-        pairs.append((source, source + ((place + shift) % size - place) * stride))
-    return pairs
-
-
-def sum_over_digits(value, digits):
-    total = lax.axis_size("lat")
-    for digit in digits:
-        parts = [value] + [
-            lax.ppermute(value, "lat", turn(total, digit, shift)) for shift in range(1, digit[1])
-        ]
-        while len(parts) > 1:
-            half = len(parts) // 2
-            parts = [parts[i] + parts[i + half] for i in range(half)]
-        value = parts[0]
+PARTS = (("x", 4), ("z_hi", 4), ("core", 2))
+LAT = tuple(name for name, _ in PARTS)
+LON_BITS = (8, 16, 1, 2, 4)
+
+
+def ring(size, step):
+    return [(i, (i + step) % size) for i in range(size)]
+
+
+def to_all(value, axes):
+    count = lax.axis_size(axes)
+    return lax.all_to_all(jnp.broadcast_to(value, (count, *value.shape)), axes, 0, 0)
+
+
+def sum_over(value, stages):
+    for axes in stages:
+        value = jnp.sum(to_all(value, axes), axis=0)
+    return value
+
+
+def pairs(size, bit):
+    return [(i, i ^ bit) for i in range(size)]
+
+
+def scatter_rows(value, axis, bits):
+    size, place = lax.axis_size(axis), lax.axis_index(axis)
+    left = sorted(bits, reverse=True)
+    value = value.reshape(*(2 for _ in left), -1, value.shape[-1])
+    for step, bit in enumerate(bits):
+        where = left.index(bit)
+        left.remove(bit)
+        low = lax.index_in_dim(value, 0, where, keepdims=False)
+        high = lax.index_in_dim(value, 1, where, keepdims=False)
+        upper = (place & bit) != 0
+        value, sent = jnp.where(upper, high, low), jnp.where(upper, low, high)
+        if step < 2:
+            sent = sent.astype(BF16)
+        value = value + lax.ppermute(sent, axis, pairs(size, bit)).astype(F32)
+    return value
+
+
+def sum_ring(value, axis):
+    far, near, back = (lax.ppermute(value, axis, ring(4, step)) for step in (2, 1, 3))
+    return (value + far) + (near + back)
+
+
+def sum_doubling(value, axis):
+    size, bit = lax.axis_size(axis), 1
+    while bit < size:
+        value = value + lax.ppermute(value, axis, pairs(size, bit))
+        bit *= 2
     return value
 
 
@@ -88,6 +115,9 @@
         out_shape=jax.ShapeDtypeStruct((channels, tall * wide), field.dtype),
         scratch_shapes=[pltpu.VMEM((tall, wide, channels), field.dtype)],
         compiler_params=pltpu.CompilerParams(vmem_limit_bytes=32 << 20),
+        cost_estimate=pl.CostEstimate(
+            flops=0, transcendentals=0, bytes_accessed=4 * channels * tall * wide
+        ),
         name="channels_first",
     )(field)
 
@@ -145,6 +175,11 @@
         out_shape=jax.ShapeDtypeStruct((groups, keep, LANES), BF16),
         scratch_shapes=[pltpu.VMEM((tall, orders * chans), F32)],
         compiler_params=pltpu.CompilerParams(vmem_limit_bytes=48 << 20),
+        cost_estimate=pl.CostEstimate(
+            flops=2 * sectors * chans * lanes * (2 * sectors * chans + 2 * turns * ROW * 2),
+            transcendentals=0,
+            bytes_accessed=2 * received.size + 2 * groups * keep * LANES + 4 * twiddle.size,
+        ),
         name="fourier_chunks",
     )(
         received.reshape(sectors * chans, lanes),
@@ -188,123 +223,143 @@
         out_shape=jax.ShapeDtypeStruct((orders, 2 * chans, used), BF16),
         scratch_shapes=[pltpu.VMEM((ceil_to(used, LANES), 2 * LANES), F32)],
         compiler_params=pltpu.CompilerParams(vmem_limit_bytes=32 << 20),
+        cost_estimate=pl.CostEstimate(
+            flops=0, transcendentals=0, bytes_accessed=2 * received.size + 4 * orders * chans * used
+        ),
         name="unfold",
     )(received)
 
 
-def padded_2(shard):
-    for axis, dim in (("lat", 0), ("lon", 1)):
-        size, length = (lax.axis_size(axis), shard.shape[dim])
-        up = [(i, (i + 1) % size) for i in range(size)]
-        down = [(j, i) for i, j in up]
-        last = lax.index_in_dim(shard, length - 1, axis=dim, keepdims=False)
-        first = lax.index_in_dim(shard, 0, axis=dim, keepdims=False)
-        before = jnp.expand_dims(lax.ppermute(last, axis, up), dim)
-        after = jnp.expand_dims(lax.ppermute(first, axis, down), dim)
-        shard = jnp.concatenate([before, shard, after], axis=dim)
-    return shard
-
-
-def total_taps(part):
-    shape = part.shape
-    lat, lon = lax.axis_size("lat"), lax.axis_size("lon")
-    core = lax.axis_index("lat") % 2
-    swap = turn(lat, CORE, 1)
-    halves = part.reshape(2, -1, shape[-1])
-    mine = lax.dynamic_index_in_dim(halves, core, 0, keepdims=False)
-    other = lax.dynamic_index_in_dim(halves, 1 - core, 0, keepdims=False)
-    mine = mine + lax.ppermute(other, "lat", swap)
-    rows, columns = mine.shape
-    parts = columns // LANES
-    high = rows * parts // lon
-    chunks = mine.reshape(lon // parts, high, parts, LANES).transpose(0, 2, 1, 3)
-    chunks = lax.all_to_all(chunks.reshape(lon, high, LANES), "lon", 0, 0)
-    chunk = sum_over_digits(jnp.sum(chunks, axis=0), (X, Z_HI)).astype(BF16)
-    chunks = lax.all_to_all(jnp.broadcast_to(chunk, (lon, high, LANES)), "lon", 0, 0)
-    mine = chunks.reshape(lon // parts, parts, high, LANES).transpose(0, 2, 1, 3)
-    mine = mine.reshape(rows, columns)
-    other = lax.ppermute(mine, "lat", swap)
-    low = jnp.where(core == 0, mine, other)
-    high = jnp.where(core == 0, other, mine)
-    return jnp.stack([low, high]).astype(F32).reshape(shape)
-
-
-def disco(grad_out, block_input, cycle_weight, cycle_shift, tap_weight):
-    rows_here, lons_here, channels = grad_out.shape
-    lon_total = lons_here * lax.axis_size("lon")
-    cycle_total = rows_here * lax.axis_size("lat")
-    padded = padded_2(grad_out)
-    cycle_start = lax.axis_index("lat") * rows_here
-    weight_pad = jnp.pad(cycle_weight, ((1, 1), (0, 0)))
-    shift_pad = jnp.pad(cycle_shift, ((1, 1), (0, 0)))
-    flat_input = block_input.reshape(-1, channels)
-    local_grad = jnp.zeros((rows_here * lons_here, channels), F32)
+def select(shifts, windows):
+    picked = jnp.zeros_like(windows[0])
+    for shift, window in zip((-1, 0, 1), windows):
+        picked = jnp.where((shifts == shift)[:, None, None], window, picked)
+    return picked
+
+
+def tap_rows(cycle_weight, cycle_shift, rows):
+    start = lax.axis_index(LAT) * rows
+    weights = jnp.pad(cycle_weight, ((1, 1), (0, 0)))
+    shifts = jnp.pad(cycle_shift, ((1, 1), (0, 0)))
+    taps = []
+    for index, offset in enumerate((-1, 0, 1)):
+        weight = lax.dynamic_slice_in_dim(weights, start + 1 - offset, rows, 0)[:, index]
+        shift = lax.dynamic_slice_in_dim(shifts, start + 1 - offset, rows, 0)[:, index]
+        taps.append((1 - offset, weight, shift))
+    return taps
+
+
+def scaled(weight, field):
+    return (weight[:, None, None] * field.astype(F32)).astype(BF16)
+
+
+def taps_part(grad_rows, block_input, before, after, taps):
+    rows, lons, channels = block_input.shape
+    wide = jnp.concatenate([before[:, None], block_input, after[:, None]], axis=1)
     partials = []
-    for tap_index, offset in enumerate((-1, 0, 1)):
-        source = padded[1 - offset : 1 - offset + rows_here]
-        coef = lax.dynamic_slice_in_dim(weight_pad, cycle_start + 1 - offset, rows_here, 0)[
-            :, tap_index
-        ]
-        shifts = lax.dynamic_slice_in_dim(shift_pad, cycle_start + 1 - offset, rows_here, 0)[
-            :, tap_index
-        ]
-        picked = jnp.zeros((rows_here, lons_here, channels), F32)
-        for column_shift in (-1, 0, 1):
-            window = source[:, 1 - column_shift : 1 - column_shift + lons_here].astype(F32)
-            picked = picked + (shifts == column_shift).astype(F32)[:, None, None] * window
-        spread = (coef[:, None, None] * picked).astype(BF16).reshape(-1, channels)
-        local_grad = local_grad + lax.dot_general(
-            spread,
-            tap_weight[tap_index],
+    for first, weight, shift in taps:
+        spread = scaled(weight, grad_rows[first : first + rows])
+        picked = select(shift, [wide[:, 1 + k : 1 + k + lons] for k in (-1, 0, 1)])
+        partials.append(
+            lax.dot_general(
+                picked.reshape(-1, channels),
+                spread.reshape(-1, channels),
+                (((0,), (0,)), ((), ())),
+                preferred_element_type=F32,
+            )
+        )
+    return jnp.concatenate(partials, axis=0)
+
+
+def input_part(grad_rows, before, after, taps, tap_weight):
+    rows, lons, channels = grad_rows.shape
+    rows -= 2
+    wide = jnp.concatenate([before[:, None], grad_rows, after[:, None]], axis=1)
+    total = jnp.zeros((rows * lons, channels), F32)
+    for index, (first, weight, shift) in enumerate(taps):
+        source = wide[first : first + rows]
+        picked = select(shift, [source[:, 1 - k : 1 - k + lons] for k in (-1, 0, 1)])
+        total = total + lax.dot_general(
+            scaled(weight, picked).reshape(-1, channels),
+            tap_weight[index],
             (((1,), (1,)), ((), ())),
             preferred_element_type=F32,
         )
-        partials.append(
-            lax.dot_general(flat_input, spread, (((0,), (0,)), ((), ())), preferred_element_type=F32)
-        )
-    taps_part = jnp.stack(partials) / math.sqrt(cycle_total * lon_total)
-    return local_grad.reshape(rows_here, lons_here, channels).astype(BF16), taps_part
+    return total.reshape(rows, lons, channels).astype(BF16)
 
 
 def on_device(
     grad_out, block_input, leg_table, spec_coeff, spec_filter, cycle_weight, cycle_shift, tap_weight
 ):
     rows_here, lons_here, channels = grad_out.shape
-    lat, lon = lax.axis_size("lat"), lax.axis_size("lon")
+    lat, lon = lax.axis_size(LAT), lax.axis_size("lon")
     chans = channels // lon
     orders_here, degrees, _ = leg_table.shape
     orders = orders_here * lat
+    core = lax.axis_index("core")
+    swap = ring(2, 1)
 
     sent = channels_first(grad_out).reshape(lon, chans, -1)
     rows = lax.all_to_all(sent, "lon", 0, 0)
 
-    input_grad, taps_part = disco(grad_out, block_input, cycle_weight, cycle_shift, tap_weight)
-    taps_grad = total_taps(taps_part)
+    above = lax.ppermute(grad_out[-1], LAT, ring(lat, 1))
+    below = lax.ppermute(grad_out[0], LAT, ring(lat, -1))
+    before = lax.ppermute(block_input[:, -1], "lon", ring(lon, 1))
+    after = lax.ppermute(block_input[:, 0], "lon", ring(lon, -1))
+    grad_rows = jnp.concatenate([above[None], grad_out, below[None]], axis=0)
+    taps = tap_rows(cycle_weight, cycle_shift, rows_here)
+    part = taps_part(grad_rows, block_input, before, after, taps)
+    part = part / math.sqrt(rows_here * lat * lons_here * lon)
+
+    left, right = part[:, : channels // 2], part[:, channels // 2 :]
+    mine, other = jnp.where(core == 0, left, right), jnp.where(core == 0, right, left)
+    high, width = mine.shape[0] // lon, mine.shape[1]
+    rows, other = lax.optimization_barrier((rows, other))
+    mine = mine + lax.ppermute(other, "core", swap)
 
     blocks = fourier_chunks(rows, rows_here, lons_here, orders, lat)
-    columns = lax.all_to_all(blocks, "lat", 0, 0)
+    blocks, edges = lax.optimization_barrier((blocks, (grad_rows[:, -1], grad_rows[:, 0])))
+    columns = lax.all_to_all(blocks, LAT, 0, 0)
+
+    before = lax.ppermute(edges[0], "lon", ring(lon, 1))
+    after = lax.ppermute(edges[1], "lon", ring(lon, -1))
+    input_grad = input_part(grad_rows, before, after, taps, tap_weight)
+
+    chunk = scatter_rows(mine, "lon", LON_BITS)
+    chunk = sum_ring(sum_doubling(chunk, "x"), "z_hi").astype(BF16)
     fourier = unfold(columns, rows_here, orders_here, chans)
     degree = jnp.einsum("mla,mxa->mxl", leg_table, fourier, preferred_element_type=F32)
     degree = degree.reshape(orders_here, 2, chans, degrees)
     spec_grad = (degree * spec_filter.T).astype(BF16).transpose(3, 0, 1, 2)
     coeff = spec_coeff.transpose(1, 2, 3, 0).astype(F32)
     filter_part = jnp.sum(coeff * degree, axis=(0, 1)) / math.sqrt(2 * orders)
-    filter_grad = sum_over_digits(filter_part, (CORE, X, Z_HI)).T
+    filter_part = sum_over(filter_part, (("x", "core"),))
+    filter_part, chunk = lax.optimization_barrier((filter_part, chunk))
+    filter_grad = sum_ring(filter_part, "z_hi").T
+
+    mine = to_all(chunk, "lon").reshape(lon * high, width)
+    mine, filter_grad = lax.optimization_barrier((mine, filter_grad))
+    other = lax.ppermute(mine, "core", swap)
+    left, right = jnp.where(core == 0, mine, other), jnp.where(core == 0, other, mine)
+    taps_grad = jnp.concatenate([left, right], axis=1).astype(F32)
+    taps_grad = taps_grad.reshape(len(taps), channels, channels)
     return (spec_grad, filter_grad, input_grad, taps_grad)
 
 
 def solution(mesh):
+    sizes = tuple(size for _, size in PARTS)
+    split = jax.sharding.Mesh(mesh.devices.reshape(*sizes, mesh.shape["lon"]), (*LAT, "lon"))
     in_specs = (
-        P("lat", "lon", None),
-        P("lat", "lon", None),
-        P("lat", None, None),
-        P(None, "lat", None, "lon"),
+        P(LAT, "lon", None),
+        P(LAT, "lon", None),
+        P(LAT, None, None),
+        P(None, LAT, None, "lon"),
         P(None, "lon"),
         P(),
         P(),
         P(),
     )
-    out_specs = (P(None, "lat", None, "lon"), P(None, "lon"), P("lat", "lon", None), P())
+    out_specs = (P(None, LAT, None, "lon"), P(None, "lon"), P(LAT, "lon", None), P())
     return jax.shard_map(
-        on_device, mesh=mesh, in_specs=in_specs, out_specs=out_specs, check_vma=False
+        on_device, mesh=split, in_specs=in_specs, out_specs=out_specs, check_vma=False
     )

time: 260 us -> 261 us (level)
  waiting for transfers between devices: 59.2 us -> 64.6 us
  local copies, waits for them, and re-layouts: 9.54 us -> 5 us
    ppermute x19 -> x21, waiting for transfers between devices: 37.8 us -> 59.6 us  [the longest x5 29.3 us: scatter_rows(): value = value + lax.ppermute(sent, axis, pairs(size, bit)).astype(F32)]
    all_to_all x3, waiting for transfers between devices: 21.3 us -> 4.97 us  [the longest x2 4.97 us: to_all(): lax.all_to_all(jnp.broadcast_to(value, (count, *value.shape)), axes, 0, 0)]
    ppermute x19 -> x21, starting transfers between devices: 128 us -> 127 us  [the longest x6 54.1 us: sum_ring(): lax.ppermute(value, axis, ring(4, step))]
  transfers between devices with their start and end apart: 23 -> 25, of which waited for: 8 -> 10; matrix products, arithmetic and copies ran while one was open for 7% -> 7% of each run, Pallas kernels for 1% -> 1%
where the time goes in v2:
time: 261 us; the launch traced here: 260 us
  starting transfers between devices  170 us (65%)
  waiting for transfers between devices  64.6 us (25%)
  matrix products  8.71 us (3%)
  other arithmetic  5.74 us (2%)
  local copies, waits for them, and re-layouts  5 us (2%)
  Pallas kernels  3.98 us (2%)
    ppermute x6, starting transfers between devices, sum_ring(): lax.ppermute(value, axis, ring(4, step))  54.1 us
    ppermute x5, waiting for transfers between devices, scatter_rows(): value = value + lax.ppermute(sent, axis, pairs(size, bit)).astype(F32)  29.3 us
    ppermute x6, waiting for transfers between devices, sum_ring(): lax.ppermute(value, axis, ring(4, step))  19.1 us
    ppermute x1, starting transfers between devices, on_device(): above = lax.ppermute(grad_out[-1], LAT, ring(lat, 1))  16.3 us
    all_to_all x1, starting transfers between devices, on_device(): rows = lax.all_to_all(sent, 'lon', 0, 0)  16.1 us
    all_to_all x1, starting transfers between devices, on_device(): columns = lax.all_to_all(blocks, LAT, 0, 0)  14.3 us
    all_to_all x2, starting transfers between devices, to_all(): lax.all_to_all(jnp.broadcast_to(value, (count, *value.shape)), axes, 0, 0)  12.7 us
    ppermute x5, starting transfers between devices, scatter_rows(): value = value + lax.ppermute(sent, axis, pairs(size, bit)).astype(F32)  12.6 us
  transfers between devices with their start and end apart: 25, of which 10 were waited for; matrix products, arithmetic and copies ran while one was open for 7% of the time, Pallas kernels for 1%

profile of v2, /device:TPU:1, one launch (start us, length us, event | category | flops | bytes accessed | tf_op | source)
XLA Modules:
  0.0 259.9 jit_solution(12964842791923229710)
XLA Ops:
  0.6 1.0 copy-done
  1.7 1.0 channels_first.1
  2.7 16.1 %all-to-all-start = ((bf16[32,8,1152]{2,1,0:T(8,128)(2,1)}), bf16[32,8,1152]{2,1,0:T(8,128)(2,1)S(1)}, u32[]{:S(2)}, u32[]{:S(2)}) async-start(bf16[32,8,1152]{2,1,0:T(8,128)(2,1)} %bitcast), calls=%async_computation | async-start | bytes 1179648 | tf_op jit(solution)/shard_map/all_to_all | solution.py:303
  18.9 16.3 %collective-permute-start.3 = (bf16[45,256]{1,0:T(8,128)(2,1)S(1)}, bf16[45,256]{1,0:T(8,128)(2,1)S(1)}, u32[]{:S(2)}, u32[]{:S(2)}) collective-permute-start(bf16[45,256]{1,0:T(8,128)(2,1)S(1)} %get-tuple-element.29), channel_id=1, source_target_pairs={{0,32},{32,64},{64,96},{96,128},{128,160},{160,192},{192,224},{224... | collective-permute-start | bytes 69128 | tf_op jit(solution)/shard_map/ppermute | solution.py:305
  35.2 12.2 %collective-permute-start = (bf16[22,256]{1,0:T(8,128)(2,1)S(1)}, bf16[22,256]{1,0:T(8,128)(2,1)S(1)}, u32[]{:S(2)}, u32[]{:S(2)}) collective-permute-start(bf16[22,256]{1,0:T(8,128)(2,1)S(1)} %bitcast.163), channel_id=1, source_target_pairs={{0,31},{1,0},{2,1},{3,2},{4,3},{5,4},{6,5},{7,6},{8,7},{9,8},{10,9... | collective-permute-start | bytes 33800 | tf_op jit(solution)/shard_map/ppermute | solution.py:308
  47.5 1.9 collective-permute-start.1
  49.4 1.9 collective-permute-start.2
  51.3 0.1 pad_dynamic-slice_fusion.2
  51.4 0.1 pad_dynamic-slice_fusion.5
  51.7 8.9 %collective-permute-done.1 = bf16[22,256]{1,0:T(8,128)(2,1)S(1)} collective-permute-done((bf16[22,256]{1,0:T(8,128)(2,1)S(1)}, bf16[22,256]{1,0:T(8,128)(2,1)S(1)}, u32[]{:S(2)}, u32[]{:S(2)}) %collective-permute-start.1) | collective-permute-done | bytes 11296 | tf_op jit(solution)/shard_map/ppermute | solution.py:307
  60.6 0.7 convolution_bitcast_fusion.2
  61.5 0.7 convolution_bitcast_fusion.1
  62.2 1.0 collective-permute-done.2
  63.3 0.7 convolution_bitcast_fusion.3
  64.0 0.1 maximum_multiply_fusion
  64.1 0.8 slice_select_fusion.3
  64.9 1.9 collective-permute-start.4
  66.9 0.6 copy_bitcast_fusion.2
  67.5 2.7 %fourier_chunks.1 = bf16[32,40,128]{2,1,0:T(8,128)(2,1)} custom-call(bf16[256,1152]{1,0:T(8,128)(2,1)S(1)} %bitcast.147, bf16[512,256]{1,0:T(8,128)(2,1)S(1)} %copy-done.4, f32[2,256,384]{2,1,0:T(8,128)S(1)} %copy-done.2, bf16[192,768]{1,0:T(8,128)(2,1)S(1)} %copy-done.3), custom_call_target="tpu_custom_call" | custom-call | flops 528482304 | bytes 1703936 | tf_op jit(solution)/shard_map/fourier_chunks/pallas_call | solution.py:173
  70.2 14.3 %all-to-all-start.1 = ((bf16[32,40,128]{2,1,0:T(8,128)(2,1)}), bf16[32,40,128]{2,1,0:T(8,128)(2,1)S(1)}, u32[]{:S(2)}, u32[]{:S(2)}) async-start(bf16[32,40,128]{2,1,0:T(8,128)(2,1)} %fourier_chunks.1), calls=%async_computation.1 | async-start | bytes 655360 | tf_op jit(solution)/shard_map/all_to_all | solution.py:322
  84.6 1.1 select_add_fusion
  85.7 1.9 collective-permute-start.5
  87.6 4.1 %collective-permute-done.5 = bf16[2,2,2,2,24,128]{5,4,3,2,1,0:T(8,128)(2,1)S(1)} collective-permute-done((bf16[2,2,2,2,24,128]{5,4,3,2,1,0:T(8,128)(2,1)S(1)}, bf16[2,2,2,2,24,128]{5,4,3,2,1,0:T(8,128)(2,1)S(1)}, u32[]{:S(2)}, u32[]{:S(2)}) %collective-permute-start.5) | collective-permute-done | bytes 98336 | tf_op jit(solution)/shard_map/ppermute | solution.py:60
  91.8 2.5 collective-permute-start.6
  94.3 4.1 %collective-permute-done.6 = bf16[2,2,2,24,128]{4,3,2,1,0:T(8,128)(2,1)S(1)} collective-permute-done((bf16[2,2,2,24,128]{4,3,2,1,0:T(8,128)(2,1)S(1)}, bf16[2,2,2,24,128]{4,3,2,1,0:T(8,128)(2,1)S(1)}, u32[]{:S(2)}, u32[]{:S(2)}) %collective-permute-start.6) | collective-permute-done | bytes 49184 | tf_op jit(solution)/shard_map/ppermute | solution.py:60
  98.5 1.9 collective-permute-start.7
  100.4 10.5 %collective-permute-done.7 = f32[2,2,24,128]{3,2,1,0:T(8,128)S(1)} collective-permute-done((f32[2,2,24,128]{3,2,1,0:T(8,128)S(1)}, f32[2,2,24,128]{3,2,1,0:T(8,128)S(1)}, u32[]{:S(2)}, u32[]{:S(2)}) %collective-permute-start.7) | collective-permute-done | bytes 49184 | tf_op jit(solution)/shard_map/ppermute | solution.py:60
  110.9 1.9 collective-permute-start.8
  112.9 6.2 %collective-permute-done.8 = f32[2,24,128]{2,1,0:T(8,128)S(1)} collective-permute-done((f32[2,24,128]{2,1,0:T(8,128)S(1)}, f32[2,24,128]{2,1,0:T(8,128)S(1)}, u32[]{:S(2)}, u32[]{:S(2)}) %collective-permute-start.8) | collective-permute-done | bytes 24608 | tf_op jit(solution)/shard_map/ppermute | solution.py:60
  119.1 4.3 %collective-permute-start.9 = (f32[24,128]{1,0:T(8,128)S(1)}, f32[24,128]{1,0:T(8,128)S(1)}, u32[]{:S(2)}, u32[]{:S(2)}) collective-permute-start(f32[24,128]{1,0:T(8,128)S(1)} %select_bitcast_fusion.2), channel_id=1, source_target_pairs={{0,4},{1,5},{2,6},{3,7},{4,0},{5,1},{6,2},{7,3},{8,12},{9,13},{10,... | collective-permute-start | bytes 36872 | tf_op jit(solution)/shard_map/ppermute | solution.py:60
  123.5 4.4 %collective-permute-done.9 = f32[24,128]{1,0:T(8,128)S(1)} collective-permute-done((f32[24,128]{1,0:T(8,128)S(1)}, f32[24,128]{1,0:T(8,128)S(1)}, u32[]{:S(2)}, u32[]{:S(2)}) %collective-permute-start.9) | collective-permute-done | bytes 12320 | tf_op jit(solution)/shard_map/ppermute | solution.py:60
  127.8 3.1 %collective-permute-start.10 = (f32[24,128]{1,0:T(8,128)S(1)}, f32[24,128]{1,0:T(8,128)S(1)}, u32[]{:S(2)}, u32[]{:S(2)}) collective-permute-start(f32[24,128]{1,0:T(8,128)S(1)} %bitcast_add_fusion.1), channel_id=1, source_target_pairs={{0,256},{256,0},{512,768},{768,512},{1,257},{257,1},{513,769},{769... | collective-permute-start | bytes 36872 | tf_op jit(solution)/shard_map/ppermute | solution.py:72
  130.9 1.3 collective-permute-done.10
  132.3 4.5 %collective-permute-start.11 = (f32[24,128]{1,0:T(8,128)S(1)}, f32[24,128]{1,0:T(8,128)S(1)}, u32[]{:S(2)}, u32[]{:S(2)}) collective-permute-start(f32[24,128]{1,0:T(8,128)S(1)} %add.100), channel_id=1, source_target_pairs={{0,512},{256,768},{512,0},{768,256},{1,513},{257,769},{513,1},{769... | collective-permute-start | bytes 36872 | tf_op jit(solution)/shard_map/ppermute | solution.py:72
  136.7 1.9 collective-permute-start.18
  138.7 12.1 %collective-permute-start.19 = (bf16[24,256]{1,0:T(8,128)(2,1)S(1)}, bf16[24,256]{1,0:T(8,128)(2,1)S(1)}, u32[]{:S(2)}, u32[]{:S(2)}) collective-permute-start(bf16[24,256]{1,0:T(8,128)(2,1)S(1)} %get-tuple-element.20), channel_id=1, source_target_pairs={{0,31},{1,0},{2,1},{3,2},{4,3},{5,4},{6,5},{7,6},{8,7},{9,8},{10,9... | collective-permute-start | bytes 36872 | tf_op jit(solution)/shard_map/ppermute | solution.py:325
  150.8 12.1 %collective-permute-start.13 = (f32[24,128]{1,0:T(8,128)S(1)}, f32[24,128]{1,0:T(8,128)S(1)}, u32[]{:S(2)}, u32[]{:S(2)}) collective-permute-start(f32[24,128]{1,0:T(8,128)S(1)} %add.101), channel_id=1, source_target_pairs={{0,64},{64,128},{128,192},{192,0},{1,65},{65,129},{129,193},{193,1... | collective-permute-start | bytes 36872 | tf_op jit(solution)/shard_map/ppermute | solution.py:65
  162.9 2.8 %collective-permute-start.14 = (f32[24,128]{1,0:T(8,128)S(1)}, f32[24,128]{1,0:T(8,128)S(1)}, u32[]{:S(2)}, u32[]{:S(2)}) collective-permute-start(f32[24,128]{1,0:T(8,128)S(1)} %add.101), channel_id=1, source_target_pairs={{0,192},{64,0},{128,64},{192,128},{1,193},{65,1},{129,65},{193,129... | collective-permute-start | bytes 36872 | tf_op jit(solution)/shard_map/ppermute | solution.py:65
  165.7 21.7 %collective-permute-start.12 = (f32[24,128]{1,0:T(8,128)S(1)}, f32[24,128]{1,0:T(8,128)S(1)}, u32[]{:S(2)}, u32[]{:S(2)}) collective-permute-start(f32[24,128]{1,0:T(8,128)S(1)} %add.101), channel_id=1, source_target_pairs={{0,128},{64,192},{128,0},{192,64},{1,129},{65,193},{129,1},{193,65... | collective-permute-start | bytes 36872 | tf_op jit(solution)/shard_map/ppermute | solution.py:65
  187.4 0.2 unfold.1
  187.7 4.5 %fusion.28 = (f32[8,384]{1,0:T(8,128)S(1)}, bf16[384,12,2,8]{0,3,2,1:T(8,128)(2,1)}) fusion(bf16[384,12,2,8]{0,3,2,1:T(8,128)(2,1)S(1)} %copy-done.5, f32[8,384]{1,0:T(8,128)S(1)} %bitcast.162, bf16[12,16,704]{2,1,0:T(8,128)(2,1)S(1)} %unfold.1, bf16[12,384,704]{1,2,0:T(8,128)(2,1)} %param.13), kind=kOutput, calls=%fused_computation.54 | convolution fusion | flops 104174592 | bytes 7077888 | tf_op jit(solution)/shard_map/mla,mxa->mxl/dot_general | solution.py:331
  192.2 0.7 broadcast_in_dim.131
  192.9 8.8 %all-to-all-start.2 = ((f32[8,8,384]{2,1,0:T(8,128)}), f32[8,8,384]{2,1,0:T(8,128)S(1)}, u32[]{:S(2)}, u32[]{:S(2)}) async-start(f32[8,8,384]{2,1,0:T(8,128)} %broadcast_in_dim.131), calls=%async_computation.2 | async-start | bytes 196608 | tf_op jit(solution)/shard_map/all_to_all | solution.py:34
  201.7 5.0 %all-to-all-done.2 = f32[8,8,384]{2,1,0:T(8,128)S(1)} async-done(((f32[8,8,384]{2,1,0:T(8,128)}), f32[8,8,384]{2,1,0:T(8,128)S(1)}, u32[]{:S(2)}, u32[]{:S(2)}) %all-to-all-start.2) | async-done | bytes 98336 | tf_op jit(solution)/shard_map/all_to_all | solution.py:34
  206.7 0.7 broadcast_in_dim.132
  207.4 3.9 %all-to-all-start.3 = ((bf16[32,24,128]{2,1,0:T(8,128)(2,1)}), bf16[32,24,128]{2,1,0:T(8,128)(2,1)S(1)}, u32[]{:S(2)}, u32[]{:S(2)}) async-start(bf16[32,24,128]{2,1,0:T(8,128)(2,1)} %broadcast_in_dim.132), calls=%async_computation.3 | async-start | bytes 393216 | tf_op jit(solution)/shard_map/all_to_all | solution.py:34
  211.4 0.4 maximum_maximum_fusion
  211.9 0.4 multiply_convert_fusion.2
  212.3 0.2 reshape.137
  212.4 0.1 copy-done.22
  212.5 1.2 multiply_convert_fusion
  213.8 0.2 reshape.138
  213.9 1.3 fusion.37
  215.2 2.1 collective-permute-start.16
  217.3 11.9 %collective-permute-start.17 = (f32[8,384]{1,0:T(8,128)S(1)}, f32[8,384]{1,0:T(8,128)S(1)}, u32[]{:S(2)}, u32[]{:S(2)}) collective-permute-start(f32[8,384]{1,0:T(8,128)S(1)} %reduce_sum.19), channel_id=1, source_target_pairs={{0,192},{64,0},{128,64},{192,128},{1,193},{65,1},{129,65},{193,129... | collective-permute-start | bytes 36872 | tf_op jit(solution)/shard_map/ppermute | solution.py:65
  229.2 3.5 %collective-permute-start.15 = (f32[8,384]{1,0:T(8,128)S(1)}, f32[8,384]{1,0:T(8,128)S(1)}, u32[]{:S(2)}, u32[]{:S(2)}) collective-permute-start(f32[8,384]{1,0:T(8,128)S(1)} %reduce_sum.19), channel_id=1, source_target_pairs={{0,128},{64,192},{128,0},{192,64},{1,129},{65,193},{129,1},{193,65... | collective-permute-start | bytes 36872 | tf_op jit(solution)/shard_map/ppermute | solution.py:65
  232.8 0.3 convolution_add_fusion.1
  233.1 0.2 reshape.139
  233.3 19.1 %collective-permute-done.15 = f32[8,384]{1,0:T(8,128)S(1)} collective-permute-done((f32[8,384]{1,0:T(8,128)S(1)}, f32[8,384]{1,0:T(8,128)S(1)}, u32[]{:S(2)}, u32[]{:S(2)}) %collective-permute-start.15) | collective-permute-done | bytes 12320 | tf_op jit(solution)/shard_map/ppermute | solution.py:65
  252.3 0.6 add_bitcast_fusion
  252.9 4.7 %collective-permute-start.20 = (bf16[768,128]{1,0:T(8,128)(2,1)S(1)}, bf16[768,128]{1,0:T(8,128)(2,1)S(1)}, u32[]{:S(2)}, u32[]{:S(2)}) collective-permute-start(bf16[768,128]{1,0:T(8,128)(2,1)S(1)} %bitcast.152), channel_id=1, source_target_pairs={{0,32},{32,0},{1,33},{33,1},{2,34},{34,2},{3,35},{35,3},{4,36},{36... | collective-permute-start | bytes 589832 | tf_op jit(solution)/shard_map/ppermute | solution.py:342
  257.6 0.3 fusion
  258.0 1.0 convert_element_type.101
  259.0 0.9 maximum_convert_fusion
  (102 shorter events, 0.6 us)
Async XLA Ops:
  0.6 1.0 copy-start
  1.7 17.2 %copy-start.1 = (bf16[22,45,256]{2,1,0:T(8,128)(2,1)S(1)}, bf16[22,45,256]{2,1,0:T(8,128)(2,1)}, u32[]{:S(2)}) copy-start(bf16[22,45,256]{2,1,0:T(8,128)(2,1)} %x_ref.1) | copy-start | bytes 1520644
  1.7 33.5 %copy-start.10 = (bf16[22,45,256]{2,1,0:T(8,128)(2,1)S(1)}, bf16[22,45,256]{2,1,0:T(8,128)(2,1)}, u32[]{:S(2)}) copy-start(bf16[22,45,256]{2,1,0:T(8,128)(2,1)} %param.12) | copy-start | bytes 1520644
  1.7 49.6 %copy-start.8 = (f32[704,3]{0,1:T(4,128)S(1)}, f32[704,3]{0,1:T(4,128)}, u32[]{:S(2)}) copy-start(f32[704,3]{0,1:T(4,128)} %param.16) | copy-start | bytes 25348
  1.7 49.8 %copy-start.9 = (s32[704,3]{0,1:T(4,128)S(1)}, s32[704,3]{0,1:T(4,128)}, u32[]{:S(2)}) copy-start(s32[704,3]{0,1:T(4,128)} %param.17) | copy-start | bytes 25348
  2.7 62.2 %all-to-all-start = ((bf16[32,8,1152]{2,1,0:T(8,128)(2,1)}), bf16[32,8,1152]{2,1,0:T(8,128)(2,1)S(1)}, u32[]{:S(2)}, u32[]{:S(2)}) async-start(bf16[32,8,1152]{2,1,0:T(8,128)(2,1)} %bitcast), calls=%async_computation | async-start | bytes 1179648 | tf_op jit(solution)/shard_map/all_to_all | solution.py:303
  18.9 42.6 %collective-permute-start.3 = (bf16[45,256]{1,0:T(8,128)(2,1)S(1)}, bf16[45,256]{1,0:T(8,128)(2,1)S(1)}, u32[]{:S(2)}, u32[]{:S(2)}) collective-permute-start(bf16[45,256]{1,0:T(8,128)(2,1)S(1)} %get-tuple-element.29), channel_id=1, source_target_pairs={{0,32},{32,64},{64,96},{96,128},{128,160},{160,192},{192,224},{224... | collective-permute-start | bytes 69128 | tf_op jit(solution)/shard_map/ppermute | solution.py:305
  35.2 16.5 %collective-permute-start = (bf16[22,256]{1,0:T(8,128)(2,1)S(1)}, bf16[22,256]{1,0:T(8,128)(2,1)S(1)}, u32[]{:S(2)}, u32[]{:S(2)}) collective-permute-start(bf16[22,256]{1,0:T(8,128)(2,1)S(1)} %bitcast.163), channel_id=1, source_target_pairs={{0,31},{1,0},{2,1},{3,2},{4,3},{5,4},{6,5},{7,6},{8,7},{9,8},{10,9... | collective-permute-start | bytes 33800 | tf_op jit(solution)/shard_map/ppermute | solution.py:308
  47.5 13.2 %collective-permute-start.1 = (bf16[22,256]{1,0:T(8,128)(2,1)S(1)}, bf16[22,256]{1,0:T(8,128)(2,1)S(1)}, u32[]{:S(2)}, u32[]{:S(2)}) collective-permute-start(bf16[22,256]{1,0:T(8,128)(2,1)S(1)} %bitcast.165), channel_id=1, source_target_pairs={{0,1},{1,2},{2,3},{3,4},{4,5},{5,6},{6,7},{7,8},{8,9},{9,10},{10,1... | collective-permute-start | bytes 33800 | tf_op jit(solution)/shard_map/ppermute | solution.py:307
  49.4 13.9 %collective-permute-start.2 = (bf16[45,256]{1,0:T(8,128)(2,1)S(1)}, bf16[45,256]{1,0:T(8,128)(2,1)S(1)}, u32[]{:S(2)}, u32[]{:S(2)}) collective-permute-start(bf16[45,256]{1,0:T(8,128)(2,1)S(1)} %get-tuple-element.28), channel_id=1, source_target_pairs={{0,992},{32,0},{64,32},{96,64},{128,96},{160,128},{192,160},{224,1... | collective-permute-start | bytes 69128 | tf_op jit(solution)/shard_map/ppermute | solution.py:306
  51.5 11.7 %copy-start.15 = (pred[22]{0:T(512)(128)(4,1)}, pred[22]{0:T(512)(128)(4,1)S(1)}, u32[]{:S(2)}) copy-start(pred[22]{0:T(512)(128)(4,1)S(1)} %get-tuple-element.42) | copy-start | bytes 70
  51.5 11.7 %copy-start.17 = (pred[22]{0:T(512)(128)(4,1)}, pred[22]{0:T(512)(128)(4,1)S(1)}, u32[]{:S(2)}) copy-start(pred[22]{0:T(512)(128)(4,1)S(1)} %get-tuple-element.43) | copy-start | bytes 70
  51.5 11.7 %copy-start.19 = (pred[22]{0:T(512)(128)(4,1)}, pred[22]{0:T(512)(128)(4,1)S(1)}, u32[]{:S(2)}) copy-start(pred[22]{0:T(512)(128)(4,1)S(1)} %get-tuple-element.44) | copy-start | bytes 70
  51.6 9.8 %copy-start.13 = (f32[22]{0:T(128)}, f32[22]{0:T(128)S(1)}, u32[]{:S(2)}) copy-start(f32[22]{0:T(128)S(1)} %get-tuple-element.55) | copy-start | bytes 268
  51.6 9.9 %copy-start.11 = (f32[22]{0:T(128)}, f32[22]{0:T(128)S(1)}, u32[]{:S(2)}) copy-start(f32[22]{0:T(128)S(1)} %get-tuple-element.54) | copy-start | bytes 268
  51.6 9.8 %copy-start.25 = (pred[22]{0:T(512)(128)(4,1)}, pred[22]{0:T(512)(128)(4,1)S(1)}, u32[]{:S(2)}) copy-start(pred[22]{0:T(512)(128)(4,1)S(1)} %get-tuple-element.51) | copy-start | bytes 70
  51.6 9.8 %copy-start.26 = (pred[22]{0:T(512)(128)(4,1)}, pred[22]{0:T(512)(128)(4,1)S(1)}, u32[]{:S(2)}) copy-start(pred[22]{0:T(512)(128)(4,1)S(1)} %get-tuple-element.52) | copy-start | bytes 70
  51.6 9.8 %copy-start.27 = (pred[22]{0:T(512)(128)(4,1)}, pred[22]{0:T(512)(128)(4,1)S(1)}, u32[]{:S(2)}) copy-start(pred[22]{0:T(512)(128)(4,1)S(1)} %get-tuple-element.53) | copy-start | bytes 70
  51.6 9.8 %copy-start.21 = (pred[22]{0:T(512)(128)(4,1)}, pred[22]{0:T(512)(128)(4,1)S(1)}, u32[]{:S(2)}) copy-start(pred[22]{0:T(512)(128)(4,1)S(1)} %get-tuple-element.48) | copy-start | bytes 70
  51.7 10.6 %copy-start.23 = (pred[22]{0:T(512)(128)(4,1)}, pred[22]{0:T(512)(128)(4,1)S(1)}, u32[]{:S(2)}) copy-start(pred[22]{0:T(512)(128)(4,1)S(1)} %get-tuple-element.49) | copy-start | bytes 70
  51.7 10.6 %copy-start.24 = (pred[22]{0:T(512)(128)(4,1)}, pred[22]{0:T(512)(128)(4,1)S(1)}, u32[]{:S(2)}) copy-start(pred[22]{0:T(512)(128)(4,1)S(1)} %get-tuple-element.50) | copy-start | bytes 70
  51.7 11.6 %copy-start.28 = (f32[22]{0:T(128)}, f32[22]{0:T(128)S(1)}, u32[]{:S(2)}) copy-start(f32[22]{0:T(128)S(1)} %slice_bitcast_fusion.4) | copy-start | bytes 268
  64.1 3.4 %copy-start.2 = (f32[2,256,384]{2,1,0:T(8,128)S(1)}, f32[2,256,384]{2,1,0:T(8,128)}, u32[]{:S(2)}) copy-start(f32[2,256,384]{2,1,0:T(8,128)} %constant.66.clone.tw_ref) | copy-start | bytes 2359300
  64.1 3.4 %copy-start.3 = (bf16[192,768]{1,0:T(8,128)(2,1)S(1)}, bf16[192,768]{1,0:T(8,128)(2,1)}, u32[]{:S(2)}) copy-start(bf16[192,768]{1,0:T(8,128)(2,1)} %constant.67.clone.w_ref) | copy-start | bytes 884740
  64.1 3.4 %copy-start.4 = (bf16[512,256]{1,0:T(8,128)(2,1)S(1)}, bf16[512,256]{1,0:T(8,128)(2,1)}, u32[]{:S(2)}) copy-start(bf16[512,256]{1,0:T(8,128)(2,1)} %constant.65.clone.d_ref) | copy-start | bytes 786436
  64.9 19.7 %collective-permute-start.4 = (f32[768,128]{1,0:T(8,128)}, f32[768,128]{1,0:T(8,128)}, u32[]{:S(2)}, u32[]{:S(2)}) collective-permute-start(f32[768,128]{1,0:T(8,128)} %slice_select_fusion.3), channel_id=1, source_target_pairs={{0,32},{32,0},{1,33},{33,1},{2,34},{34,2},{3,35},{35,3},{4,36},{36... | collective-permute-start | bytes 1179656 | tf_op jit(solution)/shard_map/ppermute | solution.py:318
  70.2 117.2 %all-to-all-start.1 = ((bf16[32,40,128]{2,1,0:T(8,128)(2,1)}), bf16[32,40,128]{2,1,0:T(8,128)(2,1)S(1)}, u32[]{:S(2)}, u32[]{:S(2)}) async-start(bf16[32,40,128]{2,1,0:T(8,128)(2,1)} %fourier_chunks.1), calls=%async_computation.1 | async-start | bytes 655360 | tf_op jit(solution)/shard_map/all_to_all | solution.py:322
  85.7 6.1 %collective-permute-start.5 = (bf16[2,2,2,2,24,128]{5,4,3,2,1,0:T(8,128)(2,1)S(1)}, bf16[2,2,2,2,24,128]{5,4,3,2,1,0:T(8,128)(2,1)S(1)}, u32[]{:S(2)}, u32[]{:S(2)}) collective-permute-start(bf16[2,2,2,2,24,128]{5,4,3,2,1,0:T(8,128)(2,1)S(1)} %fusion.42), channel_id=1, source_target_pairs={{0,8},{1,9},{2,10},{3,11},{4,12},{5,13},{6,14},{7,15},{8,0},{9,1},... | collective-permute-start | bytes 294920 | tf_op jit(solution)/shard_map/ppermute | solution.py:60
  87.6 100.0 %copy-start.5 = (bf16[384,12,2,8]{0,3,2,1:T(8,128)(2,1)S(1)}, bf16[384,12,2,8]{0,3,2,1:T(8,128)(2,1)}, u32[]{:S(2)}) copy-start(bf16[384,12,2,8]{0,3,2,1:T(8,128)(2,1)} %param.14) | copy-start | bytes 442372
  87.6 100.0 %copy-start.7 = (f32[384,8]{0,1:T(8,128)S(1)}, f32[384,8]{0,1:T(8,128)}, u32[]{:S(2)}) copy-start(f32[384,8]{0,1:T(8,128)} %param.15) | copy-start | bytes 36868
  91.8 6.6 %collective-permute-start.6 = (bf16[2,2,2,24,128]{4,3,2,1,0:T(8,128)(2,1)S(1)}, bf16[2,2,2,24,128]{4,3,2,1,0:T(8,128)(2,1)S(1)}, u32[]{:S(2)}, u32[]{:S(2)}) collective-permute-start(bf16[2,2,2,24,128]{4,3,2,1,0:T(8,128)(2,1)S(1)} %fusion.43), channel_id=1, source_target_pairs={{0,16},{1,17},{2,18},{3,19},{4,20},{5,21},{6,22},{7,23},{8,24},{9,... | collective-permute-start | bytes 147464 | tf_op jit(solution)/shard_map/ppermute | solution.py:60
  98.5 12.5 %collective-permute-start.7 = (f32[2,2,24,128]{3,2,1,0:T(8,128)S(1)}, f32[2,2,24,128]{3,2,1,0:T(8,128)S(1)}, u32[]{:S(2)}, u32[]{:S(2)}) collective-permute-start(f32[2,2,24,128]{3,2,1,0:T(8,128)S(1)} %select_bitcast_fusion), channel_id=1, source_target_pairs={{0,1},{1,0},{2,3},{3,2},{4,5},{5,4},{6,7},{7,6},{8,9},{9,8},{10,11... | collective-permute-start | bytes 147464 | tf_op jit(solution)/shard_map/ppermute | solution.py:60
  110.9 8.2 %collective-permute-start.8 = (f32[2,24,128]{2,1,0:T(8,128)S(1)}, f32[2,24,128]{2,1,0:T(8,128)S(1)}, u32[]{:S(2)}, u32[]{:S(2)}) collective-permute-start(f32[2,24,128]{2,1,0:T(8,128)S(1)} %select_bitcast_fusion.1), channel_id=1, source_target_pairs={{0,2},{1,3},{2,0},{3,1},{4,6},{5,7},{6,4},{7,5},{8,10},{9,11},{10,... | collective-permute-start | bytes 73736 | tf_op jit(solution)/shard_map/ppermute | solution.py:60
  119.1 8.7 %collective-permute-start.9 = (f32[24,128]{1,0:T(8,128)S(1)}, f32[24,128]{1,0:T(8,128)S(1)}, u32[]{:S(2)}, u32[]{:S(2)}) collective-permute-start(f32[24,128]{1,0:T(8,128)S(1)} %select_bitcast_fusion.2), channel_id=1, source_target_pairs={{0,4},{1,5},{2,6},{3,7},{4,0},{5,1},{6,2},{7,3},{8,12},{9,13},{10,... | collective-permute-start | bytes 36872 | tf_op jit(solution)/shard_map/ppermute | solution.py:60
  127.8 4.4 %collective-permute-start.10 = (f32[24,128]{1,0:T(8,128)S(1)}, f32[24,128]{1,0:T(8,128)S(1)}, u32[]{:S(2)}, u32[]{:S(2)}) collective-permute-start(f32[24,128]{1,0:T(8,128)S(1)} %bitcast_add_fusion.1), channel_id=1, source_target_pairs={{0,256},{256,0},{512,768},{768,512},{1,257},{257,1},{513,769},{769... | collective-permute-start | bytes 36872 | tf_op jit(solution)/shard_map/ppermute | solution.py:72
  132.3 18.5 %collective-permute-start.11 = (f32[24,128]{1,0:T(8,128)S(1)}, f32[24,128]{1,0:T(8,128)S(1)}, u32[]{:S(2)}, u32[]{:S(2)}) collective-permute-start(f32[24,128]{1,0:T(8,128)S(1)} %add.100), channel_id=1, source_target_pairs={{0,512},{256,768},{512,0},{768,256},{1,513},{257,769},{513,1},{769... | collective-permute-start | bytes 36872 | tf_op jit(solution)/shard_map/ppermute | solution.py:72
  136.7 74.6 %collective-permute-start.18 = (bf16[24,256]{1,0:T(8,128)(2,1)}, bf16[24,256]{1,0:T(8,128)(2,1)S(1)}, u32[]{:S(2)}, u32[]{:S(2)}) collective-permute-start(bf16[24,256]{1,0:T(8,128)(2,1)} %get-tuple-element.19), channel_id=1, source_target_pairs={{0,1},{1,2},{2,3},{3,4},{4,5},{5,6},{6,7},{7,8},{8,9},{9,10},{10,1... | collective-permute-start | bytes 36872 | tf_op jit(solution)/shard_map/ppermute | solution.py:324
  138.7 72.7 %collective-permute-start.19 = (bf16[24,256]{1,0:T(8,128)(2,1)S(1)}, bf16[24,256]{1,0:T(8,128)(2,1)S(1)}, u32[]{:S(2)}, u32[]{:S(2)}) collective-permute-start(bf16[24,256]{1,0:T(8,128)(2,1)S(1)} %get-tuple-element.20), channel_id=1, source_target_pairs={{0,31},{1,0},{2,1},{3,2},{4,3},{5,4},{6,5},{7,6},{8,7},{9,8},{10,9... | collective-permute-start | bytes 36872 | tf_op jit(solution)/shard_map/ppermute | solution.py:325
  150.8 50.9 %collective-permute-start.13 = (f32[24,128]{1,0:T(8,128)S(1)}, f32[24,128]{1,0:T(8,128)S(1)}, u32[]{:S(2)}, u32[]{:S(2)}) collective-permute-start(f32[24,128]{1,0:T(8,128)S(1)} %add.101), channel_id=1, source_target_pairs={{0,64},{64,128},{128,192},{192,0},{1,65},{65,129},{129,193},{193,1... | collective-permute-start | bytes 36872 | tf_op jit(solution)/shard_map/ppermute | solution.py:65
  162.9 38.8 %collective-permute-start.14 = (f32[24,128]{1,0:T(8,128)S(1)}, f32[24,128]{1,0:T(8,128)S(1)}, u32[]{:S(2)}, u32[]{:S(2)}) collective-permute-start(f32[24,128]{1,0:T(8,128)S(1)} %add.101), channel_id=1, source_target_pairs={{0,192},{64,0},{128,64},{192,128},{1,193},{65,1},{129,65},{193,129... | collective-permute-start | bytes 36872 | tf_op jit(solution)/shard_map/ppermute | solution.py:65
  165.7 36.0 %collective-permute-start.12 = (f32[24,128]{1,0:T(8,128)S(1)}, f32[24,128]{1,0:T(8,128)S(1)}, u32[]{:S(2)}, u32[]{:S(2)}) collective-permute-start(f32[24,128]{1,0:T(8,128)S(1)} %add.101), channel_id=1, source_target_pairs={{0,128},{64,192},{128,0},{192,64},{1,129},{65,193},{129,1},{193,65... | collective-permute-start | bytes 36872 | tf_op jit(solution)/shard_map/ppermute | solution.py:65
  192.9 13.8 %all-to-all-start.2 = ((f32[8,8,384]{2,1,0:T(8,128)}), f32[8,8,384]{2,1,0:T(8,128)S(1)}, u32[]{:S(2)}, u32[]{:S(2)}) async-start(f32[8,8,384]{2,1,0:T(8,128)} %broadcast_in_dim.131), calls=%async_computation.2 | async-start | bytes 196608 | tf_op jit(solution)/shard_map/all_to_all | solution.py:34
  207.4 4.4 %copy-start.16 = (pred[22]{0:T(512)(128)(4,1)S(1)}, pred[22]{0:T(512)(128)(4,1)}, u32[]{:S(2)}) copy-start(pred[22]{0:T(512)(128)(4,1)} %copy-done.15) | copy-start | bytes 70
  207.4 4.4 %copy-start.18 = (pred[22]{0:T(512)(128)(4,1)S(1)}, pred[22]{0:T(512)(128)(4,1)}, u32[]{:S(2)}) copy-start(pred[22]{0:T(512)(128)(4,1)} %copy-done.17) | copy-start | bytes 70
  207.4 4.4 %copy-start.20 = (pred[22]{0:T(512)(128)(4,1)S(1)}, pred[22]{0:T(512)(128)(4,1)}, u32[]{:S(2)}) copy-start(pred[22]{0:T(512)(128)(4,1)} %copy-done.19) | copy-start | bytes 70
  207.4 4.4 %copy-start.29 = (f32[22]{0:T(128)S(1)}, f32[22]{0:T(128)}, u32[]{:S(2)}) copy-start(f32[22]{0:T(128)} %copy-done.28) | copy-start | bytes 268
  207.4 45.5 %all-to-all-start.3 = ((bf16[32,24,128]{2,1,0:T(8,128)(2,1)}), bf16[32,24,128]{2,1,0:T(8,128)(2,1)S(1)}, u32[]{:S(2)}, u32[]{:S(2)}) async-start(bf16[32,24,128]{2,1,0:T(8,128)(2,1)} %broadcast_in_dim.132), calls=%async_computation.3 | async-start | bytes 393216 | tf_op jit(solution)/shard_map/all_to_all | solution.py:34
  211.8 0.6 copy-start.12
  211.8 0.6 copy-start.14
  211.9 0.7 copy-start.22
  213.9 18.8 %copy-start.6 = (bf16[3,256,256]{2,1,0:T(8,128)(2,1)S(1)}, bf16[3,256,256]{2,1,0:T(8,128)(2,1)}, u32[]{:S(2)}) copy-start(bf16[3,256,256]{2,1,0:T(8,128)(2,1)} %param.18) | copy-start | bytes 1179652
  215.2 18.0 %collective-permute-start.16 = (f32[8,384]{1,0:T(8,128)S(1)}, f32[8,384]{1,0:T(8,128)S(1)}, u32[]{:S(2)}, u32[]{:S(2)}) collective-permute-start(f32[8,384]{1,0:T(8,128)S(1)} %reduce_sum.19), channel_id=1, source_target_pairs={{0,64},{64,128},{128,192},{192,0},{1,65},{65,129},{129,193},{193,1... | collective-permute-start | bytes 36872 | tf_op jit(solution)/shard_map/ppermute | solution.py:65
  217.3 16.0 %collective-permute-start.17 = (f32[8,384]{1,0:T(8,128)S(1)}, f32[8,384]{1,0:T(8,128)S(1)}, u32[]{:S(2)}, u32[]{:S(2)}) collective-permute-start(f32[8,384]{1,0:T(8,128)S(1)} %reduce_sum.19), channel_id=1, source_target_pairs={{0,192},{64,0},{128,64},{192,128},{1,193},{65,1},{129,65},{193,129... | collective-permute-start | bytes 36872 | tf_op jit(solution)/shard_map/ppermute | solution.py:65
  229.2 23.1 %collective-permute-start.15 = (f32[8,384]{1,0:T(8,128)S(1)}, f32[8,384]{1,0:T(8,128)S(1)}, u32[]{:S(2)}, u32[]{:S(2)}) collective-permute-start(f32[8,384]{1,0:T(8,128)S(1)} %reduce_sum.19), channel_id=1, source_target_pairs={{0,128},{64,192},{128,0},{192,64},{1,129},{65,193},{129,1},{193,65... | collective-permute-start | bytes 36872 | tf_op jit(solution)/shard_map/ppermute | solution.py:65
  252.9 6.0 %collective-permute-start.20 = (bf16[768,128]{1,0:T(8,128)(2,1)S(1)}, bf16[768,128]{1,0:T(8,128)(2,1)S(1)}, u32[]{:S(2)}, u32[]{:S(2)}) collective-permute-start(bf16[768,128]{1,0:T(8,128)(2,1)S(1)} %bitcast.152), channel_id=1, source_target_pairs={{0,32},{32,0},{1,33},{33,1},{2,34},{34,2},{3,35},{35,3},{4,36},{36... | collective-permute-start | bytes 589832 | tf_op jit(solution)/shard_map/ppermute | solution.py:342

commit v3 on v2

--- a/solution.py
+++ b/solution.py
@@ -20,9 +20,9 @@
     return -(-value // step) * step
 
 
-PARTS = (("x", 4), ("z_hi", 4), ("core", 2))
-LAT = tuple(name for name, _ in PARTS)
-LON_BITS = (8, 16, 1, 2, 4)
+PARTS = (("x", 4), ("z_hi", 4), ("core", 2), ("y", 4), ("z_lo", 8))
+LAT = ("x", "z_hi", "core")
+LON = ("y", "z_lo")
 
 
 def ring(size, step):
@@ -32,12 +32,6 @@
 def to_all(value, axes):
     count = lax.axis_size(axes)
     return lax.all_to_all(jnp.broadcast_to(value, (count, *value.shape)), axes, 0, 0)
-
-
-def sum_over(value, stages):
-    for axes in stages:
-        value = jnp.sum(to_all(value, axes), axis=0)
-    return value
 
 
 def pairs(size, bit):
@@ -48,29 +42,14 @@
     size, place = lax.axis_size(axis), lax.axis_index(axis)
     left = sorted(bits, reverse=True)
     value = value.reshape(*(2 for _ in left), -1, value.shape[-1])
-    for step, bit in enumerate(bits):
+    for bit in bits:
         where = left.index(bit)
         left.remove(bit)
         low = lax.index_in_dim(value, 0, where, keepdims=False)
         high = lax.index_in_dim(value, 1, where, keepdims=False)
         upper = (place & bit) != 0
         value, sent = jnp.where(upper, high, low), jnp.where(upper, low, high)
-        if step < 2:
-            sent = sent.astype(BF16)
-        value = value + lax.ppermute(sent, axis, pairs(size, bit)).astype(F32)
-    return value
-
-
-def sum_ring(value, axis):
-    far, near, back = (lax.ppermute(value, axis, ring(4, step)) for step in (2, 1, 3))
-    return (value + far) + (near + back)
-
-
-def sum_doubling(value, axis):
-    size, bit = lax.axis_size(axis), 1
-    while bit < size:
-        value = value + lax.ppermute(value, axis, pairs(size, bit))
-        bit *= 2
+        value = value + lax.ppermute(sent.astype(BF16), axis, pairs(size, bit)).astype(F32)
     return value
 
 
@@ -292,7 +271,7 @@
     grad_out, block_input, leg_table, spec_coeff, spec_filter, cycle_weight, cycle_shift, tap_weight
 ):
     rows_here, lons_here, channels = grad_out.shape
-    lat, lon = lax.axis_size(LAT), lax.axis_size("lon")
+    lat, lon = lax.axis_size(LAT), lax.axis_size(LON)
     chans = channels // lon
     orders_here, degrees, _ = leg_table.shape
     orders = orders_here * lat
@@ -300,12 +279,18 @@
     swap = ring(2, 1)
 
     sent = channels_first(grad_out).reshape(lon, chans, -1)
-    rows = lax.all_to_all(sent, "lon", 0, 0)
-
-    above = lax.ppermute(grad_out[-1], LAT, ring(lat, 1))
-    below = lax.ppermute(grad_out[0], LAT, ring(lat, -1))
-    before = lax.ppermute(block_input[:, -1], "lon", ring(lon, 1))
-    after = lax.ppermute(block_input[:, 0], "lon", ring(lon, -1))
+    rows = lax.all_to_all(sent, LON, 0, 0)
+
+    halos = (
+        lax.ppermute(grad_out[-1], LAT, ring(lat, 1)),
+        lax.ppermute(grad_out[0], LAT, ring(lat, -1)),
+        lax.ppermute(block_input[:, -1], LON, ring(lon, 1)),
+        lax.ppermute(block_input[:, 0], LON, ring(lon, -1)),
+    )
+    blocks = fourier_chunks(rows, rows_here, lons_here, orders, lat)
+    blocks, (above, below, before, after) = lax.optimization_barrier((blocks, halos))
+    columns = lax.all_to_all(blocks, LAT, 0, 0)
+
     grad_rows = jnp.concatenate([above[None], grad_out, below[None]], axis=0)
     taps = tap_rows(cycle_weight, cycle_shift, rows_here)
     part = taps_part(grad_rows, block_input, before, after, taps)
@@ -313,32 +298,38 @@
 
     left, right = part[:, : channels // 2], part[:, channels // 2 :]
     mine, other = jnp.where(core == 0, left, right), jnp.where(core == 0, right, left)
-    high, width = mine.shape[0] // lon, mine.shape[1]
-    rows, other = lax.optimization_barrier((rows, other))
     mine = mine + lax.ppermute(other, "core", swap)
-
-    blocks = fourier_chunks(rows, rows_here, lons_here, orders, lat)
-    blocks, edges = lax.optimization_barrier((blocks, (grad_rows[:, -1], grad_rows[:, 0])))
-    columns = lax.all_to_all(blocks, LAT, 0, 0)
-
-    before = lax.ppermute(edges[0], "lon", ring(lon, 1))
-    after = lax.ppermute(edges[1], "lon", ring(lon, -1))
-    input_grad = input_part(grad_rows, before, after, taps, tap_weight)
-
-    chunk = scatter_rows(mine, "lon", LON_BITS)
-    chunk = sum_ring(sum_doubling(chunk, "x"), "z_hi").astype(BF16)
+    mine = scatter_rows(mine, "y", (1, 2)).astype(BF16)
+    columns, mine = lax.optimization_barrier((columns, mine))
+    ring_size = lax.axis_size("z_lo")
+    chunk = lax.all_to_all(mine.reshape(ring_size, -1, mine.shape[1]), "z_lo", 0, 0)
+    chunk = jnp.sum(chunk.astype(F32), axis=0)
+    high, width = chunk.shape
+
     fourier = unfold(columns, rows_here, orders_here, chans)
     degree = jnp.einsum("mla,mxa->mxl", leg_table, fourier, preferred_element_type=F32)
     degree = degree.reshape(orders_here, 2, chans, degrees)
     spec_grad = (degree * spec_filter.T).astype(BF16).transpose(3, 0, 1, 2)
     coeff = spec_coeff.transpose(1, 2, 3, 0).astype(F32)
     filter_part = jnp.sum(coeff * degree, axis=(0, 1)) / math.sqrt(2 * orders)
-    filter_part = sum_over(filter_part, (("x", "core"),))
-    filter_part, chunk = lax.optimization_barrier((filter_part, chunk))
-    filter_grad = sum_ring(filter_part, "z_hi").T
-
-    mine = to_all(chunk, "lon").reshape(lon * high, width)
-    mine, filter_grad = lax.optimization_barrier((mine, filter_grad))
+
+    pieces = degrees // width
+    both = [chunk] + [filter_part[:, i * width : (i + 1) * width] for i in range(pieces)]
+    both = to_all(jnp.concatenate(both, axis=0), ("x", "core"))
+    cores = jnp.sum(both.reshape(-1, 2, *both.shape[1:]), axis=0)
+    chunk = jnp.where(core == 0, cores[0, :high], cores[1, :high])
+    both = jnp.concatenate([chunk, cores[0, high:] + cores[1, high:]], axis=0)
+    both, edges = lax.optimization_barrier((both, (grad_rows[:, -1], grad_rows[:, 0])))
+    both = jnp.sum(to_all(both, "z_hi"), axis=0)
+    filter_grad = both[high:].reshape(pieces, chans, width).transpose(0, 2, 1)
+    filter_grad = filter_grad.reshape(degrees, chans)
+
+    before = lax.ppermute(edges[0], LON, ring(lon, 1))
+    after = lax.ppermute(edges[1], LON, ring(lon, -1))
+    input_grad = input_part(grad_rows, before, after, taps, tap_weight)
+
+    mine = to_all(both[:high].astype(BF16), "z_lo").reshape(-1, width)
+    mine = to_all(mine, "y").reshape(-1, width)
     other = lax.ppermute(mine, "core", swap)
     left, right = jnp.where(core == 0, mine, other), jnp.where(core == 0, other, mine)
     taps_grad = jnp.concatenate([left, right], axis=1).astype(F32)
@@ -348,18 +339,19 @@
 
 def solution(mesh):
     sizes = tuple(size for _, size in PARTS)
-    split = jax.sharding.Mesh(mesh.devices.reshape(*sizes, mesh.shape["lon"]), (*LAT, "lon"))
+    names, sizes = zip(*PARTS)
+    split = jax.sharding.Mesh(mesh.devices.reshape(sizes), names)
     in_specs = (
-        P(LAT, "lon", None),
-        P(LAT, "lon", None),
+        P(LAT, LON, None),
+        P(LAT, LON, None),
         P(LAT, None, None),
-        P(None, LAT, None, "lon"),
-        P(None, "lon"),
+        P(None, LAT, None, LON),
+        P(None, LON),
         P(),
         P(),
         P(),
     )
-    out_specs = (P(None, LAT, None, "lon"), P(None, "lon"), P(LAT, "lon", None), P())
+    out_specs = (P(None, LAT, None, LON), P(None, LON), P(LAT, LON, None), P())
     return jax.shard_map(
         on_device, mesh=split, in_specs=in_specs, out_specs=out_specs, check_vma=False
     )

time: 261 us -> 227 us (0.87)
  starting transfers between devices: 170 us -> 132 us
  waiting for transfers between devices: 64.6 us -> 68.2 us
    ppermute x19 -> x8, starting transfers between devices: 121 us -> 50.7 us  [the longest x1 16.3 us: on_device(): lax.ppermute(grad_out[-1], LAT, ring(lat, 1))]
    ppermute x19 -> x8, waiting for transfers between devices: 59.6 us -> 8.27 us  [the longest x2 8.26 us: scatter_rows(): lax.ppermute(sent.astype(BF16), axis, pairs(size, bit)).astype(F32)]
    all_to_all x2 -> x4, waiting for transfers between devices: 4.97 us -> 35.6 us  [to_all(): lax.all_to_all(jnp.broadcast_to(value, (count, *value.shape)), axes, 0, 0)]
    all_to_all x1, waiting for transfers between devices: 0.01 us -> 17.4 us  [on_device(): columns = lax.all_to_all(blocks, LAT, 0, 0)]
    all_to_all x1 -> x2, starting transfers between devices: 16.1 us -> 31.8 us  [the longest x1 16.1 us: on_device(): rows = lax.all_to_all(sent, LON, 0, 0)]
    all_to_all x1, starting transfers between devices: 14.3 us -> 25.4 us  [on_device(): columns = lax.all_to_all(blocks, LAT, 0, 0)]
    all_to_all x1 -> x2, waiting for transfers between devices: 0.01 us -> 5.06 us  [the longest x1 5.05 us: on_device(): lax.all_to_all(mine.reshape(ring_size, -1, mine.shape[1]), 'z_lo', 0, 0)]
    all_to_all x2 -> x4, starting transfers between devices: 12.7 us -> 15.2 us  [to_all(): lax.all_to_all(jnp.broadcast_to(value, (count, *value.shape)), axes, 0, 0)]
  transfers between devices with their start and end apart: 25 -> 17, of which waited for: 10 -> 10; matrix products, arithmetic and copies ran while one was open for 7% -> 7% of each run, Pallas kernels for 1% -> 1%
where the time goes in v3:
time: 227 us; the launch traced here: 226 us
  starting transfers between devices  132 us (58%)
  waiting for transfers between devices  68.2 us (30%)
  matrix products  10.5 us (5%)
  local copies, waits for them, and re-layouts  7.09 us (3%)
  Pallas kernels  3.98 us (2%)
  other arithmetic  3.42 us (2%)
    all_to_all x4, waiting for transfers between devices, to_all(): lax.all_to_all(jnp.broadcast_to(value, (count, *value.shape)), axes, 0, 0)  35.6 us
    all_to_all x1, starting transfers between devices, on_device(): columns = lax.all_to_all(blocks, LAT, 0, 0)  25.4 us
    all_to_all x1, waiting for transfers between devices, on_device(): columns = lax.all_to_all(blocks, LAT, 0, 0)  17.4 us
    ppermute x1, starting transfers between devices, on_device(): lax.ppermute(grad_out[-1], LAT, ring(lat, 1))  16.3 us
    all_to_all x1, starting transfers between devices, on_device(): rows = lax.all_to_all(sent, LON, 0, 0)  16.1 us
    all_to_all x1, starting transfers between devices, on_device(): lax.all_to_all(mine.reshape(ring_size, -1, mine.shape[1]), 'z_lo', 0, 0)  15.7 us
    all_to_all x4, starting transfers between devices, to_all(): lax.all_to_all(jnp.broadcast_to(value, (count, *value.shape)), axes, 0, 0)  15.2 us
    ppermute x1, starting transfers between devices, on_device(): after = lax.ppermute(edges[1], LON, ring(lon, -1))  11.9 us
  transfers between devices with their start and end apart: 17, of which 10 were waited for; matrix products, arithmetic and copies ran while one was open for 7% of the time, Pallas kernels for 1%

profile of v3, /device:TPU:1, one launch (start us, length us, event | category | flops | bytes accessed | tf_op | source)
XLA Modules:
  0.0 226.3 jit_solution(6372288561841668720)
XLA Ops:
  0.6 1.0 copy-done
  1.7 0.0 copy-start.3
  1.7 0.0 copy-start.4
  1.7 1.0 channels_first.1
  2.7 16.1 %all-to-all-start = ((bf16[32,8,1152]{2,1,0:T(8,128)(2,1)}), bf16[32,8,1152]{2,1,0:T(8,128)(2,1)S(1)}, u32[]{:S(2)}, u32[]{:S(2)}) async-start(bf16[32,8,1152]{2,1,0:T(8,128)(2,1)} %bitcast), calls=%async_computation | async-start | bytes 1179648 | tf_op jit(solution)/shard_map/all_to_all | solution.py:282
  18.9 16.3 %collective-permute-start = (bf16[45,256]{1,0:T(8,128)(2,1)S(1)}, bf16[45,256]{1,0:T(8,128)(2,1)S(1)}, u32[]{:S(2)}, u32[]{:S(2)}) collective-permute-start(bf16[45,256]{1,0:T(8,128)(2,1)S(1)} %get-tuple-element.33), channel_id=1, source_target_pairs={{0,32},{32,64},{64,96},{96,128},{128,160},{160,192},{192,224},{224... | collective-permute-start | bytes 69128 | tf_op jit(solution)/shard_map/ppermute | solution.py:285
  35.2 1.9 collective-permute-start.1
  37.1 1.0 fusion.53
  38.1 3.4 %collective-permute-start.2 = (bf16[22,256]{1,0:T(8,128)(2,1)S(1)}, bf16[22,256]{1,0:T(8,128)(2,1)S(1)}, u32[]{:S(2)}, u32[]{:S(2)}) collective-permute-start(bf16[22,256]{1,0:T(8,128)(2,1)S(1)} %bitcast.141), channel_id=1, source_target_pairs={{0,1},{1,2},{2,3},{3,4},{4,5},{5,6},{6,7},{7,8},{8,9},{9,10},{10,1... | collective-permute-start | bytes 33800 | tf_op jit(solution)/shard_map/ppermute | solution.py:287
  41.5 10.7 %collective-permute-start.3 = (bf16[22,256]{1,0:T(8,128)(2,1)S(1)}, bf16[22,256]{1,0:T(8,128)(2,1)S(1)}, u32[]{:S(2)}, u32[]{:S(2)}) collective-permute-start(bf16[22,256]{1,0:T(8,128)(2,1)S(1)} %bitcast.142), channel_id=1, source_target_pairs={{0,31},{1,0},{2,1},{3,2},{4,3},{5,4},{6,5},{7,6},{8,7},{9,8},{10,9... | collective-permute-start | bytes 33800 | tf_op jit(solution)/shard_map/ppermute | solution.py:288
  52.3 0.1 pad_dynamic-slice_fusion.2
  52.4 0.1 pad_dynamic-slice_fusion.5
  52.5 0.0 all-to-all-done
  52.6 0.0 copy-start.9
  52.6 2.7 %fourier_chunks.1 = bf16[32,40,128]{2,1,0:T(8,128)(2,1)} custom-call(bf16[256,1152]{1,0:T(8,128)(2,1)S(1)} %bitcast.122, bf16[512,256]{1,0:T(8,128)(2,1)S(1)} %copy-done.4, f32[2,256,384]{2,1,0:T(8,128)S(1)} %copy-done.2, bf16[192,768]{1,0:T(8,128)(2,1)S(1)} %copy-done.3), custom_call_target="tpu_custom_call" | custom-call | flops 528482304 | bytes 1703936 | tf_op jit(solution)/shard_map/fourier_chunks/pallas_call | solution.py:152
  55.3 25.4 %all-to-all-start.1 = ((bf16[32,40,128]{2,1,0:T(8,128)(2,1)}), bf16[32,40,128]{2,1,0:T(8,128)(2,1)S(1)}, u32[]{:S(2)}, u32[]{:S(2)}) async-start(bf16[32,40,128]{2,1,0:T(8,128)(2,1)} %fourier_chunks.1), calls=%async_computation.1 | async-start | bytes 655360 | tf_op jit(solution)/shard_map/all_to_all | solution.py:292
  80.8 0.7 convolution_bitcast_fusion.1
  81.6 0.7 convolution_bitcast_fusion.3
  82.3 0.7 convolution_bitcast_fusion.2
  83.1 0.1 maximum_multiply_fusion
  83.2 2.1 collective-permute-start.4
  85.4 1.5 collective-permute-done.4
  86.8 0.1 select_add_fusion
  86.9 1.9 collective-permute-start.5
  88.9 0.0 copy-start.5
  88.9 0.0 copy-start.6
  88.9 4.1 %collective-permute-done.5 = bf16[2,192,128]{2,1,0:T(8,128)(2,1)S(1)} collective-permute-done((bf16[2,192,128]{2,1,0:T(8,128)(2,1)S(1)}, bf16[2,192,128]{2,1,0:T(8,128)(2,1)S(1)}, u32[]{:S(2)}, u32[]{:S(2)}) %collective-permute-start.5) | collective-permute-done | bytes 98336 | tf_op jit(solution)/shard_map/ppermute | solution.py:52
  93.0 2.4 %collective-permute-start.6 = (bf16[192,128]{1,0:T(8,128)(2,1)S(1)}, bf16[192,128]{1,0:T(8,128)(2,1)S(1)}, u32[]{:S(2)}, u32[]{:S(2)}) collective-permute-start(bf16[192,128]{1,0:T(8,128)(2,1)S(1)} %fusion.44), channel_id=1, source_target_pairs={{0,16},{8,24},{16,0},{24,8},{1,17},{9,25},{17,1},{25,9},{2,18},{10... | collective-permute-start | bytes 147464 | tf_op jit(solution)/shard_map/ppermute | solution.py:52
  95.4 0.1 pad_maximum_fusion.13
  95.5 4.2 %collective-permute-done.6 = bf16[192,128]{1,0:T(8,128)(2,1)S(1)} collective-permute-done((bf16[192,128]{1,0:T(8,128)(2,1)S(1)}, bf16[192,128]{1,0:T(8,128)(2,1)S(1)}, u32[]{:S(2)}, u32[]{:S(2)}) %collective-permute-start.6) | collective-permute-done | bytes 49184 | tf_op jit(solution)/shard_map/ppermute | solution.py:52
  99.7 0.6 fusion.43
  100.3 17.4 %all-to-all-done.1.q_ref = bf16[32,40,128]{2,1,0:T(8,128)(2,1)S(1)} async-done(((bf16[32,40,128]{2,1,0:T(8,128)(2,1)}), bf16[32,40,128]{2,1,0:T(8,128)(2,1)S(1)}, u32[]{:S(2)}, u32[]{:S(2)}) %all-to-all-start.1) | async-done | bytes 327712 | tf_op jit(solution)/shard_map/all_to_all | solution.py:292
  117.7 0.2 unfold.1
  117.9 15.7 %all-to-all-start.2 = ((bf16[8,24,128]{2,1,0:T(8,128)(2,1)}), bf16[8,24,128]{2,1,0:T(8,128)(2,1)S(1)}, u32[]{:S(2)}, u32[]{:S(2)}) async-start(bf16[8,24,128]{2,1,0:T(8,128)(2,1)} %bitcast.36), calls=%async_computation.2 | async-start | bytes 98304 | tf_op jit(solution)/shard_map/all_to_all | solution.py:305
  133.6 4.5 %fusion.28 = (f32[8,384]{1,0:T(8,128)S(1)}, bf16[384,12,2,8]{0,3,2,1:T(8,128)(2,1)}) fusion(bf16[384,12,2,8]{0,3,2,1:T(8,128)(2,1)S(1)} %copy-done.5, f32[8,384]{1,0:T(8,128)S(1)} %bitcast.138, bf16[12,16,704]{2,1,0:T(8,128)(2,1)S(1)} %unfold.1, bf16[12,384,704]{1,2,0:T(8,128)(2,1)} %param.13), kind=kOutput, calls=%fused_computation.54 | convolution fusion | flops 104174592 | bytes 7077888 | tf_op jit(solution)/shard_map/mla,mxa->mxl/dot_general | solution.py:310
  138.2 5.1 %all-to-all-done.2 = bf16[8,24,128]{2,1,0:T(8,128)(2,1)S(1)} async-done(((bf16[8,24,128]{2,1,0:T(8,128)(2,1)}), bf16[8,24,128]{2,1,0:T(8,128)(2,1)S(1)}, u32[]{:S(2)}, u32[]{:S(2)}) %all-to-all-start.2) | async-done | bytes 49184 | tf_op jit(solution)/shard_map/all_to_all | solution.py:305
  143.3 0.7 broadcast_in_dim.137
  144.0 5.2 %all-to-all-start.3 = ((f32[8,48,128]{2,1,0:T(8,128)}), f32[8,48,128]{2,1,0:T(8,128)S(1)}, u32[]{:S(2)}, u32[]{:S(2)}) async-start(f32[8,48,128]{2,1,0:T(8,128)} %broadcast_in_dim.137), calls=%async_computation.3 | async-start | bytes 393216 | tf_op jit(solution)/shard_map/all_to_all | solution.py:34
  149.2 5.9 %all-to-all-done.3 = f32[8,48,128]{2,1,0:T(8,128)S(1)} async-done(((f32[8,48,128]{2,1,0:T(8,128)}), f32[8,48,128]{2,1,0:T(8,128)S(1)}, u32[]{:S(2)}, u32[]{:S(2)}) %all-to-all-start.3) | async-done | bytes 196640 | tf_op jit(solution)/shard_map/all_to_all | solution.py:34
  155.1 2.1 collective-permute-start.7
  157.2 11.9 %collective-permute-start.8 = (bf16[24,256]{1,0:T(8,128)(2,1)S(1)}, bf16[24,256]{1,0:T(8,128)(2,1)S(1)}, u32[]{:S(2)}, u32[]{:S(2)}) collective-permute-start(bf16[24,256]{1,0:T(8,128)(2,1)S(1)} %get-tuple-element.23), channel_id=1, source_target_pairs={{0,31},{1,0},{2,1},{3,2},{4,3},{5,4},{6,5},{7,6},{8,7},{9,8},{10,9... | collective-permute-start | bytes 36872 | tf_op jit(solution)/shard_map/ppermute | solution.py:328
  169.1 0.6 broadcast_in_dim.138
  169.8 3.3 %all-to-all-start.4 = ((f32[4,48,128]{2,1,0:T(8,128)}), f32[4,48,128]{2,1,0:T(8,128)S(1)}, u32[]{:S(2)}, u32[]{:S(2)}) async-start(f32[4,48,128]{2,1,0:T(8,128)} %broadcast_in_dim.138), calls=%async_computation.4 | async-start | bytes 196608 | tf_op jit(solution)/shard_map/all_to_all | solution.py:34
  173.2 0.4 maximum_maximum_fusion
  173.6 0.4 multiply_convert_fusion.2
  174.0 0.2 reshape.146
  174.1 0.7 multiply_convert_fusion
  174.8 20.0 %all-to-all-done.4 = f32[4,48,128]{2,1,0:T(8,128)S(1)} async-done(((f32[4,48,128]{2,1,0:T(8,128)}), f32[4,48,128]{2,1,0:T(8,128)S(1)}, u32[]{:S(2)}, u32[]{:S(2)}) %all-to-all-start.4) | async-done | bytes 98336 | tf_op jit(solution)/shard_map/all_to_all | solution.py:34
  194.8 0.6 broadcast_in_dim.141
  195.4 3.3 %all-to-all-start.5 = ((bf16[8,24,128]{2,1,0:T(8,128)(2,1)}), bf16[8,24,128]{2,1,0:T(8,128)(2,1)S(1)}, u32[]{:S(2)}, u32[]{:S(2)}) async-start(bf16[8,24,128]{2,1,0:T(8,128)(2,1)} %broadcast_in_dim.141), calls=%async_computation.5 | async-start | bytes 98304 | tf_op jit(solution)/shard_map/all_to_all | solution.py:34
  198.8 1.2 fusion.37
  200.0 0.2 reshape.147
  200.2 0.2 reshape.148
  200.4 1.2 convolution_add_fusion.1
  201.6 6.8 %all-to-all-done.5 = bf16[8,24,128]{2,1,0:T(8,128)(2,1)S(1)} async-done(((bf16[8,24,128]{2,1,0:T(8,128)(2,1)}), bf16[8,24,128]{2,1,0:T(8,128)(2,1)S(1)}, u32[]{:S(2)}, u32[]{:S(2)}) %all-to-all-start.5) | async-done | bytes 49184 | tf_op jit(solution)/shard_map/all_to_all | solution.py:34
  208.4 0.7 broadcast_in_dim.142
  209.1 3.4 %all-to-all-start.6 = ((bf16[4,192,128]{2,1,0:T(8,128)(2,1)}), bf16[4,192,128]{2,1,0:T(8,128)(2,1)S(1)}, u32[]{:S(2)}, u32[]{:S(2)}) async-start(bf16[4,192,128]{2,1,0:T(8,128)(2,1)} %broadcast_in_dim.142), calls=%async_computation.6 | async-start | bytes 393216 | tf_op jit(solution)/shard_map/all_to_all | solution.py:34
  212.5 1.2 fusion
  213.7 1.0 convert_element_type.106
  214.7 2.9 %all-to-all-done.6 = bf16[4,192,128]{2,1,0:T(8,128)(2,1)S(1)} async-done(((bf16[4,192,128]{2,1,0:T(8,128)(2,1)}), bf16[4,192,128]{2,1,0:T(8,128)(2,1)S(1)}, u32[]{:S(2)}, u32[]{:S(2)}) %all-to-all-start.6) | async-done | bytes 196640 | tf_op jit(solution)/shard_map/all_to_all | solution.py:34
  217.6 6.6 %collective-permute-start.9 = (bf16[768,128]{1,0:T(8,128)(2,1)S(1)}, bf16[768,128]{1,0:T(8,128)(2,1)S(1)}, u32[]{:S(2)}, u32[]{:S(2)}) collective-permute-start(bf16[768,128]{1,0:T(8,128)(2,1)S(1)} %bitcast.127), channel_id=1, source_target_pairs={{0,32},{32,0},{1,33},{33,1},{2,34},{34,2},{3,35},{35,3},{4,36},{36... | collective-permute-start | bytes 589832 | tf_op jit(solution)/shard_map/ppermute | solution.py:333
  224.2 0.6 slice_bitcast_fusion.2
  224.8 0.4 collective-permute-done.9
  225.3 0.9 maximum_convert_fusion
  (46 shorter events, 0.4 us)
Async XLA Ops:
  0.6 1.0 copy-start
  1.7 17.2 %copy-start.1 = (bf16[22,45,256]{2,1,0:T(8,128)(2,1)S(1)}, bf16[22,45,256]{2,1,0:T(8,128)(2,1)}, u32[]{:S(2)}) copy-start(bf16[22,45,256]{2,1,0:T(8,128)(2,1)} %x_ref.1) | copy-start | bytes 1520644
  1.7 50.6 %copy-start.7 = (f32[704,3]{0,1:T(4,128)S(1)}, f32[704,3]{0,1:T(4,128)}, u32[]{:S(2)}) copy-start(f32[704,3]{0,1:T(4,128)} %param.16) | copy-start | bytes 25348
  1.7 50.7 %copy-start.8 = (s32[704,3]{0,1:T(4,128)S(1)}, s32[704,3]{0,1:T(4,128)}, u32[]{:S(2)}) copy-start(s32[704,3]{0,1:T(4,128)} %param.17) | copy-start | bytes 25348
  1.7 50.8 %copy-start.2 = (f32[2,256,384]{2,1,0:T(8,128)S(1)}, f32[2,256,384]{2,1,0:T(8,128)}, u32[]{:S(2)}) copy-start(f32[2,256,384]{2,1,0:T(8,128)} %constant.62.clone.tw_ref) | copy-start | bytes 2359300
  1.7 50.9 %copy-start.3 = (bf16[192,768]{1,0:T(8,128)(2,1)S(1)}, bf16[192,768]{1,0:T(8,128)(2,1)}, u32[]{:S(2)}) copy-start(bf16[192,768]{1,0:T(8,128)(2,1)} %constant.63.clone.w_ref) | copy-start | bytes 884740
  1.7 50.8 %copy-start.4 = (bf16[512,256]{1,0:T(8,128)(2,1)S(1)}, bf16[512,256]{1,0:T(8,128)(2,1)}, u32[]{:S(2)}) copy-start(bf16[512,256]{1,0:T(8,128)(2,1)} %constant.61.clone.d_ref) | copy-start | bytes 786436
  2.7 49.8 %all-to-all-start = ((bf16[32,8,1152]{2,1,0:T(8,128)(2,1)}), bf16[32,8,1152]{2,1,0:T(8,128)(2,1)S(1)}, u32[]{:S(2)}, u32[]{:S(2)}) async-start(bf16[32,8,1152]{2,1,0:T(8,128)(2,1)} %bitcast), calls=%async_computation | async-start | bytes 1179648 | tf_op jit(solution)/shard_map/all_to_all | solution.py:282
  18.9 36.4 %collective-permute-start = (bf16[45,256]{1,0:T(8,128)(2,1)S(1)}, bf16[45,256]{1,0:T(8,128)(2,1)S(1)}, u32[]{:S(2)}, u32[]{:S(2)}) collective-permute-start(bf16[45,256]{1,0:T(8,128)(2,1)S(1)} %get-tuple-element.33), channel_id=1, source_target_pairs={{0,32},{32,64},{64,96},{96,128},{128,160},{160,192},{192,224},{224... | collective-permute-start | bytes 69128 | tf_op jit(solution)/shard_map/ppermute | solution.py:285
  35.2 20.1 %collective-permute-start.1 = (bf16[45,256]{1,0:T(8,128)(2,1)S(1)}, bf16[45,256]{1,0:T(8,128)(2,1)S(1)}, u32[]{:S(2)}, u32[]{:S(2)}) collective-permute-start(bf16[45,256]{1,0:T(8,128)(2,1)S(1)} %get-tuple-element.32), channel_id=1, source_target_pairs={{0,992},{32,0},{64,32},{96,64},{128,96},{160,128},{192,160},{224,1... | collective-permute-start | bytes 69128 | tf_op jit(solution)/shard_map/ppermute | solution.py:286
  38.1 17.2 %collective-permute-start.2 = (bf16[22,256]{1,0:T(8,128)(2,1)S(1)}, bf16[22,256]{1,0:T(8,128)(2,1)S(1)}, u32[]{:S(2)}, u32[]{:S(2)}) collective-permute-start(bf16[22,256]{1,0:T(8,128)(2,1)S(1)} %bitcast.141), channel_id=1, source_target_pairs={{0,1},{1,2},{2,3},{3,4},{4,5},{5,6},{6,7},{7,8},{8,9},{9,10},{10,1... | collective-permute-start | bytes 33800 | tf_op jit(solution)/shard_map/ppermute | solution.py:287
  41.5 13.8 %collective-permute-start.3 = (bf16[22,256]{1,0:T(8,128)(2,1)S(1)}, bf16[22,256]{1,0:T(8,128)(2,1)S(1)}, u32[]{:S(2)}, u32[]{:S(2)}) collective-permute-start(bf16[22,256]{1,0:T(8,128)(2,1)S(1)} %bitcast.142), channel_id=1, source_target_pairs={{0,31},{1,0},{2,1},{3,2},{4,3},{5,4},{6,5},{7,6},{8,7},{9,8},{10,9... | collective-permute-start | bytes 33800 | tf_op jit(solution)/shard_map/ppermute | solution.py:288
  52.6 28.3 %copy-start.9 = (bf16[22,45,256]{2,1,0:T(8,128)(2,1)S(1)}, bf16[22,45,256]{2,1,0:T(8,128)(2,1)}, u32[]{:S(2)}) copy-start(bf16[22,45,256]{2,1,0:T(8,128)(2,1)} %param.12) | copy-start | bytes 1520644
  55.3 62.4 %all-to-all-start.1 = ((bf16[32,40,128]{2,1,0:T(8,128)(2,1)}), bf16[32,40,128]{2,1,0:T(8,128)(2,1)S(1)}, u32[]{:S(2)}, u32[]{:S(2)}) async-start(bf16[32,40,128]{2,1,0:T(8,128)(2,1)} %fourier_chunks.1), calls=%async_computation.1 | async-start | bytes 655360 | tf_op jit(solution)/shard_map/all_to_all | solution.py:292
  83.2 3.6 %collective-permute-start.4 = (f32[768,128]{1,0:T(8,128)S(1)}, f32[768,128]{1,0:T(8,128)S(1)}, u32[]{:S(2)}, u32[]{:S(2)}) collective-permute-start(f32[768,128]{1,0:T(8,128)S(1)} %slice_select_fusion.3), channel_id=1, source_target_pairs={{0,32},{32,0},{1,33},{33,1},{2,34},{34,2},{3,35},{35,3},{4,36},{36... | collective-permute-start | bytes 1179656 | tf_op jit(solution)/shard_map/ppermute | solution.py:301
  86.9 6.1 %collective-permute-start.5 = (bf16[2,192,128]{2,1,0:T(8,128)(2,1)S(1)}, bf16[2,192,128]{2,1,0:T(8,128)(2,1)S(1)}, u32[]{:S(2)}, u32[]{:S(2)}) collective-permute-start(bf16[2,192,128]{2,1,0:T(8,128)(2,1)S(1)} %fusion.42), channel_id=1, source_target_pairs={{0,8},{8,0},{16,24},{24,16},{1,9},{9,1},{17,25},{25,17},{2,10},{10... | collective-permute-start | bytes 294920 | tf_op jit(solution)/shard_map/ppermute | solution.py:52
  88.9 44.8 %copy-start.5 = (bf16[384,12,2,8]{0,3,2,1:T(8,128)(2,1)S(1)}, bf16[384,12,2,8]{0,3,2,1:T(8,128)(2,1)}, u32[]{:S(2)}) copy-start(bf16[384,12,2,8]{0,3,2,1:T(8,128)(2,1)} %param.14) | copy-start | bytes 442372
  88.9 44.8 %copy-start.6 = (f32[384,8]{0,1:T(8,128)S(1)}, f32[384,8]{0,1:T(8,128)}, u32[]{:S(2)}) copy-start(f32[384,8]{0,1:T(8,128)} %param.15) | copy-start | bytes 36868
  93.0 6.6 %collective-permute-start.6 = (bf16[192,128]{1,0:T(8,128)(2,1)S(1)}, bf16[192,128]{1,0:T(8,128)(2,1)S(1)}, u32[]{:S(2)}, u32[]{:S(2)}) collective-permute-start(bf16[192,128]{1,0:T(8,128)(2,1)S(1)} %fusion.44), channel_id=1, source_target_pairs={{0,16},{8,24},{16,0},{24,8},{1,17},{9,25},{17,1},{25,9},{2,18},{10... | collective-permute-start | bytes 147464 | tf_op jit(solution)/shard_map/ppermute | solution.py:52
  117.9 25.3 %all-to-all-start.2 = ((bf16[8,24,128]{2,1,0:T(8,128)(2,1)}), bf16[8,24,128]{2,1,0:T(8,128)(2,1)S(1)}, u32[]{:S(2)}, u32[]{:S(2)}) async-start(bf16[8,24,128]{2,1,0:T(8,128)(2,1)} %bitcast.36), calls=%async_computation.2 | async-start | bytes 98304 | tf_op jit(solution)/shard_map/all_to_all | solution.py:305
  144.0 11.1 %all-to-all-start.3 = ((f32[8,48,128]{2,1,0:T(8,128)}), f32[8,48,128]{2,1,0:T(8,128)S(1)}, u32[]{:S(2)}, u32[]{:S(2)}) async-start(f32[8,48,128]{2,1,0:T(8,128)} %broadcast_in_dim.137), calls=%async_computation.3 | async-start | bytes 393216 | tf_op jit(solution)/shard_map/all_to_all | solution.py:34
  155.1 18.0 %collective-permute-start.7 = (bf16[24,256]{1,0:T(8,128)(2,1)S(1)}, bf16[24,256]{1,0:T(8,128)(2,1)S(1)}, u32[]{:S(2)}, u32[]{:S(2)}) collective-permute-start(bf16[24,256]{1,0:T(8,128)(2,1)S(1)} %get-tuple-element.22), channel_id=1, source_target_pairs={{0,1},{1,2},{2,3},{3,4},{4,5},{5,6},{6,7},{7,8},{8,9},{9,10},{10,1... | collective-permute-start | bytes 36872 | tf_op jit(solution)/shard_map/ppermute | solution.py:327
  157.2 15.9 %collective-permute-start.8 = (bf16[24,256]{1,0:T(8,128)(2,1)S(1)}, bf16[24,256]{1,0:T(8,128)(2,1)S(1)}, u32[]{:S(2)}, u32[]{:S(2)}) collective-permute-start(bf16[24,256]{1,0:T(8,128)(2,1)S(1)} %get-tuple-element.23), channel_id=1, source_target_pairs={{0,31},{1,0},{2,1},{3,2},{4,3},{5,4},{6,5},{7,6},{8,7},{9,8},{10,9... | collective-permute-start | bytes 36872 | tf_op jit(solution)/shard_map/ppermute | solution.py:328
  169.8 25.0 %all-to-all-start.4 = ((f32[4,48,128]{2,1,0:T(8,128)}), f32[4,48,128]{2,1,0:T(8,128)S(1)}, u32[]{:S(2)}, u32[]{:S(2)}) async-start(f32[4,48,128]{2,1,0:T(8,128)} %broadcast_in_dim.138), calls=%async_computation.4 | async-start | bytes 196608 | tf_op jit(solution)/shard_map/all_to_all | solution.py:34
  195.4 12.9 %all-to-all-start.5 = ((bf16[8,24,128]{2,1,0:T(8,128)(2,1)}), bf16[8,24,128]{2,1,0:T(8,128)(2,1)S(1)}, u32[]{:S(2)}, u32[]{:S(2)}) async-start(bf16[8,24,128]{2,1,0:T(8,128)(2,1)} %broadcast_in_dim.141), calls=%async_computation.5 | async-start | bytes 98304 | tf_op jit(solution)/shard_map/all_to_all | solution.py:34
  209.1 8.5 %all-to-all-start.6 = ((bf16[4,192,128]{2,1,0:T(8,128)(2,1)}), bf16[4,192,128]{2,1,0:T(8,128)(2,1)S(1)}, u32[]{:S(2)}, u32[]{:S(2)}) async-start(bf16[4,192,128]{2,1,0:T(8,128)(2,1)} %broadcast_in_dim.142), calls=%async_computation.6 | async-start | bytes 393216 | tf_op jit(solution)/shard_map/all_to_all | solution.py:34
  217.6 7.7 %collective-permute-start.9 = (bf16[768,128]{1,0:T(8,128)(2,1)S(1)}, bf16[768,128]{1,0:T(8,128)(2,1)S(1)}, u32[]{:S(2)}, u32[]{:S(2)}) collective-permute-start(bf16[768,128]{1,0:T(8,128)(2,1)S(1)} %bitcast.127), channel_id=1, source_target_pairs={{0,32},{32,0},{1,33},{33,1},{2,34},{34,2},{3,35},{35,3},{4,36},{36... | collective-permute-start | bytes 589832 | tf_op jit(solution)/shard_map/ppermute | solution.py:333

commit v4 on v3

--- a/solution.py
+++ b/solution.py
@@ -300,7 +300,12 @@
     mine, other = jnp.where(core == 0, left, right), jnp.where(core == 0, right, left)
     mine = mine + lax.ppermute(other, "core", swap)
     mine = scatter_rows(mine, "y", (1, 2)).astype(BF16)
-    columns, mine = lax.optimization_barrier((columns, mine))
+    mine, edges = lax.optimization_barrier((mine, (grad_rows[:, -1], grad_rows[:, 0])))
+    edges = (
+        lax.ppermute(edges[0], LON, ring(lon, 1)),
+        lax.ppermute(edges[1], LON, ring(lon, -1)),
+    )
+    columns, mine, (before, after) = lax.optimization_barrier((columns, mine, edges))
     ring_size = lax.axis_size("z_lo")
     chunk = lax.all_to_all(mine.reshape(ring_size, -1, mine.shape[1]), "z_lo", 0, 0)
     chunk = jnp.sum(chunk.astype(F32), axis=0)
@@ -315,24 +320,19 @@
 
     pieces = degrees // width
     both = [chunk] + [filter_part[:, i * width : (i + 1) * width] for i in range(pieces)]
-    both = to_all(jnp.concatenate(both, axis=0), ("x", "core"))
+    both = to_all(jnp.concatenate(both, axis=0).astype(BF16), ("x", "core")).astype(F32)
     cores = jnp.sum(both.reshape(-1, 2, *both.shape[1:]), axis=0)
     chunk = jnp.where(core == 0, cores[0, :high], cores[1, :high])
     both = jnp.concatenate([chunk, cores[0, high:] + cores[1, high:]], axis=0)
-    both, edges = lax.optimization_barrier((both, (grad_rows[:, -1], grad_rows[:, 0])))
-    both = jnp.sum(to_all(both, "z_hi"), axis=0)
+    both = jnp.sum(to_all(both.astype(BF16), "z_hi").astype(F32), axis=0)
     filter_grad = both[high:].reshape(pieces, chans, width).transpose(0, 2, 1)
     filter_grad = filter_grad.reshape(degrees, chans)
 
-    before = lax.ppermute(edges[0], LON, ring(lon, 1))
-    after = lax.ppermute(edges[1], LON, ring(lon, -1))
     input_grad = input_part(grad_rows, before, after, taps, tap_weight)
 
     mine = to_all(both[:high].astype(BF16), "z_lo").reshape(-1, width)
-    mine = to_all(mine, "y").reshape(-1, width)
-    other = lax.ppermute(mine, "core", swap)
-    left, right = jnp.where(core == 0, mine, other), jnp.where(core == 0, other, mine)
-    taps_grad = jnp.concatenate([left, right], axis=1).astype(F32)
+    mine = to_all(mine, ("core", "y")).reshape(2, -1, width)
+    taps_grad = jnp.concatenate([mine[0], mine[1]], axis=1).astype(F32)
     taps_grad = taps_grad.reshape(len(taps), channels, channels)
     return (spec_grad, filter_grad, input_grad, taps_grad)
 

time: 227 us -> 229 us (level)
  starting transfers between devices: 132 us -> 143 us
  waiting for transfers between devices: 68.2 us -> 59 us
    all_to_all x4, starting transfers between devices: 15.2 us -> 32.9 us  [to_all(): lax.all_to_all(jnp.broadcast_to(value, (count, *value.shape)), axes, 0, 0)]
    all_to_all x1, waiting for transfers between devices: 17.4 us -> 0.01 us  [on_device(): columns = lax.all_to_all(blocks, LAT, 0, 0)]
    ppermute x3 -> x2, starting transfers between devices: 20.6 us -> 14 us  [the longest x1 10.9 us: on_device(): lax.ppermute(edges[1], LON, ring(lon, -1))]
    all_to_all x1, waiting for transfers between devices: 5.05 us -> 9.15 us  [on_device(): lax.all_to_all(mine.reshape(ring_size, -1, mine.shape[1]), 'z_lo', 0, 0)]
    ppermute x3 -> x2, waiting for transfers between devices: 0.45 us -> 3.18 us  [the longest x1 3.18 us: on_device(): lax.ppermute(edges[0], LON, ring(lon, 1))]
  transfers between devices with their start and end apart: 17 -> 16, of which waited for: 10 -> 9; matrix products, arithmetic and copies ran while one was open for 7% -> 5% of each run, Pallas kernels for 1% -> 1%
where the time goes in v4:
time: 229 us; the launch traced here: 228 us
  starting transfers between devices  143 us (62%)
  waiting for transfers between devices  59 us (26%)
  matrix products  10.5 us (5%)
  local copies, waits for them, and re-layouts  7.16 us (3%)
  Pallas kernels  3.98 us (2%)
  other arithmetic  3.4 us (1%)
    all_to_all x4, waiting for transfers between devices, to_all(): lax.all_to_all(jnp.broadcast_to(value, (count, *value.shape)), axes, 0, 0)  36.9 us
    all_to_all x4, starting transfers between devices, to_all(): lax.all_to_all(jnp.broadcast_to(value, (count, *value.shape)), axes, 0, 0)  32.9 us
    all_to_all x1, starting transfers between devices, on_device(): columns = lax.all_to_all(blocks, LAT, 0, 0)  25.4 us
    ppermute x1, starting transfers between devices, on_device(): lax.ppermute(grad_out[-1], LAT, ring(lat, 1))  16.3 us
    all_to_all x1, starting transfers between devices, on_device(): rows = lax.all_to_all(sent, LON, 0, 0)  16.1 us
    all_to_all x1, starting transfers between devices, on_device(): lax.all_to_all(mine.reshape(ring_size, -1, mine.shape[1]), 'z_lo', 0, 0)  15.8 us
    ppermute x1, starting transfers between devices, on_device(): lax.ppermute(edges[1], LON, ring(lon, -1))  10.9 us
    ppermute x1, starting transfers between devices, on_device(): lax.ppermute(block_input[:, 0], LON, ring(lon, -1))  10.7 us
  transfers between devices with their start and end apart: 16, of which 9 were waited for; matrix products, arithmetic and copies ran while one was open for 5% of the time, Pallas kernels for 1%

profile of v4, /device:TPU:1, one launch (start us, length us, event | category | flops | bytes accessed | tf_op | source)
XLA Modules:
  0.0 228.4 jit_solution(2145217362905112985)
XLA Ops:
  0.6 1.0 copy-done
  1.7 0.0 copy-start.3
  1.7 0.0 copy-start.4
  1.7 1.0 channels_first.1
  2.7 16.1 %all-to-all-start = ((bf16[32,8,1152]{2,1,0:T(8,128)(2,1)}), bf16[32,8,1152]{2,1,0:T(8,128)(2,1)S(1)}, u32[]{:S(2)}, u32[]{:S(2)}) async-start(bf16[32,8,1152]{2,1,0:T(8,128)(2,1)} %bitcast), calls=%async_computation | async-start | bytes 1179648 | tf_op jit(solution)/shard_map/all_to_all | solution.py:282
  18.9 16.3 %collective-permute-start = (bf16[45,256]{1,0:T(8,128)(2,1)S(1)}, bf16[45,256]{1,0:T(8,128)(2,1)S(1)}, u32[]{:S(2)}, u32[]{:S(2)}) collective-permute-start(bf16[45,256]{1,0:T(8,128)(2,1)S(1)} %get-tuple-element.37), channel_id=1, source_target_pairs={{0,32},{32,64},{64,96},{96,128},{128,160},{160,192},{192,224},{224... | collective-permute-start | bytes 69128 | tf_op jit(solution)/shard_map/ppermute | solution.py:285
  35.2 1.9 collective-permute-start.1
  37.1 1.0 fusion.55
  38.1 3.4 %collective-permute-start.2 = (bf16[22,256]{1,0:T(8,128)(2,1)S(1)}, bf16[22,256]{1,0:T(8,128)(2,1)S(1)}, u32[]{:S(2)}, u32[]{:S(2)}) collective-permute-start(bf16[22,256]{1,0:T(8,128)(2,1)S(1)} %bitcast.138), channel_id=1, source_target_pairs={{0,1},{1,2},{2,3},{3,4},{4,5},{5,6},{6,7},{7,8},{8,9},{9,10},{10,1... | collective-permute-start | bytes 33800 | tf_op jit(solution)/shard_map/ppermute | solution.py:287
  41.5 10.7 %collective-permute-start.3 = (bf16[22,256]{1,0:T(8,128)(2,1)S(1)}, bf16[22,256]{1,0:T(8,128)(2,1)S(1)}, u32[]{:S(2)}, u32[]{:S(2)}) collective-permute-start(bf16[22,256]{1,0:T(8,128)(2,1)S(1)} %bitcast.139), channel_id=1, source_target_pairs={{0,31},{1,0},{2,1},{3,2},{4,3},{5,4},{6,5},{7,6},{8,7},{9,8},{10,9... | collective-permute-start | bytes 33800 | tf_op jit(solution)/shard_map/ppermute | solution.py:288
  52.3 0.1 pad_dynamic-slice_fusion.2
  52.4 0.1 pad_dynamic-slice_fusion.5
  52.5 0.0 all-to-all-done
  52.6 0.0 copy-start.9
  52.6 2.7 %fourier_chunks.1 = bf16[32,40,128]{2,1,0:T(8,128)(2,1)} custom-call(bf16[256,1152]{1,0:T(8,128)(2,1)S(1)} %bitcast.120, bf16[512,256]{1,0:T(8,128)(2,1)S(1)} %copy-done.4, f32[2,256,384]{2,1,0:T(8,128)S(1)} %copy-done.2, bf16[192,768]{1,0:T(8,128)(2,1)S(1)} %copy-done.3), custom_call_target="tpu_custom_call" | custom-call | flops 528482304 | bytes 1703936 | tf_op jit(solution)/shard_map/fourier_chunks/pallas_call | solution.py:152
  55.3 0.0 collective-permute-done.1
  55.3 25.4 %all-to-all-start.1 = ((bf16[32,40,128]{2,1,0:T(8,128)(2,1)}), bf16[32,40,128]{2,1,0:T(8,128)(2,1)S(1)}, u32[]{:S(2)}, u32[]{:S(2)}) async-start(bf16[32,40,128]{2,1,0:T(8,128)(2,1)} %fourier_chunks.1), calls=%async_computation.1 | async-start | bytes 655360 | tf_op jit(solution)/shard_map/all_to_all | solution.py:292
  80.8 0.7 convolution_bitcast_fusion.2
  81.6 0.8 convolution_bitcast_fusion.1
  82.3 0.8 convolution_bitcast_fusion.3
  83.1 0.1 maximum_multiply_fusion
  83.2 2.1 collective-permute-start.4
  85.4 1.5 collective-permute-done.4
  86.8 0.1 select_add_fusion
  86.9 0.0 copy-start.5
  86.9 0.0 copy-start.6
  87.0 2.1 collective-permute-start.5
  89.0 0.1 pad_maximum_fusion.13
  89.1 4.1 %collective-permute-done.5 = bf16[2,192,128]{2,1,0:T(8,128)(2,1)S(1)} collective-permute-done((bf16[2,192,128]{2,1,0:T(8,128)(2,1)S(1)}, bf16[2,192,128]{2,1,0:T(8,128)(2,1)S(1)}, u32[]{:S(2)}, u32[]{:S(2)}) %collective-permute-start.5) | collective-permute-done | bytes 98336 | tf_op jit(solution)/shard_map/ppermute | solution.py:52
  93.2 2.4 %collective-permute-start.6 = (bf16[192,128]{1,0:T(8,128)(2,1)S(1)}, bf16[192,128]{1,0:T(8,128)(2,1)S(1)}, u32[]{:S(2)}, u32[]{:S(2)}) collective-permute-start(bf16[192,128]{1,0:T(8,128)(2,1)S(1)} %fusion.44), channel_id=1, source_target_pairs={{0,16},{8,24},{16,0},{24,8},{1,17},{9,25},{17,1},{25,9},{2,18},{10... | collective-permute-start | bytes 147464 | tf_op jit(solution)/shard_map/ppermute | solution.py:52
  95.6 4.2 %collective-permute-done.6 = bf16[192,128]{1,0:T(8,128)(2,1)S(1)} collective-permute-done((bf16[192,128]{1,0:T(8,128)(2,1)S(1)}, bf16[192,128]{1,0:T(8,128)(2,1)S(1)}, u32[]{:S(2)}, u32[]{:S(2)}) %collective-permute-start.6) | collective-permute-done | bytes 49184 | tf_op jit(solution)/shard_map/ppermute | solution.py:52
  99.8 0.6 fusion.43
  100.5 3.1 %collective-permute-start.7 = (bf16[24,256]{1,0:T(8,128)(2,1)S(1)}, bf16[24,256]{1,0:T(8,128)(2,1)S(1)}, u32[]{:S(2)}, u32[]{:S(2)}) collective-permute-start(bf16[24,256]{1,0:T(8,128)(2,1)S(1)} %get-tuple-element.22), channel_id=1, source_target_pairs={{0,1},{1,2},{2,3},{3,4},{4,5},{5,6},{6,7},{7,8},{8,9},{9,10},{10,1... | collective-permute-start | bytes 36872 | tf_op jit(solution)/shard_map/ppermute | solution.py:305
  103.6 10.9 %collective-permute-start.8 = (bf16[24,256]{1,0:T(8,128)(2,1)S(1)}, bf16[24,256]{1,0:T(8,128)(2,1)S(1)}, u32[]{:S(2)}, u32[]{:S(2)}) collective-permute-start(bf16[24,256]{1,0:T(8,128)(2,1)S(1)} %get-tuple-element.23), channel_id=1, source_target_pairs={{0,31},{1,0},{2,1},{3,2},{4,3},{5,4},{6,5},{7,6},{8,7},{9,8},{10,9... | collective-permute-start | bytes 36872 | tf_op jit(solution)/shard_map/ppermute | solution.py:306
  114.5 3.2 %collective-permute-done.7 = bf16[24,256]{1,0:T(8,128)(2,1)S(1)} collective-permute-done((bf16[24,256]{1,0:T(8,128)(2,1)S(1)}, bf16[24,256]{1,0:T(8,128)(2,1)S(1)}, u32[]{:S(2)}, u32[]{:S(2)}) %collective-permute-start.7) | collective-permute-done | bytes 12320 | tf_op jit(solution)/shard_map/ppermute | solution.py:305
  117.7 0.0 all-to-all-done.1.q_ref
  117.7 0.2 unfold.1
  117.9 4.5 %fusion.28 = (f32[8,384]{1,0:T(8,128)S(1)}, bf16[384,12,2,8]{0,3,2,1:T(8,128)(2,1)}) fusion(bf16[384,12,2,8]{0,3,2,1:T(8,128)(2,1)S(1)} %copy-done.5, f32[8,384]{1,0:T(8,128)S(1)} %bitcast.135, bf16[12,16,704]{2,1,0:T(8,128)(2,1)S(1)} %unfold.1, bf16[12,384,704]{1,2,0:T(8,128)(2,1)} %param.13), kind=kOutput, calls=%fused_computation.54 | convolution fusion | flops 104174592 | bytes 7077888 | tf_op jit(solution)/shard_map/mla,mxa->mxl/dot_general | solution.py:315
  122.5 15.8 %all-to-all-start.2 = ((bf16[8,24,128]{2,1,0:T(8,128)(2,1)}), bf16[8,24,128]{2,1,0:T(8,128)(2,1)S(1)}, u32[]{:S(2)}, u32[]{:S(2)}) async-start(bf16[8,24,128]{2,1,0:T(8,128)(2,1)} %bitcast.36), calls=%async_computation.2 | async-start | bytes 98304 | tf_op jit(solution)/shard_map/all_to_all | solution.py:310
  138.3 0.4 maximum_maximum_fusion
  138.8 9.1 %all-to-all-done.2 = bf16[8,24,128]{2,1,0:T(8,128)(2,1)S(1)} async-done(((bf16[8,24,128]{2,1,0:T(8,128)(2,1)}), bf16[8,24,128]{2,1,0:T(8,128)(2,1)S(1)}, u32[]{:S(2)}, u32[]{:S(2)}) %all-to-all-start.2) | async-done | bytes 49184 | tf_op jit(solution)/shard_map/all_to_all | solution.py:310
  147.9 0.7 broadcast_in_dim.137
  148.6 5.1 %all-to-all-start.3 = ((bf16[8,48,128]{2,1,0:T(8,128)(2,1)}), bf16[8,48,128]{2,1,0:T(8,128)(2,1)S(1)}, u32[]{:S(2)}, u32[]{:S(2)}) async-start(bf16[8,48,128]{2,1,0:T(8,128)(2,1)} %broadcast_in_dim.137), calls=%async_computation.3 | async-start | bytes 196608 | tf_op jit(solution)/shard_map/all_to_all | solution.py:34
  153.7 0.4 multiply_convert_fusion.2
  154.1 0.2 reshape.156
  154.3 4.4 %all-to-all-done.3 = bf16[8,48,128]{2,1,0:T(8,128)(2,1)S(1)} async-done(((bf16[8,48,128]{2,1,0:T(8,128)(2,1)}), bf16[8,48,128]{2,1,0:T(8,128)(2,1)S(1)}, u32[]{:S(2)}, u32[]{:S(2)}) %all-to-all-start.3) | async-done | bytes 98336 | tf_op jit(solution)/shard_map/all_to_all | solution.py:34
  158.8 0.6 broadcast_in_dim.138
  159.4 14.8 %all-to-all-start.4 = ((bf16[4,48,128]{2,1,0:T(8,128)(2,1)}), bf16[4,48,128]{2,1,0:T(8,128)(2,1)S(1)}, u32[]{:S(2)}, u32[]{:S(2)}) async-start(bf16[4,48,128]{2,1,0:T(8,128)(2,1)} %broadcast_in_dim.138), calls=%async_computation.4 | async-start | bytes 98304 | tf_op jit(solution)/shard_map/all_to_all | solution.py:34
  174.2 0.7 multiply_convert_fusion
  174.9 20.6 %all-to-all-done.4 = bf16[4,48,128]{2,1,0:T(8,128)(2,1)S(1)} async-done(((bf16[4,48,128]{2,1,0:T(8,128)(2,1)}), bf16[4,48,128]{2,1,0:T(8,128)(2,1)S(1)}, u32[]{:S(2)}, u32[]{:S(2)}) %all-to-all-start.4) | async-done | bytes 49184 | tf_op jit(solution)/shard_map/all_to_all | solution.py:34
  195.4 0.6 broadcast_in_dim.141
  196.1 3.3 %all-to-all-start.5 = ((bf16[8,24,128]{2,1,0:T(8,128)(2,1)}), bf16[8,24,128]{2,1,0:T(8,128)(2,1)S(1)}, u32[]{:S(2)}, u32[]{:S(2)}) async-start(bf16[8,24,128]{2,1,0:T(8,128)(2,1)} %broadcast_in_dim.141), calls=%async_computation.5 | async-start | bytes 98304 | tf_op jit(solution)/shard_map/all_to_all | solution.py:34
  199.4 1.2 fusion.37
  200.6 0.2 reshape.157
  200.8 0.2 reshape.158
  201.0 1.2 convolution_add_fusion.1
  202.2 6.7 %all-to-all-done.5 = bf16[8,24,128]{2,1,0:T(8,128)(2,1)S(1)} async-done(((bf16[8,24,128]{2,1,0:T(8,128)(2,1)}), bf16[8,24,128]{2,1,0:T(8,128)(2,1)S(1)}, u32[]{:S(2)}, u32[]{:S(2)}) %all-to-all-start.5) | async-done | bytes 49184 | tf_op jit(solution)/shard_map/all_to_all | solution.py:34
  209.0 0.8 broadcast_in_dim.142
  209.8 9.7 %all-to-all-start.6 = ((bf16[8,192,128]{2,1,0:T(8,128)(2,1)}), bf16[8,192,128]{2,1,0:T(8,128)(2,1)S(1)}, u32[]{:S(2)}, u32[]{:S(2)}) async-start(bf16[8,192,128]{2,1,0:T(8,128)(2,1)} %broadcast_in_dim.142), calls=%async_computation.6 | async-start | bytes 786432 | tf_op jit(solution)/shard_map/all_to_all | solution.py:34
  219.4 1.2 fusion
  220.7 1.0 convert_element_type.113
  221.6 0.6 slice_bitcast_fusion.2
  222.2 5.2 %all-to-all-done.6 = bf16[8,192,128]{2,1,0:T(8,128)(2,1)S(1)} async-done(((bf16[8,192,128]{2,1,0:T(8,128)(2,1)}), bf16[8,192,128]{2,1,0:T(8,128)(2,1)S(1)}, u32[]{:S(2)}, u32[]{:S(2)}) %all-to-all-start.6) | async-done | bytes 393248 | tf_op jit(solution)/shard_map/all_to_all | solution.py:34
  227.4 0.9 maximum_convert_fusion
  (45 shorter events, 0.4 us)
Async XLA Ops:
  0.6 1.0 copy-start
  1.7 17.2 %copy-start.1 = (bf16[22,45,256]{2,1,0:T(8,128)(2,1)S(1)}, bf16[22,45,256]{2,1,0:T(8,128)(2,1)}, u32[]{:S(2)}) copy-start(bf16[22,45,256]{2,1,0:T(8,128)(2,1)} %x_ref.1) | copy-start | bytes 1520644
  1.7 50.6 %copy-start.7 = (f32[704,3]{0,1:T(4,128)S(1)}, f32[704,3]{0,1:T(4,128)}, u32[]{:S(2)}) copy-start(f32[704,3]{0,1:T(4,128)} %param.16) | copy-start | bytes 25348
  1.7 50.7 %copy-start.8 = (s32[704,3]{0,1:T(4,128)S(1)}, s32[704,3]{0,1:T(4,128)}, u32[]{:S(2)}) copy-start(s32[704,3]{0,1:T(4,128)} %param.17) | copy-start | bytes 25348
  1.7 50.8 %copy-start.2 = (f32[2,256,384]{2,1,0:T(8,128)S(1)}, f32[2,256,384]{2,1,0:T(8,128)}, u32[]{:S(2)}) copy-start(f32[2,256,384]{2,1,0:T(8,128)} %constant.62.clone.tw_ref) | copy-start | bytes 2359300
  1.7 50.9 %copy-start.3 = (bf16[192,768]{1,0:T(8,128)(2,1)S(1)}, bf16[192,768]{1,0:T(8,128)(2,1)}, u32[]{:S(2)}) copy-start(bf16[192,768]{1,0:T(8,128)(2,1)} %constant.63.clone.w_ref) | copy-start | bytes 884740
  1.7 50.8 %copy-start.4 = (bf16[512,256]{1,0:T(8,128)(2,1)S(1)}, bf16[512,256]{1,0:T(8,128)(2,1)}, u32[]{:S(2)}) copy-start(bf16[512,256]{1,0:T(8,128)(2,1)} %constant.61.clone.d_ref) | copy-start | bytes 786436
  2.7 49.8 %all-to-all-start = ((bf16[32,8,1152]{2,1,0:T(8,128)(2,1)}), bf16[32,8,1152]{2,1,0:T(8,128)(2,1)S(1)}, u32[]{:S(2)}, u32[]{:S(2)}) async-start(bf16[32,8,1152]{2,1,0:T(8,128)(2,1)} %bitcast), calls=%async_computation | async-start | bytes 1179648 | tf_op jit(solution)/shard_map/all_to_all | solution.py:282
  18.9 36.4 %collective-permute-start = (bf16[45,256]{1,0:T(8,128)(2,1)S(1)}, bf16[45,256]{1,0:T(8,128)(2,1)S(1)}, u32[]{:S(2)}, u32[]{:S(2)}) collective-permute-start(bf16[45,256]{1,0:T(8,128)(2,1)S(1)} %get-tuple-element.37), channel_id=1, source_target_pairs={{0,32},{32,64},{64,96},{96,128},{128,160},{160,192},{192,224},{224... | collective-permute-start | bytes 69128 | tf_op jit(solution)/shard_map/ppermute | solution.py:285
  35.2 20.1 %collective-permute-start.1 = (bf16[45,256]{1,0:T(8,128)(2,1)S(1)}, bf16[45,256]{1,0:T(8,128)(2,1)S(1)}, u32[]{:S(2)}, u32[]{:S(2)}) collective-permute-start(bf16[45,256]{1,0:T(8,128)(2,1)S(1)} %get-tuple-element.36), channel_id=1, source_target_pairs={{0,992},{32,0},{64,32},{96,64},{128,96},{160,128},{192,160},{224,1... | collective-permute-start | bytes 69128 | tf_op jit(solution)/shard_map/ppermute | solution.py:286
  38.1 17.2 %collective-permute-start.2 = (bf16[22,256]{1,0:T(8,128)(2,1)S(1)}, bf16[22,256]{1,0:T(8,128)(2,1)S(1)}, u32[]{:S(2)}, u32[]{:S(2)}) collective-permute-start(bf16[22,256]{1,0:T(8,128)(2,1)S(1)} %bitcast.138), channel_id=1, source_target_pairs={{0,1},{1,2},{2,3},{3,4},{4,5},{5,6},{6,7},{7,8},{8,9},{9,10},{10,1... | collective-permute-start | bytes 33800 | tf_op jit(solution)/shard_map/ppermute | solution.py:287
  41.5 13.8 %collective-permute-start.3 = (bf16[22,256]{1,0:T(8,128)(2,1)S(1)}, bf16[22,256]{1,0:T(8,128)(2,1)S(1)}, u32[]{:S(2)}, u32[]{:S(2)}) collective-permute-start(bf16[22,256]{1,0:T(8,128)(2,1)S(1)} %bitcast.139), channel_id=1, source_target_pairs={{0,31},{1,0},{2,1},{3,2},{4,3},{5,4},{6,5},{7,6},{8,7},{9,8},{10,9... | collective-permute-start | bytes 33800 | tf_op jit(solution)/shard_map/ppermute | solution.py:288
  52.6 28.3 %copy-start.9 = (bf16[22,45,256]{2,1,0:T(8,128)(2,1)S(1)}, bf16[22,45,256]{2,1,0:T(8,128)(2,1)}, u32[]{:S(2)}) copy-start(bf16[22,45,256]{2,1,0:T(8,128)(2,1)} %param.12) | copy-start | bytes 1520644
  55.3 62.4 %all-to-all-start.1 = ((bf16[32,40,128]{2,1,0:T(8,128)(2,1)}), bf16[32,40,128]{2,1,0:T(8,128)(2,1)S(1)}, u32[]{:S(2)}, u32[]{:S(2)}) async-start(bf16[32,40,128]{2,1,0:T(8,128)(2,1)} %fourier_chunks.1), calls=%async_computation.1 | async-start | bytes 655360 | tf_op jit(solution)/shard_map/all_to_all | solution.py:292
  83.2 3.6 %collective-permute-start.4 = (f32[768,128]{1,0:T(8,128)S(1)}, f32[768,128]{1,0:T(8,128)S(1)}, u32[]{:S(2)}, u32[]{:S(2)}) collective-permute-start(f32[768,128]{1,0:T(8,128)S(1)} %slice_select_fusion.3), channel_id=1, source_target_pairs={{0,32},{32,0},{1,33},{33,1},{2,34},{34,2},{3,35},{35,3},{4,36},{36... | collective-permute-start | bytes 1179656 | tf_op jit(solution)/shard_map/ppermute | solution.py:301
  86.9 31.0 %copy-start.5 = (bf16[384,12,2,8]{0,3,2,1:T(8,128)(2,1)S(1)}, bf16[384,12,2,8]{0,3,2,1:T(8,128)(2,1)}, u32[]{:S(2)}) copy-start(bf16[384,12,2,8]{0,3,2,1:T(8,128)(2,1)} %param.14) | copy-start | bytes 442372
  86.9 31.0 %copy-start.6 = (f32[384,8]{0,1:T(8,128)S(1)}, f32[384,8]{0,1:T(8,128)}, u32[]{:S(2)}) copy-start(f32[384,8]{0,1:T(8,128)} %param.15) | copy-start | bytes 36868
  87.0 6.2 %collective-permute-start.5 = (bf16[2,192,128]{2,1,0:T(8,128)(2,1)S(1)}, bf16[2,192,128]{2,1,0:T(8,128)(2,1)S(1)}, u32[]{:S(2)}, u32[]{:S(2)}) collective-permute-start(bf16[2,192,128]{2,1,0:T(8,128)(2,1)S(1)} %fusion.42), channel_id=1, source_target_pairs={{0,8},{8,0},{16,24},{24,16},{1,9},{9,1},{17,25},{25,17},{2,10},{10... | collective-permute-start | bytes 294920 | tf_op jit(solution)/shard_map/ppermute | solution.py:52
  93.2 6.6 %collective-permute-start.6 = (bf16[192,128]{1,0:T(8,128)(2,1)S(1)}, bf16[192,128]{1,0:T(8,128)(2,1)S(1)}, u32[]{:S(2)}, u32[]{:S(2)}) collective-permute-start(bf16[192,128]{1,0:T(8,128)(2,1)S(1)} %fusion.44), channel_id=1, source_target_pairs={{0,16},{8,24},{16,0},{24,8},{1,17},{9,25},{17,1},{25,9},{2,18},{10... | collective-permute-start | bytes 147464 | tf_op jit(solution)/shard_map/ppermute | solution.py:52
  100.5 17.2 %collective-permute-start.7 = (bf16[24,256]{1,0:T(8,128)(2,1)S(1)}, bf16[24,256]{1,0:T(8,128)(2,1)S(1)}, u32[]{:S(2)}, u32[]{:S(2)}) collective-permute-start(bf16[24,256]{1,0:T(8,128)(2,1)S(1)} %get-tuple-element.22), channel_id=1, source_target_pairs={{0,1},{1,2},{2,3},{3,4},{4,5},{5,6},{6,7},{7,8},{8,9},{9,10},{10,1... | collective-permute-start | bytes 36872 | tf_op jit(solution)/shard_map/ppermute | solution.py:305
  103.6 14.1 %collective-permute-start.8 = (bf16[24,256]{1,0:T(8,128)(2,1)S(1)}, bf16[24,256]{1,0:T(8,128)(2,1)S(1)}, u32[]{:S(2)}, u32[]{:S(2)}) collective-permute-start(bf16[24,256]{1,0:T(8,128)(2,1)S(1)} %get-tuple-element.23), channel_id=1, source_target_pairs={{0,31},{1,0},{2,1},{3,2},{4,3},{5,4},{6,5},{7,6},{8,7},{9,8},{10,9... | collective-permute-start | bytes 36872 | tf_op jit(solution)/shard_map/ppermute | solution.py:306
  122.5 25.4 %all-to-all-start.2 = ((bf16[8,24,128]{2,1,0:T(8,128)(2,1)}), bf16[8,24,128]{2,1,0:T(8,128)(2,1)S(1)}, u32[]{:S(2)}, u32[]{:S(2)}) async-start(bf16[8,24,128]{2,1,0:T(8,128)(2,1)} %bitcast.36), calls=%async_computation.2 | async-start | bytes 98304 | tf_op jit(solution)/shard_map/all_to_all | solution.py:310
  148.6 10.1 %all-to-all-start.3 = ((bf16[8,48,128]{2,1,0:T(8,128)(2,1)}), bf16[8,48,128]{2,1,0:T(8,128)(2,1)S(1)}, u32[]{:S(2)}, u32[]{:S(2)}) async-start(bf16[8,48,128]{2,1,0:T(8,128)(2,1)} %broadcast_in_dim.137), calls=%async_computation.3 | async-start | bytes 196608 | tf_op jit(solution)/shard_map/all_to_all | solution.py:34
  159.4 36.0 %all-to-all-start.4 = ((bf16[4,48,128]{2,1,0:T(8,128)(2,1)}), bf16[4,48,128]{2,1,0:T(8,128)(2,1)S(1)}, u32[]{:S(2)}, u32[]{:S(2)}) async-start(bf16[4,48,128]{2,1,0:T(8,128)(2,1)} %broadcast_in_dim.138), calls=%async_computation.4 | async-start | bytes 98304 | tf_op jit(solution)/shard_map/all_to_all | solution.py:34
  196.1 12.9 %all-to-all-start.5 = ((bf16[8,24,128]{2,1,0:T(8,128)(2,1)}), bf16[8,24,128]{2,1,0:T(8,128)(2,1)S(1)}, u32[]{:S(2)}, u32[]{:S(2)}) async-start(bf16[8,24,128]{2,1,0:T(8,128)(2,1)} %broadcast_in_dim.141), calls=%async_computation.5 | async-start | bytes 98304 | tf_op jit(solution)/shard_map/all_to_all | solution.py:34
  209.8 17.6 %all-to-all-start.6 = ((bf16[8,192,128]{2,1,0:T(8,128)(2,1)}), bf16[8,192,128]{2,1,0:T(8,128)(2,1)S(1)}, u32[]{:S(2)}, u32[]{:S(2)}) async-start(bf16[8,192,128]{2,1,0:T(8,128)(2,1)} %broadcast_in_dim.142), calls=%async_computation.6 | async-start | bytes 786432 | tf_op jit(solution)/shard_map/all_to_all | solution.py:34

commit v5 on v3

--- a/solution.py
+++ b/solution.py
@@ -38,19 +38,13 @@
     return [(i, i ^ bit) for i in range(size)]
 
 
-def scatter_rows(value, axis, bits):
-    size, place = lax.axis_size(axis), lax.axis_index(axis)
-    left = sorted(bits, reverse=True)
-    value = value.reshape(*(2 for _ in left), -1, value.shape[-1])
-    for bit in bits:
-        where = left.index(bit)
-        left.remove(bit)
-        low = lax.index_in_dim(value, 0, where, keepdims=False)
-        high = lax.index_in_dim(value, 1, where, keepdims=False)
-        upper = (place & bit) != 0
-        value, sent = jnp.where(upper, high, low), jnp.where(upper, low, high)
-        value = value + lax.ppermute(sent.astype(BF16), axis, pairs(size, bit)).astype(F32)
-    return value
+def halve(value, axis, bit, where):
+    low = lax.index_in_dim(value, 0, where, keepdims=False)
+    high = lax.index_in_dim(value, 1, where, keepdims=False)
+    upper = (lax.axis_index(axis) & bit) != 0
+    value, sent = jnp.where(upper, high, low), jnp.where(upper, low, high)
+    received = lax.ppermute(sent.astype(BF16), axis, pairs(lax.axis_size(axis), bit))
+    return value + received.astype(F32)
 
 
 def transform_constants(sectors, sector, orders, chans):
@@ -299,11 +293,11 @@
     left, right = part[:, : channels // 2], part[:, channels // 2 :]
     mine, other = jnp.where(core == 0, left, right), jnp.where(core == 0, right, left)
     mine = mine + lax.ppermute(other, "core", swap)
-    mine = scatter_rows(mine, "y", (1, 2)).astype(BF16)
+    mine = mine.reshape(2, 2, 2, 2, 2, -1, mine.shape[1])
+    mine = halve(halve(mine, "y", 1, 1), "y", 2, 0)
+    mine = halve(halve(mine, "z_lo", 1, 2), "z_lo", 2, 1)
     columns, mine = lax.optimization_barrier((columns, mine))
-    ring_size = lax.axis_size("z_lo")
-    chunk = lax.all_to_all(mine.reshape(ring_size, -1, mine.shape[1]), "z_lo", 0, 0)
-    chunk = jnp.sum(chunk.astype(F32), axis=0)
+    chunk = halve(mine, "z_lo", 4, 0)
     high, width = chunk.shape
 
     fourier = unfold(columns, rows_here, orders_here, chans)
@@ -320,19 +314,21 @@
     chunk = jnp.where(core == 0, cores[0, :high], cores[1, :high])
     both = jnp.concatenate([chunk, cores[0, high:] + cores[1, high:]], axis=0)
     both, edges = lax.optimization_barrier((both, (grad_rows[:, -1], grad_rows[:, 0])))
-    both = jnp.sum(to_all(both, "z_hi"), axis=0)
+    edges = (
+        lax.ppermute(edges[0], LON, ring(lon, 1)),
+        lax.ppermute(edges[1], LON, ring(lon, -1)),
+    )
+    both = to_all(both, "z_hi")
+    both, (before, after) = lax.optimization_barrier((both, edges))
+    both = jnp.sum(both, axis=0)
     filter_grad = both[high:].reshape(pieces, chans, width).transpose(0, 2, 1)
     filter_grad = filter_grad.reshape(degrees, chans)
 
-    before = lax.ppermute(edges[0], LON, ring(lon, 1))
-    after = lax.ppermute(edges[1], LON, ring(lon, -1))
     input_grad = input_part(grad_rows, before, after, taps, tap_weight)
 
     mine = to_all(both[:high].astype(BF16), "z_lo").reshape(-1, width)
-    mine = to_all(mine, "y").reshape(-1, width)
-    other = lax.ppermute(mine, "core", swap)
-    left, right = jnp.where(core == 0, mine, other), jnp.where(core == 0, other, mine)
-    taps_grad = jnp.concatenate([left, right], axis=1).astype(F32)
+    mine = to_all(mine, ("core", "y")).reshape(2, -1, width)
+    taps_grad = jnp.concatenate([mine[0], mine[1]], axis=1).astype(F32)
     taps_grad = taps_grad.reshape(len(taps), channels, channels)
     return (spec_grad, filter_grad, input_grad, taps_grad)
 

time: 227 us -> 227 us (level)
  starting transfers between devices: 132 us -> 146 us
  waiting for transfers between devices: 68.2 us -> 56.5 us
  matrix products: 10.5 us -> 7.74 us
    all_to_all x4, starting transfers between devices: 15.2 us -> 33.8 us  [to_all(): lax.all_to_all(jnp.broadcast_to(value, (count, *value.shape)), axes, 0, 0)]
    ppermute x5 -> x7, waiting for transfers between devices: 8.71 us -> 26.1 us  [the longest x5 23 us: halve(): lax.ppermute(sent.astype(BF16), axis, pairs(lax.axis_size(axis), bit))]
    all_to_all x1 -> x0, starting transfers between devices: 15.7 us -> none  [on_device(): lax.all_to_all(mine.reshape(ring_size, -1, mine.shape[1]), 'z_lo', 0, 0)]
    all_to_all x1, waiting for transfers between devices: 17.4 us -> 5.01 us  [on_device(): columns = lax.all_to_all(blocks, LAT, 0, 0)]
    ppermute x5 -> x7, starting transfers between devices: 25 us -> 36.2 us  [the longest x5 22.2 us: halve(): lax.ppermute(sent.astype(BF16), axis, pairs(lax.axis_size(axis), bit))]
    all_to_all x4, waiting for transfers between devices: 35.6 us -> 25.3 us  [to_all(): lax.all_to_all(jnp.broadcast_to(value, (count, *value.shape)), axes, 0, 0)]
    all_to_all x1 -> x0, waiting for transfers between devices: 5.05 us -> none  [on_device(): lax.all_to_all(mine.reshape(ring_size, -1, mine.shape[1]), 'z_lo', 0, 0)]
    dot_general x3, matrix products: 3.69 us -> 0.97 us  [input_part(): lax.dot_general(scaled(weight, picked).reshape(-1, channels), tap_weight[...]
  transfers between devices with their start and end apart: 17 -> 18, of which waited for: 10 -> 11; matrix products, arithmetic and copies ran while one was open for 7% -> 2% of each run, Pallas kernels for 1% -> 1%
where the time goes in v5:
time: 227 us; the launch traced here: 225 us
  starting transfers between devices  146 us (64%)
  waiting for transfers between devices  56.5 us (25%)
  matrix products  7.74 us (3%)
  local copies, waits for them, and re-layouts  7.22 us (3%)
  Pallas kernels  3.98 us (2%)
  other arithmetic  2.84 us (1%)
    all_to_all x4, starting transfers between devices, to_all(): lax.all_to_all(jnp.broadcast_to(value, (count, *value.shape)), axes, 0, 0)  33.8 us
    all_to_all x4, waiting for transfers between devices, to_all(): lax.all_to_all(jnp.broadcast_to(value, (count, *value.shape)), axes, 0, 0)  25.3 us
    all_to_all x1, starting transfers between devices, on_device(): columns = lax.all_to_all(blocks, LAT, 0, 0)  23.6 us
    ppermute x5, waiting for transfers between devices, halve(): lax.ppermute(sent.astype(BF16), axis, pairs(lax.axis_size(axis), bit))  23 us
    ppermute x5, starting transfers between devices, halve(): lax.ppermute(sent.astype(BF16), axis, pairs(lax.axis_size(axis), bit))  22.2 us
    ppermute x1, starting transfers between devices, on_device(): lax.ppermute(grad_out[-1], LAT, ring(lat, 1))  16.3 us
    all_to_all x1, starting transfers between devices, on_device(): rows = lax.all_to_all(sent, LON, 0, 0)  16.1 us
    ppermute x1, starting transfers between devices, on_device(): lax.ppermute(edges[1], LON, ring(lon, -1))  12.1 us
  transfers between devices with their start and end apart: 18, of which 11 were waited for; matrix products, arithmetic and copies ran while one was open for 2% of the time, Pallas kernels for 1%

profile of v5, /device:TPU:1, one launch (start us, length us, event | category | flops | bytes accessed | tf_op | source)
XLA Modules:
  0.0 225.4 jit_solution(17246874227138621724)
XLA Ops:
  0.6 1.0 copy-done
  1.7 0.0 copy-start.3
  1.7 0.0 copy-start.4
  1.7 1.0 channels_first.1
  2.7 16.1 %all-to-all-start = ((bf16[32,8,1152]{2,1,0:T(8,128)(2,1)}), bf16[32,8,1152]{2,1,0:T(8,128)(2,1)S(1)}, u32[]{:S(2)}, u32[]{:S(2)}) async-start(bf16[32,8,1152]{2,1,0:T(8,128)(2,1)} %bitcast), calls=%async_computation | async-start | bytes 1179648 | tf_op jit(solution)/shard_map/all_to_all | solution.py:276
  18.9 16.3 %collective-permute-start = (bf16[45,256]{1,0:T(8,128)(2,1)S(1)}, bf16[45,256]{1,0:T(8,128)(2,1)S(1)}, u32[]{:S(2)}, u32[]{:S(2)}) collective-permute-start(bf16[45,256]{1,0:T(8,128)(2,1)S(1)} %get-tuple-element.39), channel_id=1, source_target_pairs={{0,32},{32,64},{64,96},{96,128},{128,160},{160,192},{192,224},{224... | collective-permute-start | bytes 69128 | tf_op jit(solution)/shard_map/ppermute | solution.py:279
  35.2 1.9 collective-permute-start.1
  37.1 1.0 fusion.59
  38.1 3.4 %collective-permute-start.2 = (bf16[22,256]{1,0:T(8,128)(2,1)S(1)}, bf16[22,256]{1,0:T(8,128)(2,1)S(1)}, u32[]{:S(2)}, u32[]{:S(2)}) collective-permute-start(bf16[22,256]{1,0:T(8,128)(2,1)S(1)} %bitcast.178), channel_id=1, source_target_pairs={{0,1},{1,2},{2,3},{3,4},{4,5},{5,6},{6,7},{7,8},{8,9},{9,10},{10,1... | collective-permute-start | bytes 33800 | tf_op jit(solution)/shard_map/ppermute | solution.py:281
  41.5 10.7 %collective-permute-start.3 = (bf16[22,256]{1,0:T(8,128)(2,1)S(1)}, bf16[22,256]{1,0:T(8,128)(2,1)S(1)}, u32[]{:S(2)}, u32[]{:S(2)}) collective-permute-start(bf16[22,256]{1,0:T(8,128)(2,1)S(1)} %bitcast.179), channel_id=1, source_target_pairs={{0,31},{1,0},{2,1},{3,2},{4,3},{5,4},{6,5},{7,6},{8,7},{9,8},{10,9... | collective-permute-start | bytes 33800 | tf_op jit(solution)/shard_map/ppermute | solution.py:282
  52.3 0.1 pad_dynamic-slice_fusion.2
  52.4 0.1 pad_dynamic-slice_fusion.5
  52.6 0.0 copy-start.10
  52.6 2.7 %fourier_chunks.1 = bf16[32,40,128]{2,1,0:T(8,128)(2,1)} custom-call(bf16[256,1152]{1,0:T(8,128)(2,1)S(1)} %bitcast.160, bf16[512,256]{1,0:T(8,128)(2,1)S(1)} %copy-done.4, f32[2,256,384]{2,1,0:T(8,128)S(1)} %copy-done.2, bf16[192,768]{1,0:T(8,128)(2,1)S(1)} %copy-done.3), custom_call_target="tpu_custom_call" | custom-call | flops 528482304 | bytes 1703936 | tf_op jit(solution)/shard_map/fourier_chunks/pallas_call | solution.py:146
  55.4 0.7 convolution_bitcast_fusion.2
  56.1 0.7 convolution_bitcast_fusion.1
  56.9 0.7 convolution_bitcast_fusion.3
  57.6 0.1 maximum_multiply_fusion
  57.8 3.8 %collective-permute-start.4 = (f32[768,128]{1,0:T(8,128)S(1)}, f32[768,128]{1,0:T(8,128)S(1)}, u32[]{:S(2)}, u32[]{:S(2)}) collective-permute-start(f32[768,128]{1,0:T(8,128)S(1)} %slice_select_fusion.3), channel_id=1, source_target_pairs={{0,32},{32,0},{1,33},{33,1},{2,34},{34,2},{3,35},{35,3},{4,36},{36... | collective-permute-start | bytes 1179656 | tf_op jit(solution)/shard_map/ppermute | solution.py:295
  61.6 23.6 %all-to-all-start.1 = ((bf16[32,40,128]{2,1,0:T(8,128)(2,1)}), bf16[32,40,128]{2,1,0:T(8,128)(2,1)S(1)}, u32[]{:S(2)}, u32[]{:S(2)}) async-start(bf16[32,40,128]{2,1,0:T(8,128)(2,1)} %fourier_chunks.1), calls=%async_computation.1 | async-start | bytes 655360 | tf_op jit(solution)/shard_map/all_to_all | solution.py:286
  85.3 0.1 select_add_fusion
  85.3 1.9 collective-permute-start.5
  87.3 4.1 %collective-permute-done.5 = bf16[2,2,2,2,24,128]{5,4,3,2,1,0:T(8,128)(2,1)S(1)} collective-permute-done((bf16[2,2,2,2,24,128]{5,4,3,2,1,0:T(8,128)(2,1)S(1)}, bf16[2,2,2,2,24,128]{5,4,3,2,1,0:T(8,128)(2,1)S(1)}, u32[]{:S(2)}, u32[]{:S(2)}) %collective-permute-start.5) | collective-permute-done | bytes 98336 | tf_op jit(solution)/shard_map/ppermute | solution.py:46
  91.5 0.0 copy-start.7
  91.5 2.5 %collective-permute-start.6 = (bf16[2,2,2,24,128]{4,3,2,1,0:T(8,128)(2,1)S(1)}, bf16[2,2,2,24,128]{4,3,2,1,0:T(8,128)(2,1)S(1)}, u32[]{:S(2)}, u32[]{:S(2)}) collective-permute-start(bf16[2,2,2,24,128]{4,3,2,1,0:T(8,128)(2,1)S(1)} %fusion.43), channel_id=1, source_target_pairs={{0,16},{8,24},{16,0},{24,8},{1,17},{9,25},{17,1},{25,9},{2,18},{10... | collective-permute-start | bytes 147464 | tf_op jit(solution)/shard_map/ppermute | solution.py:46
  94.0 4.2 %collective-permute-done.6 = bf16[2,2,2,24,128]{4,3,2,1,0:T(8,128)(2,1)S(1)} collective-permute-done((bf16[2,2,2,24,128]{4,3,2,1,0:T(8,128)(2,1)S(1)}, bf16[2,2,2,24,128]{4,3,2,1,0:T(8,128)(2,1)S(1)}, u32[]{:S(2)}, u32[]{:S(2)}) %collective-permute-start.6) | collective-permute-done | bytes 49184 | tf_op jit(solution)/shard_map/ppermute | solution.py:46
  98.3 3.1 %collective-permute-start.7 = (bf16[2,2,24,128]{3,2,1,0:T(8,128)(2,1)S(1)}, bf16[2,2,24,128]{3,2,1,0:T(8,128)(2,1)S(1)}, u32[]{:S(2)}, u32[]{:S(2)}) collective-permute-start(bf16[2,2,24,128]{3,2,1,0:T(8,128)(2,1)S(1)} %fusion.46), channel_id=1, source_target_pairs={{0,1},{1,0},{2,3},{3,2},{4,5},{5,4},{6,7},{7,6},{8,9},{9,8},{10,11... | collective-permute-start | bytes 73736 | tf_op jit(solution)/shard_map/ppermute | solution.py:46
  101.4 9.1 %collective-permute-done.7 = bf16[2,2,24,128]{3,2,1,0:T(8,128)(2,1)S(1)} collective-permute-done((bf16[2,2,24,128]{3,2,1,0:T(8,128)(2,1)S(1)}, bf16[2,2,24,128]{3,2,1,0:T(8,128)(2,1)S(1)}, u32[]{:S(2)}, u32[]{:S(2)}) %collective-permute-start.7) | collective-permute-done | bytes 24608 | tf_op jit(solution)/shard_map/ppermute | solution.py:46
  110.5 1.9 collective-permute-start.8
  112.4 0.1 pad_maximum_fusion.13
  112.5 4.6 %collective-permute-done.8 = bf16[2,24,128]{2,1,0:T(8,128)(2,1)S(1)} collective-permute-done((bf16[2,24,128]{2,1,0:T(8,128)(2,1)S(1)}, bf16[2,24,128]{2,1,0:T(8,128)(2,1)S(1)}, u32[]{:S(2)}, u32[]{:S(2)}) %collective-permute-start.8) | collective-permute-done | bytes 12320 | tf_op jit(solution)/shard_map/ppermute | solution.py:46
  117.1 5.0 %all-to-all-done.1.q_ref = bf16[32,40,128]{2,1,0:T(8,128)(2,1)S(1)} async-done(((bf16[32,40,128]{2,1,0:T(8,128)(2,1)}), bf16[32,40,128]{2,1,0:T(8,128)(2,1)S(1)}, u32[]{:S(2)}, u32[]{:S(2)}) %all-to-all-start.1) | async-done | bytes 327712 | tf_op jit(solution)/shard_map/all_to_all | solution.py:286
  122.1 0.2 unfold.1
  122.4 4.5 %fusion.28 = (f32[8,384]{1,0:T(8,128)S(1)}, bf16[384,12,2,8]{0,3,2,1:T(8,128)(2,1)}) fusion(bf16[384,12,2,8]{0,3,2,1:T(8,128)(2,1)S(1)} %copy-done.5, f32[8,384]{1,0:T(8,128)S(1)} %bitcast.175, bf16[12,16,704]{2,1,0:T(8,128)(2,1)S(1)} %unfold.1, bf16[12,384,704]{1,2,0:T(8,128)(2,1)} %param.13), kind=kOutput, calls=%fused_computation.54 | convolution fusion | flops 104174592 | bytes 7077888 | tf_op jit(solution)/shard_map/mla,mxa->mxl/dot_general | solution.py:304
  126.9 12.7 %collective-permute-start.9 = (bf16[24,128]{1,0:T(8,128)(2,1)S(1)}, bf16[24,128]{1,0:T(8,128)(2,1)S(1)}, u32[]{:S(2)}, u32[]{:S(2)}) collective-permute-start(bf16[24,128]{1,0:T(8,128)(2,1)S(1)} %fusion.52), channel_id=1, source_target_pairs={{0,4},{1,5},{2,6},{3,7},{4,0},{5,1},{6,2},{7,3},{8,12},{9,13},{10,... | collective-permute-start | bytes 18440 | tf_op jit(solution)/shard_map/ppermute | solution.py:46
  139.7 1.0 collective-permute-done.9
  140.7 0.7 broadcast_in_dim.137
  141.4 4.2 %all-to-all-start.2 = ((f32[8,48,128]{2,1,0:T(8,128)}), f32[8,48,128]{2,1,0:T(8,128)S(1)}, u32[]{:S(2)}, u32[]{:S(2)}) async-start(f32[8,48,128]{2,1,0:T(8,128)} %broadcast_in_dim.137), calls=%async_computation.2 | async-start | bytes 393216 | tf_op jit(solution)/shard_map/all_to_all | solution.py:34
  145.6 5.9 %all-to-all-done.2 = f32[8,48,128]{2,1,0:T(8,128)S(1)} async-done(((f32[8,48,128]{2,1,0:T(8,128)}), f32[8,48,128]{2,1,0:T(8,128)S(1)}, u32[]{:S(2)}, u32[]{:S(2)}) %all-to-all-start.2) | async-done | bytes 196640 | tf_op jit(solution)/shard_map/all_to_all | solution.py:34
  151.5 0.6 broadcast_in_dim.138
  152.2 15.4 %all-to-all-start.3 = ((f32[4,48,128]{2,1,0:T(8,128)}), f32[4,48,128]{2,1,0:T(8,128)S(1)}, u32[]{:S(2)}, u32[]{:S(2)}) async-start(f32[4,48,128]{2,1,0:T(8,128)} %broadcast_in_dim.138), calls=%async_computation.3 | async-start | bytes 196608 | tf_op jit(solution)/shard_map/all_to_all | solution.py:34
  167.5 1.9 collective-permute-start.10
  169.5 12.1 %collective-permute-start.11 = (bf16[24,256]{1,0:T(8,128)(2,1)S(1)}, bf16[24,256]{1,0:T(8,128)(2,1)S(1)}, u32[]{:S(2)}, u32[]{:S(2)}) collective-permute-start(bf16[24,256]{1,0:T(8,128)(2,1)S(1)} %get-tuple-element.26), channel_id=1, source_target_pairs={{0,31},{1,0},{2,1},{3,2},{4,3},{5,4},{6,5},{7,6},{8,7},{9,8},{10,9... | collective-permute-start | bytes 36872 | tf_op jit(solution)/shard_map/ppermute | solution.py:319
  181.5 3.2 %collective-permute-done.10 = bf16[24,256]{1,0:T(8,128)(2,1)S(1)} collective-permute-done((bf16[24,256]{1,0:T(8,128)(2,1)S(1)}, bf16[24,256]{1,0:T(8,128)(2,1)S(1)}, u32[]{:S(2)}, u32[]{:S(2)}) %collective-permute-start.10) | collective-permute-done | bytes 12320 | tf_op jit(solution)/shard_map/ppermute | solution.py:318
  184.7 4.7 %all-to-all-done.3 = f32[4,48,128]{2,1,0:T(8,128)S(1)} async-done(((f32[4,48,128]{2,1,0:T(8,128)}), f32[4,48,128]{2,1,0:T(8,128)S(1)}, u32[]{:S(2)}, u32[]{:S(2)}) %all-to-all-start.3) | async-done | bytes 98336 | tf_op jit(solution)/shard_map/all_to_all | solution.py:34
  189.5 0.4 maximum_maximum_fusion
  189.9 0.4 multiply_convert_fusion.2
  190.3 0.7 multiply_convert_fusion
  191.0 0.0 copy-start.6
  191.1 0.2 reshape.161
  191.2 0.6 broadcast_in_dim.141
  191.9 5.0 %all-to-all-start.4 = ((bf16[8,24,128]{2,1,0:T(8,128)(2,1)}), bf16[8,24,128]{2,1,0:T(8,128)(2,1)S(1)}, u32[]{:S(2)}, u32[]{:S(2)}) async-start(bf16[8,24,128]{2,1,0:T(8,128)(2,1)} %broadcast_in_dim.141), calls=%async_computation.4 | async-start | bytes 98304 | tf_op jit(solution)/shard_map/all_to_all | solution.py:34
  196.9 0.3 fusion.37
  197.2 0.2 reshape.162
  197.4 0.2 reshape.163
  197.5 0.3 convolution_add_fusion.1
  197.9 8.6 %all-to-all-done.4 = bf16[8,24,128]{2,1,0:T(8,128)(2,1)S(1)} async-done(((bf16[8,24,128]{2,1,0:T(8,128)(2,1)}), bf16[8,24,128]{2,1,0:T(8,128)(2,1)S(1)}, u32[]{:S(2)}, u32[]{:S(2)}) %all-to-all-start.4) | async-done | bytes 49184 | tf_op jit(solution)/shard_map/all_to_all | solution.py:34
  206.5 0.8 broadcast_in_dim.142
  207.3 9.2 %all-to-all-start.5 = ((bf16[8,192,128]{2,1,0:T(8,128)(2,1)}), bf16[8,192,128]{2,1,0:T(8,128)(2,1)S(1)}, u32[]{:S(2)}, u32[]{:S(2)}) async-start(bf16[8,192,128]{2,1,0:T(8,128)(2,1)} %broadcast_in_dim.142), calls=%async_computation.5 | async-start | bytes 786432 | tf_op jit(solution)/shard_map/all_to_all | solution.py:34
  216.5 0.3 fusion
  216.8 1.0 convert_element_type.134
  217.8 0.6 slice_bitcast_fusion.2
  218.4 6.1 %all-to-all-done.5 = bf16[8,192,128]{2,1,0:T(8,128)(2,1)S(1)} async-done(((bf16[8,192,128]{2,1,0:T(8,128)(2,1)}), bf16[8,192,128]{2,1,0:T(8,128)(2,1)S(1)}, u32[]{:S(2)}, u32[]{:S(2)}) %all-to-all-start.5) | async-done | bytes 393248 | tf_op jit(solution)/shard_map/all_to_all | solution.py:34
  224.5 0.9 maximum_convert_fusion
  (55 shorter events, 0.4 us)
Async XLA Ops:
  0.6 1.0 copy-start
  1.7 17.2 %copy-start.1 = (bf16[22,45,256]{2,1,0:T(8,128)(2,1)S(1)}, bf16[22,45,256]{2,1,0:T(8,128)(2,1)}, u32[]{:S(2)}) copy-start(bf16[22,45,256]{2,1,0:T(8,128)(2,1)} %x_ref.1) | copy-start | bytes 1520644
  1.7 50.6 %copy-start.8 = (f32[704,3]{0,1:T(4,128)S(1)}, f32[704,3]{0,1:T(4,128)}, u32[]{:S(2)}) copy-start(f32[704,3]{0,1:T(4,128)} %param.16) | copy-start | bytes 25348
  1.7 50.7 %copy-start.9 = (s32[704,3]{0,1:T(4,128)S(1)}, s32[704,3]{0,1:T(4,128)}, u32[]{:S(2)}) copy-start(s32[704,3]{0,1:T(4,128)} %param.17) | copy-start | bytes 25348
  1.7 50.8 %copy-start.2 = (f32[2,256,384]{2,1,0:T(8,128)S(1)}, f32[2,256,384]{2,1,0:T(8,128)}, u32[]{:S(2)}) copy-start(f32[2,256,384]{2,1,0:T(8,128)} %constant.67.clone.tw_ref) | copy-start | bytes 2359300
  1.7 50.9 %copy-start.3 = (bf16[192,768]{1,0:T(8,128)(2,1)S(1)}, bf16[192,768]{1,0:T(8,128)(2,1)}, u32[]{:S(2)}) copy-start(bf16[192,768]{1,0:T(8,128)(2,1)} %constant.68.clone.w_ref) | copy-start | bytes 884740
  1.7 50.8 %copy-start.4 = (bf16[512,256]{1,0:T(8,128)(2,1)S(1)}, bf16[512,256]{1,0:T(8,128)(2,1)}, u32[]{:S(2)}) copy-start(bf16[512,256]{1,0:T(8,128)(2,1)} %constant.66.clone.d_ref) | copy-start | bytes 786436
  2.7 49.8 %all-to-all-start = ((bf16[32,8,1152]{2,1,0:T(8,128)(2,1)}), bf16[32,8,1152]{2,1,0:T(8,128)(2,1)S(1)}, u32[]{:S(2)}, u32[]{:S(2)}) async-start(bf16[32,8,1152]{2,1,0:T(8,128)(2,1)} %bitcast), calls=%async_computation | async-start | bytes 1179648 | tf_op jit(solution)/shard_map/all_to_all | solution.py:276
  18.9 36.4 %collective-permute-start = (bf16[45,256]{1,0:T(8,128)(2,1)S(1)}, bf16[45,256]{1,0:T(8,128)(2,1)S(1)}, u32[]{:S(2)}, u32[]{:S(2)}) collective-permute-start(bf16[45,256]{1,0:T(8,128)(2,1)S(1)} %get-tuple-element.39), channel_id=1, source_target_pairs={{0,32},{32,64},{64,96},{96,128},{128,160},{160,192},{192,224},{224... | collective-permute-start | bytes 69128 | tf_op jit(solution)/shard_map/ppermute | solution.py:279
  35.2 20.1 %collective-permute-start.1 = (bf16[45,256]{1,0:T(8,128)(2,1)S(1)}, bf16[45,256]{1,0:T(8,128)(2,1)S(1)}, u32[]{:S(2)}, u32[]{:S(2)}) collective-permute-start(bf16[45,256]{1,0:T(8,128)(2,1)S(1)} %get-tuple-element.38), channel_id=1, source_target_pairs={{0,992},{32,0},{64,32},{96,64},{128,96},{160,128},{192,160},{224,1... | collective-permute-start | bytes 69128 | tf_op jit(solution)/shard_map/ppermute | solution.py:280
  38.1 17.2 %collective-permute-start.2 = (bf16[22,256]{1,0:T(8,128)(2,1)S(1)}, bf16[22,256]{1,0:T(8,128)(2,1)S(1)}, u32[]{:S(2)}, u32[]{:S(2)}) collective-permute-start(bf16[22,256]{1,0:T(8,128)(2,1)S(1)} %bitcast.178), channel_id=1, source_target_pairs={{0,1},{1,2},{2,3},{3,4},{4,5},{5,6},{6,7},{7,8},{8,9},{9,10},{10,1... | collective-permute-start | bytes 33800 | tf_op jit(solution)/shard_map/ppermute | solution.py:281
  41.5 13.8 %collective-permute-start.3 = (bf16[22,256]{1,0:T(8,128)(2,1)S(1)}, bf16[22,256]{1,0:T(8,128)(2,1)S(1)}, u32[]{:S(2)}, u32[]{:S(2)}) collective-permute-start(bf16[22,256]{1,0:T(8,128)(2,1)S(1)} %bitcast.179), channel_id=1, source_target_pairs={{0,31},{1,0},{2,1},{3,2},{4,3},{5,4},{6,5},{7,6},{8,7},{9,8},{10,9... | collective-permute-start | bytes 33800 | tf_op jit(solution)/shard_map/ppermute | solution.py:282
  52.6 2.8 %copy-start.10 = (bf16[22,45,256]{2,1,0:T(8,128)(2,1)S(1)}, bf16[22,45,256]{2,1,0:T(8,128)(2,1)}, u32[]{:S(2)}) copy-start(bf16[22,45,256]{2,1,0:T(8,128)(2,1)} %param.12) | copy-start | bytes 1520644
  57.8 27.5 %collective-permute-start.4 = (f32[768,128]{1,0:T(8,128)S(1)}, f32[768,128]{1,0:T(8,128)S(1)}, u32[]{:S(2)}, u32[]{:S(2)}) collective-permute-start(f32[768,128]{1,0:T(8,128)S(1)} %slice_select_fusion.3), channel_id=1, source_target_pairs={{0,32},{32,0},{1,33},{33,1},{2,34},{34,2},{3,35},{35,3},{4,36},{36... | collective-permute-start | bytes 1179656 | tf_op jit(solution)/shard_map/ppermute | solution.py:295
  61.6 60.5 %all-to-all-start.1 = ((bf16[32,40,128]{2,1,0:T(8,128)(2,1)}), bf16[32,40,128]{2,1,0:T(8,128)(2,1)S(1)}, u32[]{:S(2)}, u32[]{:S(2)}) async-start(bf16[32,40,128]{2,1,0:T(8,128)(2,1)} %fourier_chunks.1), calls=%async_computation.1 | async-start | bytes 655360 | tf_op jit(solution)/shard_map/all_to_all | solution.py:286
  85.3 6.1 %collective-permute-start.5 = (bf16[2,2,2,2,24,128]{5,4,3,2,1,0:T(8,128)(2,1)S(1)}, bf16[2,2,2,2,24,128]{5,4,3,2,1,0:T(8,128)(2,1)S(1)}, u32[]{:S(2)}, u32[]{:S(2)}) collective-permute-start(bf16[2,2,2,2,24,128]{5,4,3,2,1,0:T(8,128)(2,1)S(1)} %fusion.42), channel_id=1, source_target_pairs={{0,8},{8,0},{16,24},{24,16},{1,9},{9,1},{17,25},{25,17},{2,10},{10... | collective-permute-start | bytes 294920 | tf_op jit(solution)/shard_map/ppermute | solution.py:46
  91.4 30.9 %copy-start.5 = (bf16[384,12,2,8]{0,3,2,1:T(8,128)(2,1)S(1)}, bf16[384,12,2,8]{0,3,2,1:T(8,128)(2,1)}, u32[]{:S(2)}) copy-start(bf16[384,12,2,8]{0,3,2,1:T(8,128)(2,1)} %param.14) | copy-start | bytes 442372
  91.5 30.9 %copy-start.7 = (f32[384,8]{0,1:T(8,128)S(1)}, f32[384,8]{0,1:T(8,128)}, u32[]{:S(2)}) copy-start(f32[384,8]{0,1:T(8,128)} %param.15) | copy-start | bytes 36868
  91.5 6.8 %collective-permute-start.6 = (bf16[2,2,2,24,128]{4,3,2,1,0:T(8,128)(2,1)S(1)}, bf16[2,2,2,24,128]{4,3,2,1,0:T(8,128)(2,1)S(1)}, u32[]{:S(2)}, u32[]{:S(2)}) collective-permute-start(bf16[2,2,2,24,128]{4,3,2,1,0:T(8,128)(2,1)S(1)} %fusion.43), channel_id=1, source_target_pairs={{0,16},{8,24},{16,0},{24,8},{1,17},{9,25},{17,1},{25,9},{2,18},{10... | collective-permute-start | bytes 147464 | tf_op jit(solution)/shard_map/ppermute | solution.py:46
  98.3 12.2 %collective-permute-start.7 = (bf16[2,2,24,128]{3,2,1,0:T(8,128)(2,1)S(1)}, bf16[2,2,24,128]{3,2,1,0:T(8,128)(2,1)S(1)}, u32[]{:S(2)}, u32[]{:S(2)}) collective-permute-start(bf16[2,2,24,128]{3,2,1,0:T(8,128)(2,1)S(1)} %fusion.46), channel_id=1, source_target_pairs={{0,1},{1,0},{2,3},{3,2},{4,5},{5,4},{6,7},{7,6},{8,9},{9,8},{10,11... | collective-permute-start | bytes 73736 | tf_op jit(solution)/shard_map/ppermute | solution.py:46
  110.5 6.6 %collective-permute-start.8 = (bf16[2,24,128]{2,1,0:T(8,128)(2,1)S(1)}, bf16[2,24,128]{2,1,0:T(8,128)(2,1)S(1)}, u32[]{:S(2)}, u32[]{:S(2)}) collective-permute-start(bf16[2,24,128]{2,1,0:T(8,128)(2,1)S(1)} %fusion.49), channel_id=1, source_target_pairs={{0,2},{1,3},{2,0},{3,1},{4,6},{5,7},{6,4},{7,5},{8,10},{9,11},{10,... | collective-permute-start | bytes 36872 | tf_op jit(solution)/shard_map/ppermute | solution.py:46
  126.9 13.7 %collective-permute-start.9 = (bf16[24,128]{1,0:T(8,128)(2,1)S(1)}, bf16[24,128]{1,0:T(8,128)(2,1)S(1)}, u32[]{:S(2)}, u32[]{:S(2)}) collective-permute-start(bf16[24,128]{1,0:T(8,128)(2,1)S(1)} %fusion.52), channel_id=1, source_target_pairs={{0,4},{1,5},{2,6},{3,7},{4,0},{5,1},{6,2},{7,3},{8,12},{9,13},{10,... | collective-permute-start | bytes 18440 | tf_op jit(solution)/shard_map/ppermute | solution.py:46
  141.4 10.1 %all-to-all-start.2 = ((f32[8,48,128]{2,1,0:T(8,128)}), f32[8,48,128]{2,1,0:T(8,128)S(1)}, u32[]{:S(2)}, u32[]{:S(2)}) async-start(f32[8,48,128]{2,1,0:T(8,128)} %broadcast_in_dim.137), calls=%async_computation.2 | async-start | bytes 393216 | tf_op jit(solution)/shard_map/all_to_all | solution.py:34
  152.2 37.3 %all-to-all-start.3 = ((f32[4,48,128]{2,1,0:T(8,128)}), f32[4,48,128]{2,1,0:T(8,128)S(1)}, u32[]{:S(2)}, u32[]{:S(2)}) async-start(f32[4,48,128]{2,1,0:T(8,128)} %broadcast_in_dim.138), calls=%async_computation.3 | async-start | bytes 196608 | tf_op jit(solution)/shard_map/all_to_all | solution.py:34
  167.5 17.2 %collective-permute-start.10 = (bf16[24,256]{1,0:T(8,128)(2,1)S(1)}, bf16[24,256]{1,0:T(8,128)(2,1)S(1)}, u32[]{:S(2)}, u32[]{:S(2)}) collective-permute-start(bf16[24,256]{1,0:T(8,128)(2,1)S(1)} %get-tuple-element.25), channel_id=1, source_target_pairs={{0,1},{1,2},{2,3},{3,4},{4,5},{5,6},{6,7},{7,8},{8,9},{9,10},{10,1... | collective-permute-start | bytes 36872 | tf_op jit(solution)/shard_map/ppermute | solution.py:318
  169.5 15.3 %collective-permute-start.11 = (bf16[24,256]{1,0:T(8,128)(2,1)S(1)}, bf16[24,256]{1,0:T(8,128)(2,1)S(1)}, u32[]{:S(2)}, u32[]{:S(2)}) collective-permute-start(bf16[24,256]{1,0:T(8,128)(2,1)S(1)} %get-tuple-element.26), channel_id=1, source_target_pairs={{0,31},{1,0},{2,1},{3,2},{4,3},{5,4},{6,5},{7,6},{8,7},{9,8},{10,9... | collective-permute-start | bytes 36872 | tf_op jit(solution)/shard_map/ppermute | solution.py:319
  191.0 5.8 %copy-start.6 = (bf16[3,256,256]{2,1,0:T(8,128)(2,1)S(1)}, bf16[3,256,256]{2,1,0:T(8,128)(2,1)}, u32[]{:S(2)}) copy-start(bf16[3,256,256]{2,1,0:T(8,128)(2,1)} %param.18) | copy-start | bytes 1179652
  191.9 14.6 %all-to-all-start.4 = ((bf16[8,24,128]{2,1,0:T(8,128)(2,1)}), bf16[8,24,128]{2,1,0:T(8,128)(2,1)S(1)}, u32[]{:S(2)}, u32[]{:S(2)}) async-start(bf16[8,24,128]{2,1,0:T(8,128)(2,1)} %broadcast_in_dim.141), calls=%async_computation.4 | async-start | bytes 98304 | tf_op jit(solution)/shard_map/all_to_all | solution.py:34
  207.3 17.2 %all-to-all-start.5 = ((bf16[8,192,128]{2,1,0:T(8,128)(2,1)}), bf16[8,192,128]{2,1,0:T(8,128)(2,1)S(1)}, u32[]{:S(2)}, u32[]{:S(2)}) async-start(bf16[8,192,128]{2,1,0:T(8,128)(2,1)} %broadcast_in_dim.142), calls=%async_computation.5 | async-start | bytes 786432 | tf_op jit(solution)/shard_map/all_to_all | solution.py:34

commit v6 on v5

--- a/solution.py
+++ b/solution.py
@@ -244,10 +244,9 @@
     return jnp.concatenate(partials, axis=0)
 
 
-def input_part(grad_rows, before, after, taps, tap_weight):
-    rows, lons, channels = grad_rows.shape
-    rows -= 2
-    wide = jnp.concatenate([before[:, None], grad_rows, after[:, None]], axis=1)
+def input_part(wide, taps, tap_weight):
+    rows, lons, channels = wide.shape
+    rows, lons = rows - 2, lons - 2
     total = jnp.zeros((rows * lons, channels), F32)
     for index, (first, weight, shift) in enumerate(taps):
         source = wide[first : first + rows]
@@ -275,19 +274,22 @@
     sent = channels_first(grad_out).reshape(lon, chans, -1)
     rows = lax.all_to_all(sent, LON, 0, 0)
 
+    column = [jnp.concatenate([block_input[:, i], grad_out[:, i]], axis=0) for i in (0, -1)]
+    before = lax.ppermute(column[1], LON, ring(lon, 1))
+    after = lax.ppermute(column[0], LON, ring(lon, -1))
+    before, after = before.reshape(2, rows_here, channels), after.reshape(2, rows_here, channels)
+    wide = jnp.concatenate([before[1][:, None], grad_out, after[1][:, None]], axis=1)
     halos = (
-        lax.ppermute(grad_out[-1], LAT, ring(lat, 1)),
-        lax.ppermute(grad_out[0], LAT, ring(lat, -1)),
-        lax.ppermute(block_input[:, -1], LON, ring(lon, 1)),
-        lax.ppermute(block_input[:, 0], LON, ring(lon, -1)),
+        lax.ppermute(wide[-1], LAT, ring(lat, 1)),
+        lax.ppermute(wide[0], LAT, ring(lat, -1)),
     )
     blocks = fourier_chunks(rows, rows_here, lons_here, orders, lat)
-    blocks, (above, below, before, after) = lax.optimization_barrier((blocks, halos))
+    blocks, (above, below) = lax.optimization_barrier((blocks, halos))
     columns = lax.all_to_all(blocks, LAT, 0, 0)
 
-    grad_rows = jnp.concatenate([above[None], grad_out, below[None]], axis=0)
+    wide = jnp.concatenate([above[None], wide, below[None]], axis=0)
     taps = tap_rows(cycle_weight, cycle_shift, rows_here)
-    part = taps_part(grad_rows, block_input, before, after, taps)
+    part = taps_part(wide[:, 1:-1], block_input, before[0], after[0], taps)
     part = part / math.sqrt(rows_here * lat * lons_here * lon)
 
     left, right = part[:, : channels // 2], part[:, channels // 2 :]
@@ -296,7 +298,6 @@
     mine = mine.reshape(2, 2, 2, 2, 2, -1, mine.shape[1])
     mine = halve(halve(mine, "y", 1, 1), "y", 2, 0)
     mine = halve(halve(mine, "z_lo", 1, 2), "z_lo", 2, 1)
-    columns, mine = lax.optimization_barrier((columns, mine))
     chunk = halve(mine, "z_lo", 4, 0)
     high, width = chunk.shape
 
@@ -313,18 +314,11 @@
     cores = jnp.sum(both.reshape(-1, 2, *both.shape[1:]), axis=0)
     chunk = jnp.where(core == 0, cores[0, :high], cores[1, :high])
     both = jnp.concatenate([chunk, cores[0, high:] + cores[1, high:]], axis=0)
-    both, edges = lax.optimization_barrier((both, (grad_rows[:, -1], grad_rows[:, 0])))
-    edges = (
-        lax.ppermute(edges[0], LON, ring(lon, 1)),
-        lax.ppermute(edges[1], LON, ring(lon, -1)),
-    )
-    both = to_all(both, "z_hi")
-    both, (before, after) = lax.optimization_barrier((both, edges))
-    both = jnp.sum(both, axis=0)
+    both = jnp.sum(to_all(both, "z_hi"), axis=0)
     filter_grad = both[high:].reshape(pieces, chans, width).transpose(0, 2, 1)
     filter_grad = filter_grad.reshape(degrees, chans)
 
-    input_grad = input_part(grad_rows, before, after, taps, tap_weight)
+    input_grad = input_part(wide, taps, tap_weight)
 
     mine = to_all(both[:high].astype(BF16), "z_lo").reshape(-1, width)
     mine = to_all(mine, ("core", "y")).reshape(2, -1, width)

time: 227 us -> 232 us (1.022)
  starting transfers between devices: 146 us -> 114 us
  waiting for transfers between devices: 56.5 us -> 76.3 us
  blocking collectives: 0 us -> 12.6 us
  matrix products: 7.74 us -> 10.4 us
    ppermute x6 -> x4, waiting for transfers between devices: 3.18 us -> 17.8 us  [the longest x1 11.1 us: on_device(): before = lax.ppermute(column[1], LON, ring(lon, 1))]
    all_to_all x0 -> x1, blocking collectives: none -> 12.6 us  [to_all(): lax.all_to_all(jnp.broadcast_to(value, (count, *value.shape)), axes, 0, 0)]
    ppermute x6 -> x4, starting transfers between devices: 46.3 us -> 33.8 us  [the longest x1 18 us: on_device(): lax.ppermute(wide[-1], LAT, ring(lat, 1))]
    ppermute x5, starting transfers between devices: 22.2 us -> 12.5 us  [halve(): lax.ppermute(sent.astype(BF16), axis, pairs(lax.axis_size(axis), bit))]
    all_to_all x1, starting transfers between devices: 23.6 us -> 14.4 us  [on_device(): columns = lax.all_to_all(blocks, LAT, 0, 0)]
    all_to_all x4 -> x3, waiting for transfers between devices: 25.3 us -> 33.4 us  [to_all(): lax.all_to_all(jnp.broadcast_to(value, (count, *value.shape)), axes, 0, 0)]
    all_to_all x1, waiting for transfers between devices: 5.01 us -> 0.01 us  [on_device(): columns = lax.all_to_all(blocks, LAT, 0, 0)]
    all_to_all x4 -> x3, starting transfers between devices: 33.8 us -> 35.1 us  [to_all(): lax.all_to_all(jnp.broadcast_to(value, (count, *value.shape)), axes, 0, 0)]
  transfers between devices with their start and end apart: 18 -> 15, of which waited for: 11 -> 10; matrix products, arithmetic and copies ran while one was open for 2% -> 4% of each run, Pallas kernels for 1% -> 1%
where the time goes in v6:
time: 232 us; the launch traced here: 231 us
  starting transfers between devices  114 us (49%)
  waiting for transfers between devices  76.3 us (33%)
  blocking collectives  12.6 us (5%)
  matrix products  10.4 us (4%)
  local copies, waits for them, and re-layouts  7.75 us (3%)
  other arithmetic  4.28 us (2%)
  Pallas kernels  3.98 us (2%)
    all_to_all x3, starting transfers between devices, to_all(): lax.all_to_all(jnp.broadcast_to(value, (count, *value.shape)), axes, 0, 0)  35.1 us
    all_to_all x3, waiting for transfers between devices, to_all(): lax.all_to_all(jnp.broadcast_to(value, (count, *value.shape)), axes, 0, 0)  33.4 us
    ppermute x5, waiting for transfers between devices, halve(): lax.ppermute(sent.astype(BF16), axis, pairs(lax.axis_size(axis), bit))  25.1 us
    ppermute x1, starting transfers between devices, on_device(): lax.ppermute(wide[-1], LAT, ring(lat, 1))  18 us
    all_to_all x1, starting transfers between devices, on_device(): rows = lax.all_to_all(sent, LON, 0, 0)  16.2 us
    all_to_all x1, starting transfers between devices, on_device(): columns = lax.all_to_all(blocks, LAT, 0, 0)  14.4 us
    all_to_all x1, blocking collectives, to_all(): lax.all_to_all(jnp.broadcast_to(value, (count, *value.shape)), axes, 0, 0)  12.6 us
    ppermute x5, starting transfers between devices, halve(): lax.ppermute(sent.astype(BF16), axis, pairs(lax.axis_size(axis), bit))  12.5 us
  transfers between devices with their start and end apart: 15, of which 10 were waited for; matrix products, arithmetic and copies ran while one was open for 4% of the time, Pallas kernels for 1%

profile of v6, /device:TPU:1, one launch (start us, length us, event | category | flops | bytes accessed | tf_op | source)
XLA Modules:
  0.0 230.6 jit_solution(3896201098295009828)
XLA Ops:
  0.6 1.0 copy-done
  1.7 1.0 channels_first.1
  2.7 16.2 %all-to-all-start = ((bf16[32,8,1152]{2,1,0:T(8,128)(2,1)}), bf16[32,8,1152]{2,1,0:T(8,128)(2,1)S(1)}, u32[]{:S(2)}, u32[]{:S(2)}) async-start(bf16[32,8,1152]{2,1,0:T(8,128)(2,1)} %bitcast), calls=%async_computation | async-start | bytes 1179648 | tf_op jit(solution)/shard_map/all_to_all | solution.py:275
  19.0 1.0 fusion.63
  20.0 11.9 %collective-permute-start.1 = (bf16[44,256]{1,0:T(8,128)(2,1)S(1)}, bf16[44,256]{1,0:T(8,128)(2,1)S(1)}, u32[]{:S(2)}, u32[]{:S(2)}) collective-permute-start(bf16[44,256]{1,0:T(8,128)(2,1)S(1)} %pad_maximum_fusion.14), channel_id=1, source_target_pairs={{0,31},{1,0},{2,1},{3,2},{4,3},{5,4},{6,5},{7,6},{8,7},{9,8},{10,9... | collective-permute-start | bytes 67592 | tf_op jit(solution)/shard_map/ppermute | solution.py:279
  32.0 1.9 collective-permute-start
  34.0 0.1 pad_dynamic-slice_fusion.2
  34.1 0.1 pad_dynamic-slice_fusion.5
  34.2 0.0 copy-start.11
  34.3 11.1 %collective-permute-done = bf16[44,256]{1,0:T(8,128)(2,1)S(1)} collective-permute-done((bf16[44,256]{1,0:T(8,128)(2,1)S(1)}, bf16[44,256]{1,0:T(8,128)(2,1)S(1)}, u32[]{:S(2)}, u32[]{:S(2)}) %collective-permute-start) | collective-permute-done | bytes 22560 | tf_op jit(solution)/shard_map/ppermute | solution.py:278
  45.5 18.0 %collective-permute-start.2 = (bf16[47,256]{1,0:T(8,128)(2,1)S(1)}, bf16[47,256]{1,0:T(8,128)(2,1)S(1)}, u32[]{:S(2)}, u32[]{:S(2)}) collective-permute-start(bf16[47,256]{1,0:T(8,128)(2,1)S(1)} %get-tuple-element.13), channel_id=1, source_target_pairs={{0,32},{32,64},{64,96},{96,128},{128,160},{160,192},{192,224},{224... | collective-permute-start | bytes 72200 | tf_op jit(solution)/shard_map/ppermute | solution.py:283
  63.5 1.9 collective-permute-start.3
  65.4 0.0 copy-start.2
  65.5 0.0 copy-start.3
  65.5 0.0 copy-start.4
  65.5 2.3 %convolution_bitcast_fusion.2 = f32[256,256]{1,0:T(8,128)S(1)} fusion(bf16[22,45,256]{2,1,0:T(8,128)(2,1)S(1)} %copy-done.1, f32[22]{0:T(128)S(1)} %get-tuple-element.54, bf16[22,45,256]{2,1,0:T(8,128)(2,1)} %param.12, pred[22]{0:T(512)(128)(4,1)S(1)} %get-tuple-element.50, pred[22]{0:T(512)(128)(4,1)S(1)} %get-tuple-element.51, ...), kind=kOutput, calls=%fused_computation.5 | convolution fusion | flops 133309440 | bytes 1298586 | tf_op jit(solution)/shard_map/dot_general | solution.py:237
  67.9 2.7 %fourier_chunks.1 = bf16[32,40,128]{2,1,0:T(8,128)(2,1)} custom-call(bf16[256,1152]{1,0:T(8,128)(2,1)S(1)} %bitcast.162, bf16[512,256]{1,0:T(8,128)(2,1)S(1)} %copy-done.4, f32[2,256,384]{2,1,0:T(8,128)S(1)} %copy-done.2, bf16[192,768]{1,0:T(8,128)(2,1)S(1)} %copy-done.3), custom_call_target="tpu_custom_call" | custom-call | flops 528482304 | bytes 1703936 | tf_op jit(solution)/shard_map/fourier_chunks/pallas_call | solution.py:146
  70.6 6.7 %collective-permute-done.3 = bf16[47,256]{1,0:T(8,128)(2,1)S(1)} collective-permute-done((bf16[47,256]{1,0:T(8,128)(2,1)S(1)}, bf16[47,256]{1,0:T(8,128)(2,1)S(1)}, u32[]{:S(2)}, u32[]{:S(2)}) %collective-permute-start.3) | collective-permute-done | bytes 24096 | tf_op jit(solution)/shard_map/ppermute | solution.py:284
  77.3 0.4 pad_maximum_fusion
  77.8 0.8 convolution_bitcast_fusion.1
  78.6 0.8 convolution_bitcast_fusion.3
  79.4 0.1 maximum_multiply_fusion
  79.5 1.9 collective-permute-start.4
  81.5 14.4 %all-to-all-start.1 = ((bf16[32,40,128]{2,1,0:T(8,128)(2,1)}), bf16[32,40,128]{2,1,0:T(8,128)(2,1)S(1)}, u32[]{:S(2)}, u32[]{:S(2)}) async-start(bf16[32,40,128]{2,1,0:T(8,128)(2,1)} %fourier_chunks.1), calls=%async_computation.1 | async-start | bytes 655360 | tf_op jit(solution)/shard_map/all_to_all | solution.py:288
  95.9 1.1 select_add_fusion
  97.0 1.9 collective-permute-start.5
  98.9 0.0 copy-start.5
  98.9 0.0 copy-start.7
  99.0 4.1 %collective-permute-done.5 = bf16[2,2,2,2,24,128]{5,4,3,2,1,0:T(8,128)(2,1)S(1)} collective-permute-done((bf16[2,2,2,2,24,128]{5,4,3,2,1,0:T(8,128)(2,1)S(1)}, bf16[2,2,2,2,24,128]{5,4,3,2,1,0:T(8,128)(2,1)S(1)}, u32[]{:S(2)}, u32[]{:S(2)}) %collective-permute-start.5) | collective-permute-done | bytes 98336 | tf_op jit(solution)/shard_map/ppermute | solution.py:46
  103.1 1.9 collective-permute-start.6
  105.0 4.7 %collective-permute-done.6 = bf16[2,2,2,24,128]{4,3,2,1,0:T(8,128)(2,1)S(1)} collective-permute-done((bf16[2,2,2,24,128]{4,3,2,1,0:T(8,128)(2,1)S(1)}, bf16[2,2,2,24,128]{4,3,2,1,0:T(8,128)(2,1)S(1)}, u32[]{:S(2)}, u32[]{:S(2)}) %collective-permute-start.6) | collective-permute-done | bytes 49184 | tf_op jit(solution)/shard_map/ppermute | solution.py:46
  109.8 1.9 collective-permute-start.7
  111.7 9.0 %collective-permute-done.7 = bf16[2,2,24,128]{3,2,1,0:T(8,128)(2,1)S(1)} collective-permute-done((bf16[2,2,24,128]{3,2,1,0:T(8,128)(2,1)S(1)}, bf16[2,2,24,128]{3,2,1,0:T(8,128)(2,1)S(1)}, u32[]{:S(2)}, u32[]{:S(2)}) %collective-permute-start.7) | collective-permute-done | bytes 24608 | tf_op jit(solution)/shard_map/ppermute | solution.py:46
  120.7 2.7 %collective-permute-start.8 = (bf16[2,24,128]{2,1,0:T(8,128)(2,1)S(1)}, bf16[2,24,128]{2,1,0:T(8,128)(2,1)S(1)}, u32[]{:S(2)}, u32[]{:S(2)}) collective-permute-start(bf16[2,24,128]{2,1,0:T(8,128)(2,1)S(1)} %fusion.53), channel_id=1, source_target_pairs={{0,2},{1,3},{2,0},{3,1},{4,6},{5,7},{6,4},{7,5},{8,10},{9,11},{10,... | collective-permute-start | bytes 36872 | tf_op jit(solution)/shard_map/ppermute | solution.py:46
  123.5 3.0 %collective-permute-done.8 = bf16[2,24,128]{2,1,0:T(8,128)(2,1)S(1)} collective-permute-done((bf16[2,24,128]{2,1,0:T(8,128)(2,1)S(1)}, bf16[2,24,128]{2,1,0:T(8,128)(2,1)S(1)}, u32[]{:S(2)}, u32[]{:S(2)}) %collective-permute-start.8) | collective-permute-done | bytes 12320 | tf_op jit(solution)/shard_map/ppermute | solution.py:46
  126.4 4.0 %collective-permute-start.9 = (bf16[24,128]{1,0:T(8,128)(2,1)S(1)}, bf16[24,128]{1,0:T(8,128)(2,1)S(1)}, u32[]{:S(2)}, u32[]{:S(2)}) collective-permute-start(bf16[24,128]{1,0:T(8,128)(2,1)S(1)} %fusion.56), channel_id=1, source_target_pairs={{0,4},{1,5},{2,6},{3,7},{4,0},{5,1},{6,2},{7,3},{8,12},{9,13},{10,... | collective-permute-start | bytes 18440 | tf_op jit(solution)/shard_map/ppermute | solution.py:46
  130.4 4.3 %collective-permute-done.9 = bf16[24,128]{1,0:T(8,128)(2,1)S(1)} collective-permute-done((bf16[24,128]{1,0:T(8,128)(2,1)S(1)}, bf16[24,128]{1,0:T(8,128)(2,1)S(1)}, u32[]{:S(2)}, u32[]{:S(2)}) %collective-permute-start.9) | collective-permute-done | bytes 6176 | tf_op jit(solution)/shard_map/ppermute | solution.py:46
  134.8 0.2 unfold.1
  135.0 4.5 %fusion.31 = (f32[8,384]{1,0:T(8,128)S(1)}, bf16[384,12,2,8]{0,3,2,1:T(8,128)(2,1)}) fusion(bf16[384,12,2,8]{0,3,2,1:T(8,128)(2,1)S(1)} %copy-done.5, f32[8,384]{1,0:T(8,128)S(1)} %bitcast.168, bf16[12,16,704]{2,1,0:T(8,128)(2,1)S(1)} %unfold.1, bf16[12,384,704]{1,2,0:T(8,128)(2,1)} %param.13), kind=kOutput, calls=%fused_computation.56 | convolution fusion | flops 104174592 | bytes 7077888 | tf_op jit(solution)/shard_map/mla,mxa->mxl/dot_general | solution.py:305
  139.6 12.6 %all_to_all.30 = f32[8,48,128]{2,1,0:T(8,128)S(1)} all-to-all(f32[8,48,128]{2,1,0:T(8,128)S(1)} %broadcast_in_dim.123), channel_id=1, replica_groups=mesh['x'=4,'z_hi'=4,'core'=2,'y'=4,'z_lo'=8] {'x','core'}, dimensions={0} | all-to-all | bytes 393216 | tf_op jit(solution)/shard_map/all_to_all | solution.py:34
  152.3 0.6 broadcast_in_dim.124
  152.9 18.8 %all-to-all-start.3 = ((f32[4,48,128]{2,1,0:T(8,128)}), f32[4,48,128]{2,1,0:T(8,128)S(1)}, u32[]{:S(2)}, u32[]{:S(2)}) async-start(f32[4,48,128]{2,1,0:T(8,128)} %broadcast_in_dim.124), calls=%async_computation.3 | async-start | bytes 196608 | tf_op jit(solution)/shard_map/all_to_all | solution.py:34
  171.7 0.6 multiply_convert_fusion.1
  172.3 0.2 reshape.172
  172.4 0.5 multiply_convert_fusion.2
  172.9 0.2 reshape.171
  173.1 0.0 copy-start.12
  173.1 1.2 fusion.40
  174.4 19.0 %all-to-all-done.3 = f32[4,48,128]{2,1,0:T(8,128)S(1)} async-done(((f32[4,48,128]{2,1,0:T(8,128)}), f32[4,48,128]{2,1,0:T(8,128)S(1)}, u32[]{:S(2)}, u32[]{:S(2)}) %all-to-all-start.3) | async-done | bytes 98336 | tf_op jit(solution)/shard_map/all_to_all | solution.py:34
  193.3 0.6 broadcast_in_dim.125
  194.0 6.5 %all-to-all-start.4 = ((bf16[8,24,128]{2,1,0:T(8,128)(2,1)}), bf16[8,24,128]{2,1,0:T(8,128)(2,1)}, u32[]{:S(2)}, u32[]{:S(2)}) async-start(bf16[8,24,128]{2,1,0:T(8,128)(2,1)} %broadcast_in_dim.125), calls=%async_computation.4 | async-start | bytes 98304 | tf_op jit(solution)/shard_map/all_to_all | solution.py:34
  200.6 0.0 copy-start.6
  200.6 0.5 multiply_convert_fusion
  201.1 0.2 reshape.173
  201.2 0.3 copy-done.6
  201.6 0.3 convolution_add_fusion.1
  201.9 8.4 %all-to-all-done.4 = bf16[8,24,128]{2,1,0:T(8,128)(2,1)} async-done(((bf16[8,24,128]{2,1,0:T(8,128)(2,1)}), bf16[8,24,128]{2,1,0:T(8,128)(2,1)}, u32[]{:S(2)}, u32[]{:S(2)}) %all-to-all-start.4) | async-done | bytes 49184 | tf_op jit(solution)/shard_map/all_to_all | solution.py:34
  210.2 1.6 broadcast_in_dim.126
  211.8 9.8 %all-to-all-start.5 = ((bf16[8,192,128]{2,1,0:T(8,128)(2,1)}), bf16[8,192,128]{2,1,0:T(8,128)(2,1)S(1)}, u32[]{:S(2)}, u32[]{:S(2)}) async-start(bf16[8,192,128]{2,1,0:T(8,128)(2,1)} %broadcast_in_dim.126), calls=%async_computation.5 | async-start | bytes 786432 | tf_op jit(solution)/shard_map/all_to_all | solution.py:34
  221.7 0.3 fusion
  222.0 1.0 convert_element_type.134
  223.0 0.6 slice_bitcast_fusion
  223.6 6.1 %all-to-all-done.5 = bf16[8,192,128]{2,1,0:T(8,128)(2,1)S(1)} async-done(((bf16[8,192,128]{2,1,0:T(8,128)(2,1)}), bf16[8,192,128]{2,1,0:T(8,128)(2,1)S(1)}, u32[]{:S(2)}, u32[]{:S(2)}) %all-to-all-start.5) | async-done | bytes 393248 | tf_op jit(solution)/shard_map/all_to_all | solution.py:34
  229.7 0.9 maximum_convert_fusion
  (70 shorter events, 0.6 us)
Async XLA Ops:
  0.6 1.0 copy-start
  1.7 17.3 %copy-start.1 = (bf16[22,45,256]{2,1,0:T(8,128)(2,1)S(1)}, bf16[22,45,256]{2,1,0:T(8,128)(2,1)}, u32[]{:S(2)}) copy-start(bf16[22,45,256]{2,1,0:T(8,128)(2,1)} %x_ref.1) | copy-start | bytes 1520644
  2.7 31.2 %copy-start.8 = (f32[704,3]{0,1:T(4,128)S(1)}, f32[704,3]{0,1:T(4,128)}, u32[]{:S(2)}) copy-start(f32[704,3]{0,1:T(4,128)} %param.16) | copy-start | bytes 25348
  2.7 31.3 %copy-start.9 = (s32[704,3]{0,1:T(4,128)S(1)}, s32[704,3]{0,1:T(4,128)}, u32[]{:S(2)}) copy-start(s32[704,3]{0,1:T(4,128)} %param.17) | copy-start | bytes 25348
  2.7 65.1 %all-to-all-start = ((bf16[32,8,1152]{2,1,0:T(8,128)(2,1)}), bf16[32,8,1152]{2,1,0:T(8,128)(2,1)S(1)}, u32[]{:S(2)}, u32[]{:S(2)}) async-start(bf16[32,8,1152]{2,1,0:T(8,128)(2,1)} %bitcast), calls=%async_computation | async-start | bytes 1179648 | tf_op jit(solution)/shard_map/all_to_all | solution.py:275
  20.0 14.2 %collective-permute-start.1 = (bf16[44,256]{1,0:T(8,128)(2,1)S(1)}, bf16[44,256]{1,0:T(8,128)(2,1)S(1)}, u32[]{:S(2)}, u32[]{:S(2)}) collective-permute-start(bf16[44,256]{1,0:T(8,128)(2,1)S(1)} %pad_maximum_fusion.14), channel_id=1, source_target_pairs={{0,31},{1,0},{2,1},{3,2},{4,3},{5,4},{6,5},{7,6},{8,7},{9,8},{10,9... | collective-permute-start | bytes 67592 | tf_op jit(solution)/shard_map/ppermute | solution.py:279
  32.0 13.4 %collective-permute-start = (bf16[44,256]{1,0:T(8,128)(2,1)S(1)}, bf16[44,256]{1,0:T(8,128)(2,1)S(1)}, u32[]{:S(2)}, u32[]{:S(2)}) collective-permute-start(bf16[44,256]{1,0:T(8,128)(2,1)S(1)} %pad_maximum_fusion.13), channel_id=1, source_target_pairs={{0,1},{1,2},{2,3},{3,4},{4,5},{5,6},{6,7},{7,8},{8,9},{9,10},{10,1... | collective-permute-start | bytes 67592 | tf_op jit(solution)/shard_map/ppermute | solution.py:278
  34.2 43.6 %copy-start.11 = (f32[22]{0:T(128)}, f32[22]{0:T(128)S(1)}, u32[]{:S(2)}) copy-start(f32[22]{0:T(128)S(1)} %get-tuple-element.53) | copy-start | bytes 268
  34.2 43.5 %copy-start.13 = (pred[22]{0:T(512)(128)(4,1)}, pred[22]{0:T(512)(128)(4,1)S(1)}, u32[]{:S(2)}) copy-start(pred[22]{0:T(512)(128)(4,1)S(1)} %get-tuple-element.43) | copy-start | bytes 70
  34.2 43.5 %copy-start.15 = (pred[22]{0:T(512)(128)(4,1)}, pred[22]{0:T(512)(128)(4,1)S(1)}, u32[]{:S(2)}) copy-start(pred[22]{0:T(512)(128)(4,1)S(1)} %get-tuple-element.44) | copy-start | bytes 70
  34.2 43.5 %copy-start.17 = (pred[22]{0:T(512)(128)(4,1)}, pred[22]{0:T(512)(128)(4,1)S(1)}, u32[]{:S(2)}) copy-start(pred[22]{0:T(512)(128)(4,1)S(1)} %get-tuple-element.45) | copy-start | bytes 70
  45.5 25.1 %collective-permute-start.2 = (bf16[47,256]{1,0:T(8,128)(2,1)S(1)}, bf16[47,256]{1,0:T(8,128)(2,1)S(1)}, u32[]{:S(2)}, u32[]{:S(2)}) collective-permute-start(bf16[47,256]{1,0:T(8,128)(2,1)S(1)} %get-tuple-element.13), channel_id=1, source_target_pairs={{0,32},{32,64},{64,96},{96,128},{128,160},{160,192},{192,224},{224... | collective-permute-start | bytes 72200 | tf_op jit(solution)/shard_map/ppermute | solution.py:283
  63.5 13.9 %collective-permute-start.3 = (bf16[47,256]{1,0:T(8,128)(2,1)S(1)}, bf16[47,256]{1,0:T(8,128)(2,1)S(1)}, u32[]{:S(2)}, u32[]{:S(2)}) collective-permute-start(bf16[47,256]{1,0:T(8,128)(2,1)S(1)} %get-tuple-element.12), channel_id=1, source_target_pairs={{0,992},{32,0},{64,32},{96,64},{128,96},{160,128},{192,160},{224,1... | collective-permute-start | bytes 72200 | tf_op jit(solution)/shard_map/ppermute | solution.py:284
  65.4 2.4 %copy-start.2 = (f32[2,256,384]{2,1,0:T(8,128)S(1)}, f32[2,256,384]{2,1,0:T(8,128)}, u32[]{:S(2)}) copy-start(f32[2,256,384]{2,1,0:T(8,128)} %constant.67.clone.tw_ref) | copy-start | bytes 2359300
  65.5 2.4 %copy-start.3 = (bf16[192,768]{1,0:T(8,128)(2,1)S(1)}, bf16[192,768]{1,0:T(8,128)(2,1)}, u32[]{:S(2)}) copy-start(bf16[192,768]{1,0:T(8,128)(2,1)} %constant.68.clone.w_ref) | copy-start | bytes 884740
  65.5 2.4 %copy-start.4 = (bf16[512,256]{1,0:T(8,128)(2,1)S(1)}, bf16[512,256]{1,0:T(8,128)(2,1)}, u32[]{:S(2)}) copy-start(bf16[512,256]{1,0:T(8,128)(2,1)} %constant.66.clone.d_ref) | copy-start | bytes 786436
  70.6 7.2 %copy-start.10 = (bf16[22,45,256]{2,1,0:T(8,128)(2,1)S(1)}, bf16[22,45,256]{2,1,0:T(8,128)(2,1)}, u32[]{:S(2)}) copy-start(bf16[22,45,256]{2,1,0:T(8,128)(2,1)} %param.12) | copy-start | bytes 1520644
  79.5 16.4 %collective-permute-start.4 = (f32[768,128]{1,0:T(8,128)S(1)}, f32[768,128]{1,0:T(8,128)}, u32[]{:S(2)}, u32[]{:S(2)}) collective-permute-start(f32[768,128]{1,0:T(8,128)S(1)} %slice_select_fusion.2), channel_id=1, source_target_pairs={{0,32},{32,0},{1,33},{33,1},{2,34},{34,2},{3,35},{35,3},{4,36},{36... | collective-permute-start | bytes 1179656 | tf_op jit(solution)/shard_map/ppermute | solution.py:297
  81.5 53.3 %all-to-all-start.1 = ((bf16[32,40,128]{2,1,0:T(8,128)(2,1)}), bf16[32,40,128]{2,1,0:T(8,128)(2,1)S(1)}, u32[]{:S(2)}, u32[]{:S(2)}) async-start(bf16[32,40,128]{2,1,0:T(8,128)(2,1)} %fourier_chunks.1), calls=%async_computation.1 | async-start | bytes 655360 | tf_op jit(solution)/shard_map/all_to_all | solution.py:288
  97.0 6.1 %collective-permute-start.5 = (bf16[2,2,2,2,24,128]{5,4,3,2,1,0:T(8,128)(2,1)S(1)}, bf16[2,2,2,2,24,128]{5,4,3,2,1,0:T(8,128)(2,1)S(1)}, u32[]{:S(2)}, u32[]{:S(2)}) collective-permute-start(bf16[2,2,2,2,24,128]{5,4,3,2,1,0:T(8,128)(2,1)S(1)} %fusion.45), channel_id=1, source_target_pairs={{0,8},{8,0},{16,24},{24,16},{1,9},{9,1},{17,25},{25,17},{2,10},{10... | collective-permute-start | bytes 294920 | tf_op jit(solution)/shard_map/ppermute | solution.py:46
  98.9 36.1 %copy-start.5 = (bf16[384,12,2,8]{0,3,2,1:T(8,128)(2,1)S(1)}, bf16[384,12,2,8]{0,3,2,1:T(8,128)(2,1)}, u32[]{:S(2)}) copy-start(bf16[384,12,2,8]{0,3,2,1:T(8,128)(2,1)} %param.14) | copy-start | bytes 442372
  98.9 36.1 %copy-start.7 = (f32[384,8]{0,1:T(8,128)S(1)}, f32[384,8]{0,1:T(8,128)}, u32[]{:S(2)}) copy-start(f32[384,8]{0,1:T(8,128)} %param.15) | copy-start | bytes 36868
  103.1 6.6 %collective-permute-start.6 = (bf16[2,2,2,24,128]{4,3,2,1,0:T(8,128)(2,1)S(1)}, bf16[2,2,2,24,128]{4,3,2,1,0:T(8,128)(2,1)S(1)}, u32[]{:S(2)}, u32[]{:S(2)}) collective-permute-start(bf16[2,2,2,24,128]{4,3,2,1,0:T(8,128)(2,1)S(1)} %fusion.46), channel_id=1, source_target_pairs={{0,16},{8,24},{16,0},{24,8},{1,17},{9,25},{17,1},{25,9},{2,18},{10... | collective-permute-start | bytes 147464 | tf_op jit(solution)/shard_map/ppermute | solution.py:46
  109.8 10.9 %collective-permute-start.7 = (bf16[2,2,24,128]{3,2,1,0:T(8,128)(2,1)S(1)}, bf16[2,2,24,128]{3,2,1,0:T(8,128)(2,1)S(1)}, u32[]{:S(2)}, u32[]{:S(2)}) collective-permute-start(bf16[2,2,24,128]{3,2,1,0:T(8,128)(2,1)S(1)} %fusion.49), channel_id=1, source_target_pairs={{0,1},{1,0},{2,3},{3,2},{4,5},{5,4},{6,7},{7,6},{8,9},{9,8},{10,11... | collective-permute-start | bytes 73736 | tf_op jit(solution)/shard_map/ppermute | solution.py:46
  120.7 5.7 %collective-permute-start.8 = (bf16[2,24,128]{2,1,0:T(8,128)(2,1)S(1)}, bf16[2,24,128]{2,1,0:T(8,128)(2,1)S(1)}, u32[]{:S(2)}, u32[]{:S(2)}) collective-permute-start(bf16[2,24,128]{2,1,0:T(8,128)(2,1)S(1)} %fusion.53), channel_id=1, source_target_pairs={{0,2},{1,3},{2,0},{3,1},{4,6},{5,7},{6,4},{7,5},{8,10},{9,11},{10,... | collective-permute-start | bytes 36872 | tf_op jit(solution)/shard_map/ppermute | solution.py:46
  126.4 8.3 %collective-permute-start.9 = (bf16[24,128]{1,0:T(8,128)(2,1)S(1)}, bf16[24,128]{1,0:T(8,128)(2,1)S(1)}, u32[]{:S(2)}, u32[]{:S(2)}) collective-permute-start(bf16[24,128]{1,0:T(8,128)(2,1)S(1)} %fusion.56), channel_id=1, source_target_pairs={{0,4},{1,5},{2,6},{3,7},{4,0},{5,1},{6,2},{7,3},{8,12},{9,13},{10,... | collective-permute-start | bytes 18440 | tf_op jit(solution)/shard_map/ppermute | solution.py:46
  152.9 40.4 %all-to-all-start.3 = ((f32[4,48,128]{2,1,0:T(8,128)}), f32[4,48,128]{2,1,0:T(8,128)S(1)}, u32[]{:S(2)}, u32[]{:S(2)}) async-start(f32[4,48,128]{2,1,0:T(8,128)} %broadcast_in_dim.124), calls=%async_computation.3 | async-start | bytes 196608 | tf_op jit(solution)/shard_map/all_to_all | solution.py:34
  173.1 27.4 %copy-start.12 = (f32[22]{0:T(128)S(1)}, f32[22]{0:T(128)}, u32[]{:S(2)}) copy-start(f32[22]{0:T(128)} %copy-done.11) | copy-start | bytes 268
  173.1 27.4 %copy-start.14 = (pred[22]{0:T(512)(128)(4,1)S(1)}, pred[22]{0:T(512)(128)(4,1)}, u32[]{:S(2)}) copy-start(pred[22]{0:T(512)(128)(4,1)} %copy-done.13) | copy-start | bytes 70
  173.1 27.4 %copy-start.16 = (pred[22]{0:T(512)(128)(4,1)S(1)}, pred[22]{0:T(512)(128)(4,1)}, u32[]{:S(2)}) copy-start(pred[22]{0:T(512)(128)(4,1)} %copy-done.15) | copy-start | bytes 70
  173.1 27.4 %copy-start.18 = (pred[22]{0:T(512)(128)(4,1)S(1)}, pred[22]{0:T(512)(128)(4,1)}, u32[]{:S(2)}) copy-start(pred[22]{0:T(512)(128)(4,1)} %copy-done.17) | copy-start | bytes 70
  194.0 16.3 %all-to-all-start.4 = ((bf16[8,24,128]{2,1,0:T(8,128)(2,1)}), bf16[8,24,128]{2,1,0:T(8,128)(2,1)}, u32[]{:S(2)}, u32[]{:S(2)}) async-start(bf16[8,24,128]{2,1,0:T(8,128)(2,1)} %broadcast_in_dim.125), calls=%async_computation.4 | async-start | bytes 98304 | tf_op jit(solution)/shard_map/all_to_all | solution.py:34
  200.6 1.0 copy-start.6
  211.8 17.8 %all-to-all-start.5 = ((bf16[8,192,128]{2,1,0:T(8,128)(2,1)}), bf16[8,192,128]{2,1,0:T(8,128)(2,1)S(1)}, u32[]{:S(2)}, u32[]{:S(2)}) async-start(bf16[8,192,128]{2,1,0:T(8,128)(2,1)} %broadcast_in_dim.126), calls=%async_computation.5 | async-start | bytes 786432 | tf_op jit(solution)/shard_map/all_to_all | solution.py:34

commit v7 on v5

--- a/solution.py
+++ b/solution.py
@@ -296,7 +296,6 @@
     mine = mine.reshape(2, 2, 2, 2, 2, -1, mine.shape[1])
     mine = halve(halve(mine, "y", 1, 1), "y", 2, 0)
     mine = halve(halve(mine, "z_lo", 1, 2), "z_lo", 2, 1)
-    columns, mine = lax.optimization_barrier((columns, mine))
     chunk = halve(mine, "z_lo", 4, 0)
     high, width = chunk.shape
 

time: 227 us -> 227 us (level)
  waiting for transfers between devices: 56.5 us -> 53.3 us
  starting transfers between devices: 146 us -> 149 us
    all_to_all x4, starting transfers between devices: 33.8 us -> 44 us  [to_all(): lax.all_to_all(jnp.broadcast_to(value, (count, *value.shape)), axes, 0, 0)]
    ppermute x5, starting transfers between devices: 22.2 us -> 15.1 us  [halve(): lax.ppermute(sent.astype(BF16), axis, pairs(lax.axis_size(axis), bit))]
    all_to_all x1, waiting for transfers between devices: 5.01 us -> 0.01 us  [on_device(): columns = lax.all_to_all(blocks, LAT, 0, 0)]
  transfers between devices with their start and end apart: 18 -> 18, of which waited for: 11 -> 10; matrix products, arithmetic and copies ran while one was open for 2% -> 2% of each run, Pallas kernels for 1% -> 1%
where the time goes in v7:
time: 227 us; the launch traced here: 225 us
  starting transfers between devices  149 us (66%)
  waiting for transfers between devices  53.3 us (23%)
  matrix products  7.74 us (3%)
  local copies, waits for them, and re-layouts  7.22 us (3%)
  Pallas kernels  3.98 us (2%)
  other arithmetic  2.84 us (1%)
    all_to_all x4, starting transfers between devices, to_all(): lax.all_to_all(jnp.broadcast_to(value, (count, *value.shape)), axes, 0, 0)  44 us
    all_to_all x4, waiting for transfers between devices, to_all(): lax.all_to_all(jnp.broadcast_to(value, (count, *value.shape)), axes, 0, 0)  25.3 us
    ppermute x5, waiting for transfers between devices, halve(): lax.ppermute(sent.astype(BF16), axis, pairs(lax.axis_size(axis), bit))  24.8 us
    all_to_all x1, starting transfers between devices, on_device(): columns = lax.all_to_all(blocks, LAT, 0, 0)  23.6 us
    ppermute x1, starting transfers between devices, on_device(): lax.ppermute(grad_out[-1], LAT, ring(lat, 1))  16.3 us
    all_to_all x1, starting transfers between devices, on_device(): rows = lax.all_to_all(sent, LON, 0, 0)  16.1 us
    ppermute x5, starting transfers between devices, halve(): lax.ppermute(sent.astype(BF16), axis, pairs(lax.axis_size(axis), bit))  15.1 us
    ppermute x1, starting transfers between devices, on_device(): lax.ppermute(edges[1], LON, ring(lon, -1))  12.1 us
  transfers between devices with their start and end apart: 18, of which 10 were waited for; matrix products, arithmetic and copies ran while one was open for 2% of the time, Pallas kernels for 1%

profile of v7, /device:TPU:1, one launch (start us, length us, event | category | flops | bytes accessed | tf_op | source)
XLA Modules:
  0.0 225.4 jit_solution(9018306684545438761)
XLA Ops:
  0.6 1.0 copy-done
  1.7 0.0 copy-start.3
  1.7 0.0 copy-start.4
  1.7 1.0 channels_first.1
  2.7 16.1 %all-to-all-start = ((bf16[32,8,1152]{2,1,0:T(8,128)(2,1)}), bf16[32,8,1152]{2,1,0:T(8,128)(2,1)S(1)}, u32[]{:S(2)}, u32[]{:S(2)}) async-start(bf16[32,8,1152]{2,1,0:T(8,128)(2,1)} %bitcast), calls=%async_computation | async-start | bytes 1179648 | tf_op jit(solution)/shard_map/all_to_all | solution.py:276
  18.9 16.3 %collective-permute-start = (bf16[45,256]{1,0:T(8,128)(2,1)S(1)}, bf16[45,256]{1,0:T(8,128)(2,1)S(1)}, u32[]{:S(2)}, u32[]{:S(2)}) collective-permute-start(bf16[45,256]{1,0:T(8,128)(2,1)S(1)} %get-tuple-element.35), channel_id=1, source_target_pairs={{0,32},{32,64},{64,96},{96,128},{128,160},{160,192},{192,224},{224... | collective-permute-start | bytes 69128 | tf_op jit(solution)/shard_map/ppermute | solution.py:279
  35.2 1.9 collective-permute-start.1
  37.1 1.0 fusion.59
  38.1 3.4 %collective-permute-start.2 = (bf16[22,256]{1,0:T(8,128)(2,1)S(1)}, bf16[22,256]{1,0:T(8,128)(2,1)S(1)}, u32[]{:S(2)}, u32[]{:S(2)}) collective-permute-start(bf16[22,256]{1,0:T(8,128)(2,1)S(1)} %bitcast.178), channel_id=1, source_target_pairs={{0,1},{1,2},{2,3},{3,4},{4,5},{5,6},{6,7},{7,8},{8,9},{9,10},{10,1... | collective-permute-start | bytes 33800 | tf_op jit(solution)/shard_map/ppermute | solution.py:281
  41.5 10.7 %collective-permute-start.3 = (bf16[22,256]{1,0:T(8,128)(2,1)S(1)}, bf16[22,256]{1,0:T(8,128)(2,1)S(1)}, u32[]{:S(2)}, u32[]{:S(2)}) collective-permute-start(bf16[22,256]{1,0:T(8,128)(2,1)S(1)} %bitcast.179), channel_id=1, source_target_pairs={{0,31},{1,0},{2,1},{3,2},{4,3},{5,4},{6,5},{7,6},{8,7},{9,8},{10,9... | collective-permute-start | bytes 33800 | tf_op jit(solution)/shard_map/ppermute | solution.py:282
  52.3 0.1 pad_dynamic-slice_fusion.2
  52.4 0.1 pad_dynamic-slice_fusion.5
  52.6 0.0 copy-start.10
  52.6 2.7 %fourier_chunks.1 = bf16[32,40,128]{2,1,0:T(8,128)(2,1)} custom-call(bf16[256,1152]{1,0:T(8,128)(2,1)S(1)} %bitcast.160, bf16[512,256]{1,0:T(8,128)(2,1)S(1)} %copy-done.4, f32[2,256,384]{2,1,0:T(8,128)S(1)} %copy-done.2, bf16[192,768]{1,0:T(8,128)(2,1)S(1)} %copy-done.3), custom_call_target="tpu_custom_call" | custom-call | flops 528482304 | bytes 1703936 | tf_op jit(solution)/shard_map/fourier_chunks/pallas_call | solution.py:146
  55.4 0.7 convolution_bitcast_fusion.2
  56.1 0.7 convolution_bitcast_fusion.1
  56.9 0.7 convolution_bitcast_fusion.3
  57.6 0.1 maximum_multiply_fusion
  57.8 3.8 %collective-permute-start.4 = (f32[768,128]{1,0:T(8,128)S(1)}, f32[768,128]{1,0:T(8,128)S(1)}, u32[]{:S(2)}, u32[]{:S(2)}) collective-permute-start(f32[768,128]{1,0:T(8,128)S(1)} %slice_select_fusion.3), channel_id=1, source_target_pairs={{0,32},{32,0},{1,33},{33,1},{2,34},{34,2},{3,35},{35,3},{4,36},{36... | collective-permute-start | bytes 1179656 | tf_op jit(solution)/shard_map/ppermute | solution.py:295
  61.6 23.6 %all-to-all-start.1 = ((bf16[32,40,128]{2,1,0:T(8,128)(2,1)}), bf16[32,40,128]{2,1,0:T(8,128)(2,1)S(1)}, u32[]{:S(2)}, u32[]{:S(2)}) async-start(bf16[32,40,128]{2,1,0:T(8,128)(2,1)} %fourier_chunks.1), calls=%async_computation.1 | async-start | bytes 655360 | tf_op jit(solution)/shard_map/all_to_all | solution.py:286
  85.3 0.1 select_add_fusion
  85.3 1.9 collective-permute-start.5
  87.3 4.1 %collective-permute-done.5 = bf16[2,2,2,2,24,128]{5,4,3,2,1,0:T(8,128)(2,1)S(1)} collective-permute-done((bf16[2,2,2,2,24,128]{5,4,3,2,1,0:T(8,128)(2,1)S(1)}, bf16[2,2,2,2,24,128]{5,4,3,2,1,0:T(8,128)(2,1)S(1)}, u32[]{:S(2)}, u32[]{:S(2)}) %collective-permute-start.5) | collective-permute-done | bytes 98336 | tf_op jit(solution)/shard_map/ppermute | solution.py:46
  91.4 0.0 copy-start.5
  91.5 0.0 copy-start.7
  91.5 2.5 %collective-permute-start.6 = (bf16[2,2,2,24,128]{4,3,2,1,0:T(8,128)(2,1)S(1)}, bf16[2,2,2,24,128]{4,3,2,1,0:T(8,128)(2,1)S(1)}, u32[]{:S(2)}, u32[]{:S(2)}) collective-permute-start(bf16[2,2,2,24,128]{4,3,2,1,0:T(8,128)(2,1)S(1)} %fusion.43), channel_id=1, source_target_pairs={{0,16},{8,24},{16,0},{24,8},{1,17},{9,25},{17,1},{25,9},{2,18},{10... | collective-permute-start | bytes 147464 | tf_op jit(solution)/shard_map/ppermute | solution.py:46
  94.0 4.2 %collective-permute-done.6 = bf16[2,2,2,24,128]{4,3,2,1,0:T(8,128)(2,1)S(1)} collective-permute-done((bf16[2,2,2,24,128]{4,3,2,1,0:T(8,128)(2,1)S(1)}, bf16[2,2,2,24,128]{4,3,2,1,0:T(8,128)(2,1)S(1)}, u32[]{:S(2)}, u32[]{:S(2)}) %collective-permute-start.6) | collective-permute-done | bytes 49184 | tf_op jit(solution)/shard_map/ppermute | solution.py:46
  98.3 3.1 %collective-permute-start.7 = (bf16[2,2,24,128]{3,2,1,0:T(8,128)(2,1)S(1)}, bf16[2,2,24,128]{3,2,1,0:T(8,128)(2,1)S(1)}, u32[]{:S(2)}, u32[]{:S(2)}) collective-permute-start(bf16[2,2,24,128]{3,2,1,0:T(8,128)(2,1)S(1)} %fusion.46), channel_id=1, source_target_pairs={{0,1},{1,0},{2,3},{3,2},{4,5},{5,4},{6,7},{7,6},{8,9},{9,8},{10,11... | collective-permute-start | bytes 73736 | tf_op jit(solution)/shard_map/ppermute | solution.py:46
  101.4 9.1 %collective-permute-done.7 = bf16[2,2,24,128]{3,2,1,0:T(8,128)(2,1)S(1)} collective-permute-done((bf16[2,2,24,128]{3,2,1,0:T(8,128)(2,1)S(1)}, bf16[2,2,24,128]{3,2,1,0:T(8,128)(2,1)S(1)}, u32[]{:S(2)}, u32[]{:S(2)}) %collective-permute-start.7) | collective-permute-done | bytes 24608 | tf_op jit(solution)/shard_map/ppermute | solution.py:46
  110.5 1.9 collective-permute-start.8
  112.5 4.6 %collective-permute-done.8 = bf16[2,24,128]{2,1,0:T(8,128)(2,1)S(1)} collective-permute-done((bf16[2,24,128]{2,1,0:T(8,128)(2,1)S(1)}, bf16[2,24,128]{2,1,0:T(8,128)(2,1)S(1)}, u32[]{:S(2)}, u32[]{:S(2)}) %collective-permute-start.8) | collective-permute-done | bytes 12320 | tf_op jit(solution)/shard_map/ppermute | solution.py:46
  117.1 5.6 %collective-permute-start.9 = (bf16[24,128]{1,0:T(8,128)(2,1)S(1)}, bf16[24,128]{1,0:T(8,128)(2,1)S(1)}, u32[]{:S(2)}, u32[]{:S(2)}) collective-permute-start(bf16[24,128]{1,0:T(8,128)(2,1)S(1)} %fusion.52), channel_id=1, source_target_pairs={{0,4},{1,5},{2,6},{3,7},{4,0},{5,1},{6,2},{7,3},{8,12},{9,13},{10,... | collective-permute-start | bytes 18440 | tf_op jit(solution)/shard_map/ppermute | solution.py:46
  122.8 0.1 pad_maximum_fusion.13
  122.8 2.8 %collective-permute-done.9 = bf16[24,128]{1,0:T(8,128)(2,1)S(1)} collective-permute-done((bf16[24,128]{1,0:T(8,128)(2,1)S(1)}, bf16[24,128]{1,0:T(8,128)(2,1)S(1)}, u32[]{:S(2)}, u32[]{:S(2)}) %collective-permute-start.9) | collective-permute-done | bytes 6176 | tf_op jit(solution)/shard_map/ppermute | solution.py:46
  125.6 0.2 unfold.1
  125.9 4.5 %fusion.28 = (f32[8,384]{1,0:T(8,128)S(1)}, bf16[384,12,2,8]{0,3,2,1:T(8,128)(2,1)}) fusion(bf16[384,12,2,8]{0,3,2,1:T(8,128)(2,1)S(1)} %copy-done.5, f32[8,384]{1,0:T(8,128)S(1)} %bitcast.175, bf16[12,16,704]{2,1,0:T(8,128)(2,1)S(1)} %unfold.1, bf16[12,384,704]{1,2,0:T(8,128)(2,1)} %param.13), kind=kOutput, calls=%fused_computation.54 | convolution fusion | flops 104174592 | bytes 7077888 | tf_op jit(solution)/shard_map/mla,mxa->mxl/dot_general | solution.py:303
  130.5 0.7 broadcast_in_dim.137
  131.2 6.2 %all-to-all-start.2 = ((f32[8,48,128]{2,1,0:T(8,128)}), f32[8,48,128]{2,1,0:T(8,128)S(1)}, u32[]{:S(2)}, u32[]{:S(2)}) async-start(f32[8,48,128]{2,1,0:T(8,128)} %broadcast_in_dim.137), calls=%async_computation.2 | async-start | bytes 393216 | tf_op jit(solution)/shard_map/all_to_all | solution.py:34
  137.4 5.9 %all-to-all-done.2 = f32[8,48,128]{2,1,0:T(8,128)S(1)} async-done(((f32[8,48,128]{2,1,0:T(8,128)}), f32[8,48,128]{2,1,0:T(8,128)S(1)}, u32[]{:S(2)}, u32[]{:S(2)}) %all-to-all-start.2) | async-done | bytes 196640 | tf_op jit(solution)/shard_map/all_to_all | solution.py:34
  143.3 0.6 broadcast_in_dim.138
  144.0 23.6 %all-to-all-start.3 = ((f32[4,48,128]{2,1,0:T(8,128)}), f32[4,48,128]{2,1,0:T(8,128)S(1)}, u32[]{:S(2)}, u32[]{:S(2)}) async-start(f32[4,48,128]{2,1,0:T(8,128)} %broadcast_in_dim.138), calls=%async_computation.3 | async-start | bytes 196608 | tf_op jit(solution)/shard_map/all_to_all | solution.py:34
  167.6 1.9 collective-permute-start.10
  169.5 12.1 %collective-permute-start.11 = (bf16[24,256]{1,0:T(8,128)(2,1)S(1)}, bf16[24,256]{1,0:T(8,128)(2,1)S(1)}, u32[]{:S(2)}, u32[]{:S(2)}) collective-permute-start(bf16[24,256]{1,0:T(8,128)(2,1)S(1)} %get-tuple-element.22), channel_id=1, source_target_pairs={{0,31},{1,0},{2,1},{3,2},{4,3},{5,4},{6,5},{7,6},{8,7},{9,8},{10,9... | collective-permute-start | bytes 36872 | tf_op jit(solution)/shard_map/ppermute | solution.py:318
  181.6 3.2 %collective-permute-done.10 = bf16[24,256]{1,0:T(8,128)(2,1)S(1)} collective-permute-done((bf16[24,256]{1,0:T(8,128)(2,1)S(1)}, bf16[24,256]{1,0:T(8,128)(2,1)S(1)}, u32[]{:S(2)}, u32[]{:S(2)}) %collective-permute-start.10) | collective-permute-done | bytes 12320 | tf_op jit(solution)/shard_map/ppermute | solution.py:317
  184.7 4.7 %all-to-all-done.3 = f32[4,48,128]{2,1,0:T(8,128)S(1)} async-done(((f32[4,48,128]{2,1,0:T(8,128)}), f32[4,48,128]{2,1,0:T(8,128)S(1)}, u32[]{:S(2)}, u32[]{:S(2)}) %all-to-all-start.3) | async-done | bytes 98336 | tf_op jit(solution)/shard_map/all_to_all | solution.py:34
  189.5 0.4 maximum_maximum_fusion
  189.9 0.4 multiply_convert_fusion.2
  190.3 0.7 multiply_convert_fusion
  191.0 0.0 copy-start.6
  191.1 0.2 reshape.161
  191.2 0.6 broadcast_in_dim.141
  191.9 5.0 %all-to-all-start.4 = ((bf16[8,24,128]{2,1,0:T(8,128)(2,1)}), bf16[8,24,128]{2,1,0:T(8,128)(2,1)S(1)}, u32[]{:S(2)}, u32[]{:S(2)}) async-start(bf16[8,24,128]{2,1,0:T(8,128)(2,1)} %broadcast_in_dim.141), calls=%async_computation.4 | async-start | bytes 98304 | tf_op jit(solution)/shard_map/all_to_all | solution.py:34
  196.9 0.3 fusion.37
  197.2 0.2 reshape.162
  197.4 0.2 reshape.163
  197.5 0.3 convolution_add_fusion.1
  197.9 8.6 %all-to-all-done.4 = bf16[8,24,128]{2,1,0:T(8,128)(2,1)S(1)} async-done(((bf16[8,24,128]{2,1,0:T(8,128)(2,1)}), bf16[8,24,128]{2,1,0:T(8,128)(2,1)S(1)}, u32[]{:S(2)}, u32[]{:S(2)}) %all-to-all-start.4) | async-done | bytes 49184 | tf_op jit(solution)/shard_map/all_to_all | solution.py:34
  206.5 0.8 broadcast_in_dim.142
  207.3 9.2 %all-to-all-start.5 = ((bf16[8,192,128]{2,1,0:T(8,128)(2,1)}), bf16[8,192,128]{2,1,0:T(8,128)(2,1)S(1)}, u32[]{:S(2)}, u32[]{:S(2)}) async-start(bf16[8,192,128]{2,1,0:T(8,128)(2,1)} %broadcast_in_dim.142), calls=%async_computation.5 | async-start | bytes 786432 | tf_op jit(solution)/shard_map/all_to_all | solution.py:34
  216.5 0.3 fusion
  216.8 1.0 convert_element_type.134
  217.8 0.6 slice_bitcast_fusion.2
  218.4 6.1 %all-to-all-done.5 = bf16[8,192,128]{2,1,0:T(8,128)(2,1)S(1)} async-done(((bf16[8,192,128]{2,1,0:T(8,128)(2,1)}), bf16[8,192,128]{2,1,0:T(8,128)(2,1)S(1)}, u32[]{:S(2)}, u32[]{:S(2)}) %all-to-all-start.5) | async-done | bytes 393248 | tf_op jit(solution)/shard_map/all_to_all | solution.py:34
  224.5 0.9 maximum_convert_fusion
  (55 shorter events, 0.4 us)
Async XLA Ops:
  0.6 1.0 copy-start
  1.7 17.2 %copy-start.1 = (bf16[22,45,256]{2,1,0:T(8,128)(2,1)S(1)}, bf16[22,45,256]{2,1,0:T(8,128)(2,1)}, u32[]{:S(2)}) copy-start(bf16[22,45,256]{2,1,0:T(8,128)(2,1)} %x_ref.1) | copy-start | bytes 1520644
  1.7 50.6 %copy-start.8 = (f32[704,3]{0,1:T(4,128)S(1)}, f32[704,3]{0,1:T(4,128)}, u32[]{:S(2)}) copy-start(f32[704,3]{0,1:T(4,128)} %param.16) | copy-start | bytes 25348
  1.7 50.7 %copy-start.9 = (s32[704,3]{0,1:T(4,128)S(1)}, s32[704,3]{0,1:T(4,128)}, u32[]{:S(2)}) copy-start(s32[704,3]{0,1:T(4,128)} %param.17) | copy-start | bytes 25348
  1.7 50.8 %copy-start.2 = (f32[2,256,384]{2,1,0:T(8,128)S(1)}, f32[2,256,384]{2,1,0:T(8,128)}, u32[]{:S(2)}) copy-start(f32[2,256,384]{2,1,0:T(8,128)} %constant.67.clone.tw_ref) | copy-start | bytes 2359300
  1.7 50.9 %copy-start.3 = (bf16[192,768]{1,0:T(8,128)(2,1)S(1)}, bf16[192,768]{1,0:T(8,128)(2,1)}, u32[]{:S(2)}) copy-start(bf16[192,768]{1,0:T(8,128)(2,1)} %constant.68.clone.w_ref) | copy-start | bytes 884740
  1.7 50.8 %copy-start.4 = (bf16[512,256]{1,0:T(8,128)(2,1)S(1)}, bf16[512,256]{1,0:T(8,128)(2,1)}, u32[]{:S(2)}) copy-start(bf16[512,256]{1,0:T(8,128)(2,1)} %constant.66.clone.d_ref) | copy-start | bytes 786436
  2.7 49.8 %all-to-all-start = ((bf16[32,8,1152]{2,1,0:T(8,128)(2,1)}), bf16[32,8,1152]{2,1,0:T(8,128)(2,1)S(1)}, u32[]{:S(2)}, u32[]{:S(2)}) async-start(bf16[32,8,1152]{2,1,0:T(8,128)(2,1)} %bitcast), calls=%async_computation | async-start | bytes 1179648 | tf_op jit(solution)/shard_map/all_to_all | solution.py:276
  18.9 36.4 %collective-permute-start = (bf16[45,256]{1,0:T(8,128)(2,1)S(1)}, bf16[45,256]{1,0:T(8,128)(2,1)S(1)}, u32[]{:S(2)}, u32[]{:S(2)}) collective-permute-start(bf16[45,256]{1,0:T(8,128)(2,1)S(1)} %get-tuple-element.35), channel_id=1, source_target_pairs={{0,32},{32,64},{64,96},{96,128},{128,160},{160,192},{192,224},{224... | collective-permute-start | bytes 69128 | tf_op jit(solution)/shard_map/ppermute | solution.py:279
  35.2 20.1 %collective-permute-start.1 = (bf16[45,256]{1,0:T(8,128)(2,1)S(1)}, bf16[45,256]{1,0:T(8,128)(2,1)S(1)}, u32[]{:S(2)}, u32[]{:S(2)}) collective-permute-start(bf16[45,256]{1,0:T(8,128)(2,1)S(1)} %get-tuple-element.34), channel_id=1, source_target_pairs={{0,992},{32,0},{64,32},{96,64},{128,96},{160,128},{192,160},{224,1... | collective-permute-start | bytes 69128 | tf_op jit(solution)/shard_map/ppermute | solution.py:280
  38.1 17.2 %collective-permute-start.2 = (bf16[22,256]{1,0:T(8,128)(2,1)S(1)}, bf16[22,256]{1,0:T(8,128)(2,1)S(1)}, u32[]{:S(2)}, u32[]{:S(2)}) collective-permute-start(bf16[22,256]{1,0:T(8,128)(2,1)S(1)} %bitcast.178), channel_id=1, source_target_pairs={{0,1},{1,2},{2,3},{3,4},{4,5},{5,6},{6,7},{7,8},{8,9},{9,10},{10,1... | collective-permute-start | bytes 33800 | tf_op jit(solution)/shard_map/ppermute | solution.py:281
  41.5 13.8 %collective-permute-start.3 = (bf16[22,256]{1,0:T(8,128)(2,1)S(1)}, bf16[22,256]{1,0:T(8,128)(2,1)S(1)}, u32[]{:S(2)}, u32[]{:S(2)}) collective-permute-start(bf16[22,256]{1,0:T(8,128)(2,1)S(1)} %bitcast.179), channel_id=1, source_target_pairs={{0,31},{1,0},{2,1},{3,2},{4,3},{5,4},{6,5},{7,6},{8,7},{9,8},{10,9... | collective-permute-start | bytes 33800 | tf_op jit(solution)/shard_map/ppermute | solution.py:282
  52.6 2.8 %copy-start.10 = (bf16[22,45,256]{2,1,0:T(8,128)(2,1)S(1)}, bf16[22,45,256]{2,1,0:T(8,128)(2,1)}, u32[]{:S(2)}) copy-start(bf16[22,45,256]{2,1,0:T(8,128)(2,1)} %param.12) | copy-start | bytes 1520644
  57.8 27.5 %collective-permute-start.4 = (f32[768,128]{1,0:T(8,128)S(1)}, f32[768,128]{1,0:T(8,128)S(1)}, u32[]{:S(2)}, u32[]{:S(2)}) collective-permute-start(f32[768,128]{1,0:T(8,128)S(1)} %slice_select_fusion.3), channel_id=1, source_target_pairs={{0,32},{32,0},{1,33},{33,1},{2,34},{34,2},{3,35},{35,3},{4,36},{36... | collective-permute-start | bytes 1179656 | tf_op jit(solution)/shard_map/ppermute | solution.py:295
  61.6 64.0 %all-to-all-start.1 = ((bf16[32,40,128]{2,1,0:T(8,128)(2,1)}), bf16[32,40,128]{2,1,0:T(8,128)(2,1)S(1)}, u32[]{:S(2)}, u32[]{:S(2)}) async-start(bf16[32,40,128]{2,1,0:T(8,128)(2,1)} %fourier_chunks.1), calls=%async_computation.1 | async-start | bytes 655360 | tf_op jit(solution)/shard_map/all_to_all | solution.py:286
  85.3 6.1 %collective-permute-start.5 = (bf16[2,2,2,2,24,128]{5,4,3,2,1,0:T(8,128)(2,1)S(1)}, bf16[2,2,2,2,24,128]{5,4,3,2,1,0:T(8,128)(2,1)S(1)}, u32[]{:S(2)}, u32[]{:S(2)}) collective-permute-start(bf16[2,2,2,2,24,128]{5,4,3,2,1,0:T(8,128)(2,1)S(1)} %fusion.42), channel_id=1, source_target_pairs={{0,8},{8,0},{16,24},{24,16},{1,9},{9,1},{17,25},{25,17},{2,10},{10... | collective-permute-start | bytes 294920 | tf_op jit(solution)/shard_map/ppermute | solution.py:46
  91.4 34.4 %copy-start.5 = (bf16[384,12,2,8]{0,3,2,1:T(8,128)(2,1)S(1)}, bf16[384,12,2,8]{0,3,2,1:T(8,128)(2,1)}, u32[]{:S(2)}) copy-start(bf16[384,12,2,8]{0,3,2,1:T(8,128)(2,1)} %param.14) | copy-start | bytes 442372
  91.5 34.4 %copy-start.7 = (f32[384,8]{0,1:T(8,128)S(1)}, f32[384,8]{0,1:T(8,128)}, u32[]{:S(2)}) copy-start(f32[384,8]{0,1:T(8,128)} %param.15) | copy-start | bytes 36868
  91.5 6.8 %collective-permute-start.6 = (bf16[2,2,2,24,128]{4,3,2,1,0:T(8,128)(2,1)S(1)}, bf16[2,2,2,24,128]{4,3,2,1,0:T(8,128)(2,1)S(1)}, u32[]{:S(2)}, u32[]{:S(2)}) collective-permute-start(bf16[2,2,2,24,128]{4,3,2,1,0:T(8,128)(2,1)S(1)} %fusion.43), channel_id=1, source_target_pairs={{0,16},{8,24},{16,0},{24,8},{1,17},{9,25},{17,1},{25,9},{2,18},{10... | collective-permute-start | bytes 147464 | tf_op jit(solution)/shard_map/ppermute | solution.py:46
  98.3 12.2 %collective-permute-start.7 = (bf16[2,2,24,128]{3,2,1,0:T(8,128)(2,1)S(1)}, bf16[2,2,24,128]{3,2,1,0:T(8,128)(2,1)S(1)}, u32[]{:S(2)}, u32[]{:S(2)}) collective-permute-start(bf16[2,2,24,128]{3,2,1,0:T(8,128)(2,1)S(1)} %fusion.46), channel_id=1, source_target_pairs={{0,1},{1,0},{2,3},{3,2},{4,5},{5,4},{6,7},{7,6},{8,9},{9,8},{10,11... | collective-permute-start | bytes 73736 | tf_op jit(solution)/shard_map/ppermute | solution.py:46
  110.5 6.6 %collective-permute-start.8 = (bf16[2,24,128]{2,1,0:T(8,128)(2,1)S(1)}, bf16[2,24,128]{2,1,0:T(8,128)(2,1)S(1)}, u32[]{:S(2)}, u32[]{:S(2)}) collective-permute-start(bf16[2,24,128]{2,1,0:T(8,128)(2,1)S(1)} %fusion.49), channel_id=1, source_target_pairs={{0,2},{1,3},{2,0},{3,1},{4,6},{5,7},{6,4},{7,5},{8,10},{9,11},{10,... | collective-permute-start | bytes 36872 | tf_op jit(solution)/shard_map/ppermute | solution.py:46
  117.1 8.5 %collective-permute-start.9 = (bf16[24,128]{1,0:T(8,128)(2,1)S(1)}, bf16[24,128]{1,0:T(8,128)(2,1)S(1)}, u32[]{:S(2)}, u32[]{:S(2)}) collective-permute-start(bf16[24,128]{1,0:T(8,128)(2,1)S(1)} %fusion.52), channel_id=1, source_target_pairs={{0,4},{1,5},{2,6},{3,7},{4,0},{5,1},{6,2},{7,3},{8,12},{9,13},{10,... | collective-permute-start | bytes 18440 | tf_op jit(solution)/shard_map/ppermute | solution.py:46
  131.2 12.1 %all-to-all-start.2 = ((f32[8,48,128]{2,1,0:T(8,128)}), f32[8,48,128]{2,1,0:T(8,128)S(1)}, u32[]{:S(2)}, u32[]{:S(2)}) async-start(f32[8,48,128]{2,1,0:T(8,128)} %broadcast_in_dim.137), calls=%async_computation.2 | async-start | bytes 393216 | tf_op jit(solution)/shard_map/all_to_all | solution.py:34
  144.0 45.5 %all-to-all-start.3 = ((f32[4,48,128]{2,1,0:T(8,128)}), f32[4,48,128]{2,1,0:T(8,128)S(1)}, u32[]{:S(2)}, u32[]{:S(2)}) async-start(f32[4,48,128]{2,1,0:T(8,128)} %broadcast_in_dim.138), calls=%async_computation.3 | async-start | bytes 196608 | tf_op jit(solution)/shard_map/all_to_all | solution.py:34
  167.6 17.2 %collective-permute-start.10 = (bf16[24,256]{1,0:T(8,128)(2,1)S(1)}, bf16[24,256]{1,0:T(8,128)(2,1)S(1)}, u32[]{:S(2)}, u32[]{:S(2)}) collective-permute-start(bf16[24,256]{1,0:T(8,128)(2,1)S(1)} %get-tuple-element.21), channel_id=1, source_target_pairs={{0,1},{1,2},{2,3},{3,4},{4,5},{5,6},{6,7},{7,8},{8,9},{9,10},{10,1... | collective-permute-start | bytes 36872 | tf_op jit(solution)/shard_map/ppermute | solution.py:317
  169.5 15.3 %collective-permute-start.11 = (bf16[24,256]{1,0:T(8,128)(2,1)S(1)}, bf16[24,256]{1,0:T(8,128)(2,1)S(1)}, u32[]{:S(2)}, u32[]{:S(2)}) collective-permute-start(bf16[24,256]{1,0:T(8,128)(2,1)S(1)} %get-tuple-element.22), channel_id=1, source_target_pairs={{0,31},{1,0},{2,1},{3,2},{4,3},{5,4},{6,5},{7,6},{8,7},{9,8},{10,9... | collective-permute-start | bytes 36872 | tf_op jit(solution)/shard_map/ppermute | solution.py:318
  191.0 5.8 %copy-start.6 = (bf16[3,256,256]{2,1,0:T(8,128)(2,1)S(1)}, bf16[3,256,256]{2,1,0:T(8,128)(2,1)}, u32[]{:S(2)}) copy-start(bf16[3,256,256]{2,1,0:T(8,128)(2,1)} %param.18) | copy-start | bytes 1179652
  191.9 14.6 %all-to-all-start.4 = ((bf16[8,24,128]{2,1,0:T(8,128)(2,1)}), bf16[8,24,128]{2,1,0:T(8,128)(2,1)S(1)}, u32[]{:S(2)}, u32[]{:S(2)}) async-start(bf16[8,24,128]{2,1,0:T(8,128)(2,1)} %broadcast_in_dim.141), calls=%async_computation.4 | async-start | bytes 98304 | tf_op jit(solution)/shard_map/all_to_all | solution.py:34
  207.3 17.2 %all-to-all-start.5 = ((bf16[8,192,128]{2,1,0:T(8,128)(2,1)}), bf16[8,192,128]{2,1,0:T(8,128)(2,1)S(1)}, u32[]{:S(2)}, u32[]{:S(2)}) async-start(bf16[8,192,128]{2,1,0:T(8,128)(2,1)} %broadcast_in_dim.142), calls=%async_computation.5 | async-start | bytes 786432 | tf_op jit(solution)/shard_map/all_to_all | solution.py:34
